TPU v7x, 32 devices: a whole 2x2x4 slice. The times are simulated.
32 devices in a mesh: pix: 16 (over z, x, core), rep: 2 (over y).
Axes of the slice: x: 2, y: 2, z: 4, core: 2. Of those that a mesh axis runs over, the one named last changes fastest.
Arguments:
- tokens: bfloat16 [256, 16, 1152], P(('pix', 'rep')), may hold values from -48 to 48
- out_grad: bfloat16 [256, 16, 1152], P(('pix', 'rep')), may hold values from -6 to 6
- query_weight: bfloat16 [1152, 1152], P('pix'), may hold values from -0.1875 to 0.1875
- key_weight: bfloat16 [1152, 1152], P('pix'), may hold values from -0.1875 to 0.1875
- value_weight: bfloat16 [1152, 1152], P('pix'), may hold values from -0.1875 to 0.1875
- output_weight: bfloat16 [1152, 1152], P('pix'), may hold values from -0.1875 to 0.1875
Outputs:
- input_grad: bfloat16 [256, 16, 1152], P(('pix', 'rep'))
- weight_grads: float32 [1152, 4608], P('pix')
All inputs are finite; a program needn't handle non-finite values.
Results may differ from a plain program's by a relative error of at most 0.025.
The roundings to bfloat16 on the way count: a program that leaves them out, or rounds other values in their place, can miss the bound.
Values may be sent and summed in bfloat16 or wider, within the bound.
No kernel may reach another device: no remote copies, remote signals or barrier semaphores. Data moves between devices by JAX's collectives and lax.ppermute only.
A program may use at most 128 MiB of HBM per device.

v0:
```python
import functools

import jax
import jax.numpy as jnp
from jax import lax
from jax.experimental import pallas as pl
from jax.experimental.pallas import tpu as pltpu
from jax.sharding import PartitionSpec as P


HEADS = 16
FRAMES = 16
KEPT = 2
BLOCK = 256
BOTH = ("pix", "rep")
VMEM = pl.BlockSpec(memory_space=pltpu.VMEM)
SMEM = pl.BlockSpec(memory_space=pltpu.SMEM)


def matmul(left, right, dims):
    return lax.dot_general(left, right, (dims, ((), ())), preferred_element_type=jnp.float32)


def shape_of(*dims, dtype=jnp.bfloat16):
    return jax.ShapeDtypeStruct(dims, dtype)


class Grid:
    def __init__(self, pix, rep):
        self.lines, self.groups, self.rep = pix // 4, rep // 2, rep

    def all(self):
        for a in range(self.lines):
            for b in range(2):
                for c in range(2):
                    for g in range(self.groups):
                        for y in range(2):
                            yield a, b, c, g, y

    def flat(self, a, b, c, g, y):
        return (4 * a + 2 * b + c) * self.rep + 2 * g + y

    def send(self, value, target):
        pairs = []
        for source in self.all():
            to = target(*source)
            if to is not None:
                pairs.append((self.flat(*source), self.flat(*to)))
        return lax.ppermute(value, BOTH, pairs)

    def flip(self, value, db, dc, dy):
        return self.send(value, lambda a, b, c, g, y: (a, b ^ db, c ^ dc, g, y ^ dy))

    def shift(self, value, step):
        return self.send(value, lambda a, b, c, g, y: ((a + step) % self.lines, b, c, g, y))

    def gather_lines(self, value):
        lines = self.lines
        found = {0: value}
        for s in range(1, lines):
            if lines == 2 or 1 < s < lines - 1:
                found[s] = self.shift(value, s)
        if lines > 2:
            last = lines - 1
            step = lambda by: (
                lambda a, b, c, g, y: (a + by, b, c, g, y) if 0 <= a + by < lines else None
            )
            up = self.send(value, step(1))
            down = self.send(value, step(-1))
            if lines == 4:
                ends = self.send(
                    found[2],
                    lambda a, b, c, g, y: (
                        (3, b, c, g, y) if a == 2 else (0, b, c, g, y) if a == 1 else None
                    ),
                )
            else:
                ends = self.send(
                    value, lambda a, b, c, g, y: (last - a, b, c, g, y) if a in (0, last) else None
                )
            found[1], found[last], found[lines] = up, down, ends
        return [found[s] for s in range(len(found))]


def pack_kernel(dim, at_ref, *refs):
    weights, outs = refs[:3], refs[3:]
    even, b_here, c_here = at_ref[3] == 0, at_ref[1], at_ref[2]
    values = [ref[...] for ref in weights]
    for b in range(2):
        for c in range(2):
            pieces = []
            for value in values:
                for k in range(KEPT):
                    low = (8 * c + 4 * k + 2 * b) * dim
                    first, second = value[:, low : low + dim], value[:, low + dim : low + 2 * dim]
                    pieces.append(jnp.where(even, first, second))
            block = jnp.concatenate(pieces, axis=1)
            for db in range(2):
                for dc in range(2):

                    @pl.when((b_here == b ^ db) & (c_here == c ^ dc))
                    def _(db=db, dc=dc):
                        outs[2 * db + dc][...] = block


def plane_kernel(at_ref, *refs):
    *pieces, out_ref = refs
    here = 2 * at_ref[1] + at_ref[2]
    for n, piece in enumerate(pieces):
        out_ref[here ^ n] = piece[...]


def sum_kernel(at_ref, *refs):
    parts, outs = refs[: len(refs) - 4], refs[len(refs) - 4 :]
    here = 2 * at_ref[1] + at_ref[2]
    for n, out in enumerate(outs):
        out[...] = sum(p[here ^ n].astype(jnp.float32) for p in parts).astype(jnp.bfloat16)


def attend(query, keyed, valued, dattn, scale):
    rows = query.shape[0]
    site = lambda axis: lax.broadcasted_iota(jnp.int32, (rows, rows), axis) // FRAMES
    scores = matmul(query, keyed, ((1,), (1,))) * scale
    scores = jnp.where(site(0) == site(1), scores, -1e30)
    expo = jnp.exp(scores - jnp.max(scores, axis=1, keepdims=True))
    probs = expo / jnp.sum(expo, axis=1, keepdims=True)
    probs_b = probs.astype(jnp.bfloat16)
    attended = matmul(probs_b, valued, ((1,), (0,)))
    dvalue = matmul(probs_b, dattn, ((0,), (0,)))
    dprobs = matmul(dattn, valued, ((1,), (1,)))
    inner = jnp.sum(dprobs * probs, axis=1, keepdims=True)
    dscore = (probs * (dprobs - inner) * scale).astype(jnp.bfloat16)
    dquery = matmul(dscore, keyed, ((1,), (0,)))
    dkey = matmul(dscore, query, ((0,), (0,)))
    return [v.astype(jnp.bfloat16) for v in (attended, dquery, dkey, dvalue)]


def full_weights(lines, at_ref, planes, loose, full):
    def store(plane, line):
        for n in range(4):
            loose[4 * line + n] = plane[n]

    last = lines - 1
    for s in range(lines):
        line = lax.rem(at_ref[0] + lines - s, lines)
        if lines > 2 and s in (1, last):
            edge = at_ref[0] == (0 if s == 1 else last)
            pl.when(edge)(functools.partial(store, planes[lines], line))
            pl.when(jnp.logical_not(edge))(functools.partial(store, planes[s], line))
        else:
            store(planes[s], line)
    shard = loose.shape[1]
    for p in range(4 * lines):
        full[p * shard : (p + 1) * shard, :] = loose[p]


def attention_kernel(scale, sub, lines, at_ref, *refs):
    xs, xc, ds, dc = refs[:4]
    moved = 4 + lines + (lines > 2)
    planes, out_ws = refs[4:moved], refs[moved : len(refs) - lines - 7]
    grads_in = refs[len(refs) - lines - 7 : len(refs) - 7]
    grad_out, dqkv_ref, full, loose, out_w, att, grads = refs[len(refs) - 7 :]
    shard, wide = loose.shape[1:]
    dim = wide // (3 * KEPT)
    width = xs.shape[-1]
    full_weights(lines, at_ref, planes, loose, full)
    if len(out_ws) == 1:
        out_w[...] = out_ws[0][...]
    else:
        for s, held in enumerate(out_ws):
            line = lax.rem(at_ref[0] + lines - s, lines)
            for k in range(KEPT):

                @pl.when(line == KEPT * at_ref[2] + k)
                def _(k=k, held=held):
                    out_w[k * dim : (k + 1) * dim, :] = held[...]

    half = xs.shape[0] * xs.shape[1]
    each = BLOCK // xs.shape[1]
    for part, (x_ref, d_ref) in enumerate(((xs, ds), (xc, dc))):

        def block(j, _, part=part, x_ref=x_ref, d_ref=d_ref):
            x = x_ref[pl.ds(each * j, each)].reshape(BLOCK, width)
            d = d_ref[pl.ds(each * j, each)].reshape(BLOCK, width)
            qkv = matmul(x, full[...], ((1,), (0,))).astype(jnp.bfloat16)
            da = matmul(d, out_w[...], ((1,), (1,))).astype(jnp.bfloat16)
            row = pl.multiple_of(part * half + j * BLOCK, BLOCK)
            for low in range(0, BLOCK, sub):
                outs = []
                for k in range(KEPT):
                    cut = lambda v, n: v[low : low + sub, n * dim : (n + 1) * dim]
                    outs.append(
                        attend(
                            cut(qkv, k), cut(qkv, KEPT + k), cut(qkv, 2 * KEPT + k), cut(da, k), scale
                        )
                    )
                att[pl.ds(row + low, sub), :] = jnp.concatenate([o[0] for o in outs], axis=1)
                dqkv_ref[pl.ds(row + low, sub), :] = jnp.concatenate(
                    [outs[k][n] for n in (1, 2, 3) for k in range(KEPT)], axis=1
                )
            return 0

        lax.fori_loop(0, half // BLOCK, block, 0)

    def columns(m, _):
        at = pl.multiple_of(m * 128, 128)
        first = matmul(att[:half, :], ds[:, :, pl.ds(at, 128)].reshape(half, 128), ((0,), (0,)))
        second = matmul(att[half:, :], dc[:, :, pl.ds(at, 128)].reshape(half, 128), ((0,), (0,)))
        grad_out[:, pl.ds(at, 128)] = (first + second).astype(jnp.bfloat16)
        first = matmul(xs[:, :, pl.ds(at, 128)].reshape(half, 128), dqkv_ref[:half, :], ((0,), (0,)))
        second = matmul(xc[:, :, pl.ds(at, 128)].reshape(half, 128), dqkv_ref[half:, :], ((0,), (0,)))
        grads[pl.ds(at, 128), :] = first + second
        return 0

    lax.fori_loop(0, width // 128, columns, 0)
    for p in range(4 * lines):
        loose[p] = grads[p * shard : (p + 1) * shard, :].astype(jnp.bfloat16)
    for s, out in enumerate(grads_in):
        line = lax.rem(at_ref[0] + s, lines)
        for n in range(4):
            out[n] = loose[4 * line + n]


def input_kernel(lines, at_ref, dqkv_ref, *refs):
    *planes, own_ref, other_ref, full, loose = refs
    full_weights(lines, at_ref, planes, loose, full)
    chunks, count, width = own_ref.shape
    each = BLOCK // count
    for part, out in enumerate((own_ref, other_ref)):

        def block(j, _, part=part, out=out):
            row = pl.multiple_of((part * chunks + each * j) * count, BLOCK)
            value = matmul(dqkv_ref[pl.ds(row, BLOCK), :], full[...], ((1,), (1,)))
            out[pl.ds(each * j, each)] = value.astype(jnp.bfloat16).reshape(each, count, width)
            return 0

        lax.fori_loop(0, chunks // each, block, 0)


def spread_kernel(dim, at_ref, *refs):
    *pieces, kept_ref, moved_ref, out_ref, table = refs
    width = HEADS * dim
    for n, piece in enumerate(pieces):
        db, dc, dy = n // 4, (n // 2) % 2, n % 2
        b = lax.rem(at_ref[1] + db, 2)
        c = lax.rem(at_ref[2] + dc, 2)
        y = lax.rem(at_ref[3] + dy, 2)
        table[4 * b + 2 * c + y] = piece[...].astype(jnp.float32)
    for b in range(2):
        for c in range(2):
            first, second = table[4 * b + 2 * c], table[4 * b + 2 * c + 1]
            for w in range(3):
                for k in range(KEPT):
                    piece = slice((w * KEPT + k) * dim, (w * KEPT + k + 1) * dim)
                    low = w * width + (8 * c + 4 * k + 2 * b) * dim
                    both = jnp.concatenate([first[:, piece], second[:, piece]], axis=1)
                    out_ref[:, low : low + 2 * dim] = both
    out_ref[:, 3 * width :] = kept_ref[...].astype(jnp.float32) + moved_ref[...].astype(jnp.float32)


def local(pix, rep, tokens, out_grad, query_weight, key_weight, value_weight, output_weight):
    grid = Grid(pix, rep)
    lines = grid.lines
    width = tokens.shape[-1]
    dim = width // HEADS
    wide = KEPT * dim
    shard = query_weight.shape[0]
    scale = 1.0 / dim**0.5
    place, rank = lax.axis_index("pix"), lax.axis_index("rep")
    a, b, c, y = place // 4, (place // 2) % 2, place % 2, rank % 2
    at = jnp.stack([a, b, c, y]).astype(jnp.int32)
    rows = tokens.reshape(-1, width)
    drows = out_grad.reshape(-1, width)
    count = rows.shape[0]
    total = 8 * count

    def gather_rows(own):
        ways = ((1, 0), (0, 1), (1, 1))
        chips = jnp.stack([own] + [grid.flip(own, db, 0, dy) for db, dy in ways])
        return chips, grid.flip(chips, 0, 1, 0)

    pieces = pl.pallas_call(
        functools.partial(pack_kernel, dim),
        out_shape=(shape_of(shard, 3 * wide),) * 4,
        in_specs=[SMEM, VMEM, VMEM, VMEM],
        out_specs=(VMEM,) * 4,
    )(at, query_weight, key_weight, value_weight)
    pieces = [pieces[0]] + [grid.flip(pieces[n], n // 2, n % 2, 0) for n in range(1, 4)]
    plane = pl.pallas_call(
        plane_kernel,
        out_shape=shape_of(4, shard, 3 * wide),
        in_specs=[SMEM] + [VMEM] * 4,
        out_specs=VMEM,
    )(at, *pieces)
    xs, xc = gather_rows(rows)
    planes = grid.gather_lines(plane)

    one_head = shard == dim
    span = lines // 2
    if one_head:
        out_ws = [
            grid.send(
                output_weight,
                lambda a, b, c, g, y: (((a + s) % lines, b, a // span, g, y) if c == y else None),
            )
            for s in range(lines)
        ]
    else:
        everything = lax.all_gather(output_weight, "pix", axis=0, tiled=True)
        everything = everything.reshape(2, KEPT, 2, 2, dim, width)
        out_w = lax.dynamic_index_in_dim(everything, c, 0, keepdims=False)
        out_w = lax.dynamic_index_in_dim(
            out_w.reshape(KEPT, 4, dim, width), 2 * b + y, 1, keepdims=False
        ).reshape(wide, width)
        out_ws = [out_w]
    ds, dc = gather_rows(drows)

    *grads_in, grad_out, dqkv = pl.pallas_call(
        functools.partial(attention_kernel, scale, 128, lines),
        out_shape=(shape_of(4, shard, 3 * wide),) * lines
        + (shape_of(wide, width), shape_of(total, 3 * wide)),
        in_specs=[SMEM] + [VMEM] * (4 + len(planes) + len(out_ws)),
        out_specs=(VMEM,) * (lines + 2),
        scratch_shapes=[
            pltpu.VMEM((width, 3 * wide), jnp.bfloat16),
            pltpu.VMEM((pix, shard, 3 * wide), jnp.bfloat16),
            pltpu.VMEM((wide, width), jnp.bfloat16),
            pltpu.VMEM((total, wide), jnp.bfloat16),
            pltpu.VMEM((width, 3 * wide), jnp.float32),
        ],
        cost_estimate=pl.CostEstimate(
            flops=8 * total * width * wide * 2, bytes_accessed=10 << 20, transcendentals=total * 32
        ),
    )(at, xs, xc, ds, dc, *planes, *out_ws)

    summed = pl.pallas_call(
        sum_kernel,
        out_shape=(shape_of(shard, 3 * wide),) * 4,
        in_specs=[SMEM] + [VMEM] * lines,
        out_specs=(VMEM,) * 4,
    )(at, grads_in[0], *[grid.shift(grads_in[s], s) for s in range(1, lines)])
    square = []
    for n in range(8):
        block = summed[n // 2]
        square.append(grid.flip(block, n // 4, (n // 2) % 2, n % 2) if n else block)

    if one_head:
        blocks = grad_out.reshape(KEPT, dim, width)
        partial = [
            grid.send(
                lax.dynamic_index_in_dim(
                    blocks, jnp.clip((a + s) % lines - span * c, 0, KEPT - 1), 0, keepdims=False
                ),
                lambda a, b, c, g, y: (
                    ((a + s) % lines, b, y, g, y) if ((a + s) % lines) // span == c else None
                ),
            )
            for s in range(lines)
        ]
        kept = sum(p.astype(jnp.float32) for p in partial).astype(jnp.bfloat16)
        moved = grid.send(kept, lambda a, b, c, g, y: (a, b, c, g, y ^ 1) if c == y else None)
    else:
        whole = jnp.zeros((2, KEPT, 2, 2, dim, width), jnp.float32)
        whole = lax.dynamic_update_slice(
            whole,
            grad_out.astype(jnp.float32).reshape(1, KEPT, 1, 1, dim, width),
            (c, 0, b, y, 0, 0),
        ).reshape(width, width)
        pairs = [[2 * g, 2 * g + 1] for g in range(grid.groups)]
        whole = lax.psum(whole, "rep", axis_index_groups=pairs)
        kept = lax.psum_scatter(whole, "pix", scatter_dimension=0, tiled=True)
        moved = jnp.zeros_like(kept)

    input_call = pl.pallas_call(
        functools.partial(input_kernel, lines),
        out_shape=(shape_of(4, count, width),) * 2,
        in_specs=[SMEM] + [VMEM] * (1 + len(planes)),
        out_specs=(VMEM,) * 2,
        scratch_shapes=[
            pltpu.VMEM((width, 3 * wide), jnp.bfloat16),
            pltpu.VMEM((pix, shard, 3 * wide), jnp.bfloat16),
        ],
        cost_estimate=pl.CostEstimate(
            flops=6 * total * width * wide, bytes_accessed=8 << 20, transcendentals=0
        ),
    )
    own_part, other_part = input_call(at, dqkv, *planes)
    pair = own_part.astype(jnp.float32) + grid.flip(other_part, 0, 1, 0).astype(jnp.float32)
    sent = pair.astype(jnp.bfloat16)
    dinput = pair[0]
    for i, (db, dy) in enumerate(((1, 0), (0, 1), (1, 1))):
        dinput = dinput + grid.flip(sent[i + 1], db, 0, dy).astype(jnp.float32)

    grads = pl.pallas_call(
        functools.partial(spread_kernel, dim),
        out_shape=shape_of(shard, 4 * width, dtype=jnp.float32),
        in_specs=[SMEM] + [VMEM] * 10,
        out_specs=VMEM,
        scratch_shapes=[pltpu.VMEM((8, shard, 3 * wide), jnp.float32)],
    )(at, *square, kept, moved)
    if grid.groups > 1:
        same = [[2 * g + y for g in range(grid.groups)] for y in range(2)]
        grads = lax.psum(grads, "rep", axis_index_groups=same)
    return dinput.astype(jnp.bfloat16).reshape(tokens.shape), grads


def solution(mesh):
    pix, rep = mesh.shape["pix"], mesh.shape["rep"]
    sites = P(BOTH, None, None)
    rows = P("pix", None)

    def step(*operands):
        return local(pix, rep, *operands)

    return jax.shard_map(
        step,
        mesh=mesh,
        in_specs=(sites, sites, rows, rows, rows, rows),
        out_specs=(sites, rows),
        check_vma=False,
    )
```

profile of v0, /device:TPU:0, one launch (start us, length us, event | category | flops | bytes accessed | tf_op | source)
XLA Modules:
  0.0 185.0 jit_solution(16680809308016508484)
XLA Ops:
  0.6 3.0 %collective-permute-start = (bf16[128,1152]{1,0:T(8,128)(2,1)}, bf16[128,1152]{1,0:T(8,128)(2,1)S(1)}, u32[]{:S(2)}, u32[]{:S(2)}) collective-permute-start(bf16[128,1152]{1,0:T(8,128)(2,1)} %bitcast.41), channel_id=1, source_target_pairs={{0,4},{1,5},{2,6},{3,7},{4,0},{5,1},{6,2},{7,3},{8,12},{9,13},{10,... | collective-permute-start | bytes 884744 | tf_op jit(solution)/shard_map/ppermute | solution.py:49
  5.2 1.9 %collective-permute-start.4 = (bf16[128,1152]{1,0:T(8,128)(2,1)}, bf16[128,1152]{1,0:T(8,128)(2,1)S(1)}, u32[]{:S(2)}, u32[]{:S(2)}) collective-permute-start(bf16[128,1152]{1,0:T(8,128)(2,1)} %bitcast.45), channel_id=1, source_target_pairs={{0,4},{1,5},{2,6},{3,7},{4,0},{5,1},{6,2},{7,3},{8,12},{9,13},{10,... | collective-permute-start | bytes 884744 | tf_op jit(solution)/shard_map/ppermute | solution.py:49
  8.7 3.1 %collective-permute-done = bf16[128,1152]{1,0:T(8,128)(2,1)S(1)} collective-permute-done((bf16[128,1152]{1,0:T(8,128)(2,1)}, bf16[128,1152]{1,0:T(8,128)(2,1)S(1)}, u32[]{:S(2)}, u32[]{:S(2)}) %collective-permute-start) | collective-permute-done | bytes 294944 | tf_op jit(solution)/shard_map/ppermute | solution.py:49
  11.7 3.0 %collective-permute-start.6 = (bf16[128,1152]{1,0:T(8,128)(2,1)}, bf16[128,1152]{1,0:T(8,128)(2,1)S(1)}, u32[]{:S(2)}, u32[]{:S(2)}) collective-permute-start(bf16[128,1152]{1,0:T(8,128)(2,1)} %bitcast.47), channel_id=1, source_target_pairs={{0,5},{1,4},{2,7},{3,6},{4,1},{5,0},{6,3},{7,2},{8,13},{9,12},{10,... | collective-permute-start | bytes 884744 | tf_op jit(solution)/shard_map/ppermute | solution.py:49
  14.7 5.4 %collective-permute-done.1 = bf16[128,1152]{1,0:T(8,128)(2,1)S(1)} collective-permute-done((bf16[128,1152]{1,0:T(8,128)(2,1)}, bf16[128,1152]{1,0:T(8,128)(2,1)S(1)}, u32[]{:S(2)}, u32[]{:S(2)}) %collective-permute-start.1) | collective-permute-done | bytes 294944 | tf_op jit(solution)/shard_map/ppermute | solution.py:49
  21.4 3.1 %collective-permute-done.4 = bf16[128,1152]{1,0:T(8,128)(2,1)S(1)} collective-permute-done((bf16[128,1152]{1,0:T(8,128)(2,1)}, bf16[128,1152]{1,0:T(8,128)(2,1)S(1)}, u32[]{:S(2)}, u32[]{:S(2)}) %collective-permute-start.4) | collective-permute-done | bytes 294944 | tf_op jit(solution)/shard_map/ppermute | solution.py:49
  24.4 6.9 %collective-permute-done.5 = bf16[128,1152]{1,0:T(8,128)(2,1)S(1)} collective-permute-done((bf16[128,1152]{1,0:T(8,128)(2,1)}, bf16[128,1152]{1,0:T(8,128)(2,1)S(1)}, u32[]{:S(2)}, u32[]{:S(2)}) %collective-permute-start.5) | collective-permute-done | bytes 294944 | tf_op jit(solution)/shard_map/ppermute | solution.py:49
  32.5 2.8 %shard_map.77 = (bf16[72,432]{1,0:T(8,128)(2,1)}, bf16[72,432]{1,0:T(8,128)(2,1)}, bf16[72,432]{1,0:T(8,128)(2,1)}, bf16[72,432]{1,0:T(8,128)(2,1)}) custom-call(s32[4]{0:T(128)} %pad_add_fusion.at_ref, bf16[72,1152]{1,0:T(8,128)(2,1)} %refs_0_.1, bf16[72,1152]{1,0:T(8,128)(2,1)} %refs_1_.1, bf16[72,1152]{1,0:T(8,128)(2,1)} %refs_2_.1), custom_call_target="tpu_custom_call" | custom-call | tf_op jit(solution)/shard_map/pallas_call | solution.py:282
  37.3 2.3 %collective-permute-done.10.refs_3_ = bf16[72,432]{1,0:T(8,128)(2,1)S(1)} collective-permute-done((bf16[72,432]{1,0:T(8,128)(2,1)}, bf16[72,432]{1,0:T(8,128)(2,1)S(1)}, u32[]{:S(2)}, u32[]{:S(2)}) %collective-permute-start.10) | collective-permute-done | bytes 62240 | tf_op jit(solution)/shard_map/ppermute | solution.py:49
  39.7 3.5 %collective-permute-start.16 = (bf16[72,1152]{1,0:T(8,128)(2,1)S(1)}, bf16[72,1152]{1,0:T(8,128)(2,1)S(1)}, u32[]{:S(2)}, u32[]{:S(2)}) collective-permute-start(bf16[72,1152]{1,0:T(8,128)(2,1)S(1)} %copy-done.21), channel_id=1, source_target_pairs={{0,8},{3,9},{4,12},{7,13},{8,16},{11,17},{12,20},{15,21},{16,26},{... | collective-permute-start | bytes 497672 | tf_op jit(solution)/shard_map/ppermute | solution.py:49
  44.5 3.3 %collective-permute-done.9.refs_2_ = bf16[72,432]{1,0:T(8,128)(2,1)S(1)} collective-permute-done((bf16[72,432]{1,0:T(8,128)(2,1)}, bf16[72,432]{1,0:T(8,128)(2,1)S(1)}, u32[]{:S(2)}, u32[]{:S(2)}) %collective-permute-start.9) | collective-permute-done | bytes 62240 | tf_op jit(solution)/shard_map/ppermute | solution.py:49
  50.2 2.4 %collective-permute-start.12 = (bf16[4,72,432]{2,1,0:T(8,128)(2,1)}, bf16[4,72,432]{2,1,0:T(8,128)(2,1)S(1)}, u32[]{:S(2)}, u32[]{:S(2)}) collective-permute-start(bf16[4,72,432]{2,1,0:T(8,128)(2,1)} %shard_map.78.refs_4_.refs_0_), channel_id=1, source_target_pairs={{0,16},{1,17},{2,18},{3,19},{4,20},{5,21},{6,22},{7,23},{8,24},{9,... | collective-permute-start | bytes 746504 | tf_op jit(solution)/shard_map/ppermute | solution.py:49
  52.6 2.4 %collective-permute-start.17 = (bf16[72,1152]{1,0:T(8,128)(2,1)S(1)}, bf16[72,1152]{1,0:T(8,128)(2,1)S(1)}, u32[]{:S(2)}, u32[]{:S(2)}) collective-permute-start(bf16[72,1152]{1,0:T(8,128)(2,1)S(1)} %copy-done.21), channel_id=1, source_target_pairs={{0,16},{3,17},{4,20},{7,21},{8,24},{11,25},{12,28},{15,29},{16,2},... | collective-permute-start | bytes 497672 | tf_op jit(solution)/shard_map/ppermute | solution.py:49
  55.0 2.9 %collective-permute-start.18 = (bf16[72,1152]{1,0:T(8,128)(2,1)S(1)}, bf16[72,1152]{1,0:T(8,128)(2,1)S(1)}, u32[]{:S(2)}, u32[]{:S(2)}) collective-permute-start(bf16[72,1152]{1,0:T(8,128)(2,1)S(1)} %copy-done.21), channel_id=1, source_target_pairs={{0,24},{3,25},{4,28},{7,29},{8,0},{11,1},{12,4},{15,5},{16,10},{19... | collective-permute-start | bytes 497672 | tf_op jit(solution)/shard_map/ppermute | solution.py:49
  58.9 13.8 %collective-permute-start.11 = (bf16[4,72,432]{2,1,0:T(8,128)(2,1)}, bf16[4,72,432]{2,1,0:T(8,128)(2,1)S(1)}, u32[]{:S(2)}, u32[]{:S(2)}) collective-permute-start(bf16[4,72,432]{2,1,0:T(8,128)(2,1)} %shard_map.78.refs_4_.refs_0_), channel_id=1, source_target_pairs={{0,8},{1,9},{2,10},{3,11},{4,12},{5,13},{6,14},{7,15},{8,16},{9,17... | collective-permute-start | bytes 746504 | tf_op jit(solution)/shard_map/ppermute | solution.py:49
  77.2 5.2 %collective-permute-done.13.refs_7_.refs_3_ = bf16[4,72,432]{2,1,0:T(8,128)(2,1)S(1)} collective-permute-done((bf16[4,72,432]{2,1,0:T(8,128)(2,1)}, bf16[4,72,432]{2,1,0:T(8,128)(2,1)S(1)}, u32[]{:S(2)}, u32[]{:S(2)}) %collective-permute-start.13) | collective-permute-done | bytes 248864 | tf_op jit(solution)/shard_map/ppermute | solution.py:49
  82.4 3.2 %collective-permute-done.14.refs_8_.refs_4_ = bf16[4,72,432]{2,1,0:T(8,128)(2,1)S(1)} collective-permute-done((bf16[4,72,432]{2,1,0:T(8,128)(2,1)S(1)}, bf16[4,72,432]{2,1,0:T(8,128)(2,1)S(1)}, u32[]{:S(2)}, u32[]{:S(2)}) %collective-permute-start.14) | collective-permute-done | bytes 248864 | tf_op jit(solution)/shard_map/ppermute | solution.py:49
  86.3 20.0 %shard_map.79 = (bf16[4,72,432]{2,1,0:T(8,128)(2,1)}, bf16[4,72,432]{2,1,0:T(8,128)(2,1)}, bf16[4,72,432]{2,1,0:T(8,128)(2,1)}, bf16[4,72,432]{2,1,0:T(8,128)(2,...) custom-call(s32[4]{0:T(128)} %pad_add_fusion.at_ref, bf16[4,128,1152]{2,1,0:T(8,128)(2,1)} %copy-done.1, ...), custom_call_target="tpu_custom_call" | custom-call | flops 2717908992 | bytes 10485760 | tf_op jit(solution)/shard_map/pallas_call | solution.py:318
  106.4 5.1 %shard_map.80 = (bf16[4,128,1152]{2,1,0:T(8,128)(2,1)}, bf16[4,128,1152]{2,1,0:T(8,128)(2,1)}) custom-call(s32[4]{0:T(128)} %pad_add_fusion.at_ref, bf16[1024,432]{1,0:T(8,128)(2,1)} %get-tuple-element.22.dqkv_ref, bf16[4,72,432]{2,1,0:T(8,128)(2,1)} %shard_map.78.refs_4_.refs_0_, bf16[4,72,432]{2,1,0:T(8,128)(2,1)} %copy-done.18, ...), custom_call_target="tpu_custom_call" | custom-call | flops 1019215872 | bytes 8388608 | tf_op jit(solution)/shard_map/pallas_call | solution.py:387
  111.4 3.1 %collective-permute-start.24 = (bf16[4,72,432]{2,1,0:T(8,128)(2,1)}, bf16[4,72,432]{2,1,0:T(8,128)(2,1)S(1)}, u32[]{:S(2)}, u32[]{:S(2)}) collective-permute-start(bf16[4,72,432]{2,1,0:T(8,128)(2,1)} %get-tuple-element.27), channel_id=1, source_target_pairs={{0,16},{1,17},{2,18},{3,19},{4,20},{5,21},{6,22},{7,23},{8,24},{9,... | collective-permute-start | bytes 746504 | tf_op jit(solution)/shard_map/ppermute | solution.py:49
  116.1 2.9 %collective-permute-start.33 = (bf16[72,1152]{1,0:T(8,128)(2,1)}, bf16[72,1152]{1,0:T(8,128)(2,1)}, u32[]{:S(2)}, u32[]{:S(2)}) collective-permute-start(bf16[72,1152]{1,0:T(8,128)(2,1)} %get-tuple-element.39), channel_id=1, source_target_pairs={{0,0},{1,3},{4,4},{5,7},{8,8},{9,11},{12,12},{13,15},{18,16},{19,1... | collective-permute-start | bytes 497672 | tf_op jit(solution)/shard_map/ppermute | solution.py:49
  119.0 4.5 %collective-permute-done.23.refs_1_ = bf16[4,72,432]{2,1,0:T(8,128)(2,1)S(1)} collective-permute-done((bf16[4,72,432]{2,1,0:T(8,128)(2,1)}, bf16[4,72,432]{2,1,0:T(8,128)(2,1)S(1)}, u32[]{:S(2)}, u32[]{:S(2)}) %collective-permute-start.23) | collective-permute-done | bytes 248864 | tf_op jit(solution)/shard_map/ppermute | solution.py:49
  125.4 9.9 %collective-permute-done.24.refs_2_ = bf16[4,72,432]{2,1,0:T(8,128)(2,1)S(1)} collective-permute-done((bf16[4,72,432]{2,1,0:T(8,128)(2,1)}, bf16[4,72,432]{2,1,0:T(8,128)(2,1)S(1)}, u32[]{:S(2)}, u32[]{:S(2)}) %collective-permute-start.24) | collective-permute-done | bytes 248864 | tf_op jit(solution)/shard_map/ppermute | solution.py:49
  137.9 2.1 %shard_map.81 = (bf16[72,432]{1,0:T(8,128)(2,1)}, bf16[72,432]{1,0:T(8,128)(2,1)}, bf16[72,432]{1,0:T(8,128)(2,1)}, bf16[72,432]{1,0:T(8,128)(2,1)}) custom-call(s32[4]{0:T(128)} %pad_add_fusion.at_ref, bf16[4,72,432]{2,1,0:T(8,128)(2,1)} %get-tuple-element.25.refs_0_, bf16[4,72,432]{2,1,0:T(8,128)(2,1)} %copy-done.7, bf16[4,72,432]{2,1,0:T(8,128)(2,1)} %copy-done.8, ...), custom_call_target="tpu_custom_call" | custom-call | tf_op jit(solution)/shard_map/pallas_call | solution.py:336
  140.0 10.6 %collective-permute-start.27 = (bf16[72,432]{1,0:T(8,128)(2,1)}, bf16[72,432]{1,0:T(8,128)(2,1)S(1)}, u32[]{:S(2)}, u32[]{:S(2)}) collective-permute-start(bf16[72,432]{1,0:T(8,128)(2,1)} %get-tuple-element.30), channel_id=1, source_target_pairs={{0,2},{1,3},{2,0},{3,1},{4,6},{5,7},{6,4},{7,5},{8,10},{9,11},{10,... | collective-permute-start | bytes 186632 | tf_op jit(solution)/shard_map/ppermute | solution.py:49
  152.4 2.6 %collective-permute-start.26 = (bf16[72,432]{1,0:T(8,128)(2,1)S(1)}, bf16[72,432]{1,0:T(8,128)(2,1)S(1)}, u32[]{:S(2)}, u32[]{:S(2)}) collective-permute-start(bf16[72,432]{1,0:T(8,128)(2,1)S(1)} %copy-done.9), channel_id=1, source_target_pairs={{0,1},{1,0},{2,3},{3,2},{4,5},{5,4},{6,7},{7,6},{8,9},{9,8},{10,11... | collective-permute-start | bytes 186632 | tf_op jit(solution)/shard_map/ppermute | solution.py:49
  164.0 3.4 %collective-permute-start.37 = (bf16[72,1152]{1,0:T(8,128)(2,1)S(1)}, bf16[72,1152]{1,0:T(8,128)(2,1)}, u32[]{:S(2)}, u32[]{:S(2)}) collective-permute-start(bf16[72,1152]{1,0:T(8,128)(2,1)S(1)} %add_convert_fusion.refs_8_), channel_id=1, source_target_pairs={{0,1},{3,2},{4,5},{7,6},{8,9},{11,10},{12,13},{15,14},{16,17},{19,... | collective-permute-start | bytes 497672 | tf_op jit(solution)/shard_map/ppermute | solution.py:49
  167.4 6.3 %collective-permute-done.31.refs_6_ = bf16[72,432]{1,0:T(8,128)(2,1)} collective-permute-done((bf16[72,432]{1,0:T(8,128)(2,1)S(1)}, bf16[72,432]{1,0:T(8,128)(2,1)}, u32[]{:S(2)}, u32[]{:S(2)}) %collective-permute-start.31) | collective-permute-done | bytes 62240 | tf_op jit(solution)/shard_map/ppermute | solution.py:49
  173.7 2.5 %collective-permute-start.32 = (bf16[72,432]{1,0:T(8,128)(2,1)S(1)}, bf16[72,432]{1,0:T(8,128)(2,1)}, u32[]{:S(2)}, u32[]{:S(2)}) collective-permute-start(bf16[72,432]{1,0:T(8,128)(2,1)S(1)} %copy-done.26), channel_id=1, source_target_pairs={{0,7},{1,6},{2,5},{3,4},{4,3},{5,2},{6,1},{7,0},{8,15},{9,14},{10,... | collective-permute-start | bytes 186632 | tf_op jit(solution)/shard_map/ppermute | solution.py:49
  176.2 2.2 %collective-permute-done.32.refs_7_ = bf16[72,432]{1,0:T(8,128)(2,1)} collective-permute-done((bf16[72,432]{1,0:T(8,128)(2,1)S(1)}, bf16[72,432]{1,0:T(8,128)(2,1)}, u32[]{:S(2)}, u32[]{:S(2)}) %collective-permute-start.32) | collective-permute-done | bytes 62240 | tf_op jit(solution)/shard_map/ppermute | solution.py:49
  178.5 4.5 %shard_map.82 = f32[72,4608]{1,0:T(8,128)} custom-call(s32[4]{0:T(128)} %pad_add_fusion.at_ref, bf16[72,432]{1,0:T(8,128)(2,1)} %get-tuple-element.29.refs_0_, bf16[72,432]{1,0:T(8,128)(2,1)} %copy-done.12, bf16[72,432]{1,0:T(8,128)(2,1)} %copy-done.10, bf16[72,432]{1,0:T(8,128)(2,1)} %copy-done.11, bf16[72,432]{1,0:T(8,128)(2,1)} %copy-done.13, ...), custom_call_target="tpu_custom_call" | custom-call | tf_op jit(solution)/shard_map/pallas_call | solution.py:394
  183.0 2.0 %fusion.3 = bf16[128,1152]{1,0:T(8,128)(2,1)} fusion(f32[4,128,1152]{2,1,0:T(8,128)S(1)} %get-tuple-element.35, bf16[128,1152]{1,0:T(8,128)(2,1)} %collective-permute-done.22, bf16[128,1152]{1,0:T(8,128)(2,1)} %collective-permute-done.21, bf16[128,1152]{1,0:T(8,128)(2,1)} %collective-permute-done.20), kind=kLoop, calls=%fused_computation.7 | loop fusion | flops 1032192 | bytes 1769472 | tf_op jit(solution)/shard_map/convert_element_type | solution.py:404
  (116 shorter events, 34.0 us)
Async XLA Ops:
  0.6 11.1 %collective-permute-start = (bf16[128,1152]{1,0:T(8,128)(2,1)}, bf16[128,1152]{1,0:T(8,128)(2,1)S(1)}, u32[]{:S(2)}, u32[]{:S(2)}) collective-permute-start(bf16[128,1152]{1,0:T(8,128)(2,1)} %bitcast.41), channel_id=1, source_target_pairs={{0,4},{1,5},{2,6},{3,7},{4,0},{5,1},{6,2},{7,3},{8,12},{9,13},{10,... | collective-permute-start | bytes 884744 | tf_op jit(solution)/shard_map/ppermute | solution.py:49
  3.7 16.4 %collective-permute-start.1 = (bf16[128,1152]{1,0:T(8,128)(2,1)}, bf16[128,1152]{1,0:T(8,128)(2,1)S(1)}, u32[]{:S(2)}, u32[]{:S(2)}) collective-permute-start(bf16[128,1152]{1,0:T(8,128)(2,1)} %bitcast.42), channel_id=1, source_target_pairs={{0,1},{1,0},{2,3},{3,2},{4,5},{5,4},{6,7},{7,6},{8,9},{9,8},{10,11... | collective-permute-start | bytes 884744 | tf_op jit(solution)/shard_map/ppermute | solution.py:49
  5.2 14.9 %collective-permute-start.2 = (bf16[128,1152]{1,0:T(8,128)(2,1)}, bf16[128,1152]{1,0:T(8,128)(2,1)S(1)}, u32[]{:S(2)}, u32[]{:S(2)}) collective-permute-start(bf16[128,1152]{1,0:T(8,128)(2,1)} %bitcast.43), channel_id=1, source_target_pairs={{0,5},{1,4},{2,7},{3,6},{4,1},{5,0},{6,3},{7,2},{8,13},{9,12},{10,... | collective-permute-start | bytes 884744 | tf_op jit(solution)/shard_map/ppermute | solution.py:49
  5.2 19.2 %collective-permute-start.4 = (bf16[128,1152]{1,0:T(8,128)(2,1)}, bf16[128,1152]{1,0:T(8,128)(2,1)S(1)}, u32[]{:S(2)}, u32[]{:S(2)}) collective-permute-start(bf16[128,1152]{1,0:T(8,128)(2,1)} %bitcast.45), channel_id=1, source_target_pairs={{0,4},{1,5},{2,6},{3,7},{4,0},{5,1},{6,2},{7,3},{8,12},{9,13},{10,... | collective-permute-start | bytes 884744 | tf_op jit(solution)/shard_map/ppermute | solution.py:49
  7.2 24.1 %collective-permute-start.5 = (bf16[128,1152]{1,0:T(8,128)(2,1)}, bf16[128,1152]{1,0:T(8,128)(2,1)S(1)}, u32[]{:S(2)}, u32[]{:S(2)}) collective-permute-start(bf16[128,1152]{1,0:T(8,128)(2,1)} %bitcast.46), channel_id=1, source_target_pairs={{0,1},{1,0},{2,3},{3,2},{4,5},{5,4},{6,7},{7,6},{8,9},{9,8},{10,11... | collective-permute-start | bytes 884744 | tf_op jit(solution)/shard_map/ppermute | solution.py:49
  11.7 19.6 %collective-permute-start.6 = (bf16[128,1152]{1,0:T(8,128)(2,1)}, bf16[128,1152]{1,0:T(8,128)(2,1)S(1)}, u32[]{:S(2)}, u32[]{:S(2)}) collective-permute-start(bf16[128,1152]{1,0:T(8,128)(2,1)} %bitcast.47), channel_id=1, source_target_pairs={{0,5},{1,4},{2,7},{3,6},{4,1},{5,0},{6,3},{7,2},{8,13},{9,12},{10,... | collective-permute-start | bytes 884744 | tf_op jit(solution)/shard_map/ppermute | solution.py:49
  21.3 64.3 %collective-permute-start.3 = (bf16[4,128,1152]{2,1,0:T(8,128)(2,1)S(1)}, bf16[4,128,1152]{2,1,0:T(8,128)(2,1)}, u32[]{:S(2)}, u32[]{:S(2)}) collective-permute-start(bf16[4,128,1152]{2,1,0:T(8,128)(2,1)S(1)} %pad_maximum_fusion.refs_0_), channel_id=1, source_target_pairs={{0,2},{1,3},{2,0},{3,1},{4,6},{5,7},{6,4},{7,5},{8,10},{9,11},{10,... | collective-permute-start | bytes 3538952 | tf_op jit(solution)/shard_map/ppermute | solution.py:49
  31.5 54.1 %collective-permute-start.7 = (bf16[4,128,1152]{2,1,0:T(8,128)(2,1)S(1)}, bf16[4,128,1152]{2,1,0:T(8,128)(2,1)}, u32[]{:S(2)}, u32[]{:S(2)}) collective-permute-start(bf16[4,128,1152]{2,1,0:T(8,128)(2,1)S(1)} %pad_maximum_fusion.1.refs_2_), channel_id=1, source_target_pairs={{0,2},{1,3},{2,0},{3,1},{4,6},{5,7},{6,4},{7,5},{8,10},{9,11},{10,... | collective-permute-start | bytes 3538952 | tf_op jit(solution)/shard_map/ppermute | solution.py:49
  36.4 6.8 %collective-permute-start.8 = (bf16[72,432]{1,0:T(8,128)(2,1)}, bf16[72,432]{1,0:T(8,128)(2,1)S(1)}, u32[]{:S(2)}, u32[]{:S(2)}) collective-permute-start(bf16[72,432]{1,0:T(8,128)(2,1)} %get-tuple-element.19), channel_id=1, source_target_pairs={{0,2},{1,3},{2,0},{3,1},{4,6},{5,7},{6,4},{7,5},{8,10},{9,11},{10,... | collective-permute-start | bytes 186632 | tf_op jit(solution)/shard_map/ppermute | solution.py:49
  36.7 15.9 %collective-permute-start.15 = (bf16[72,1152]{1,0:T(8,128)(2,1)S(1)}, bf16[72,1152]{1,0:T(8,128)(2,1)S(1)}, u32[]{:S(2)}, u32[]{:S(2)}) collective-permute-start(bf16[72,1152]{1,0:T(8,128)(2,1)S(1)} %copy-done.21), channel_id=1, source_target_pairs={{0,0},{3,1},{4,4},{7,5},{8,8},{11,9},{12,12},{15,13},{16,18},{19,1... | collective-permute-start | bytes 497672 | tf_op jit(solution)/shard_map/ppermute | solution.py:49
  39.7 15.3 %collective-permute-start.16 = (bf16[72,1152]{1,0:T(8,128)(2,1)S(1)}, bf16[72,1152]{1,0:T(8,128)(2,1)S(1)}, u32[]{:S(2)}, u32[]{:S(2)}) collective-permute-start(bf16[72,1152]{1,0:T(8,128)(2,1)S(1)} %copy-done.21), channel_id=1, source_target_pairs={{0,8},{3,9},{4,12},{7,13},{8,16},{11,17},{12,20},{15,21},{16,26},{... | collective-permute-start | bytes 497672 | tf_op jit(solution)/shard_map/ppermute | solution.py:49
  50.2 23.8 %collective-permute-start.12 = (bf16[4,72,432]{2,1,0:T(8,128)(2,1)}, bf16[4,72,432]{2,1,0:T(8,128)(2,1)S(1)}, u32[]{:S(2)}, u32[]{:S(2)}) collective-permute-start(bf16[4,72,432]{2,1,0:T(8,128)(2,1)} %shard_map.78.refs_4_.refs_0_), channel_id=1, source_target_pairs={{0,16},{1,17},{2,18},{3,19},{4,20},{5,21},{6,22},{7,23},{8,24},{9,... | collective-permute-start | bytes 746504 | tf_op jit(solution)/shard_map/ppermute | solution.py:49
  55.0 17.6 %collective-permute-start.18 = (bf16[72,1152]{1,0:T(8,128)(2,1)S(1)}, bf16[72,1152]{1,0:T(8,128)(2,1)S(1)}, u32[]{:S(2)}, u32[]{:S(2)}) collective-permute-start(bf16[72,1152]{1,0:T(8,128)(2,1)S(1)} %copy-done.21), channel_id=1, source_target_pairs={{0,24},{3,25},{4,28},{7,29},{8,0},{11,1},{12,4},{15,5},{16,10},{19... | collective-permute-start | bytes 497672 | tf_op jit(solution)/shard_map/ppermute | solution.py:49
  58.9 18.3 %collective-permute-start.11 = (bf16[4,72,432]{2,1,0:T(8,128)(2,1)}, bf16[4,72,432]{2,1,0:T(8,128)(2,1)S(1)}, u32[]{:S(2)}, u32[]{:S(2)}) collective-permute-start(bf16[4,72,432]{2,1,0:T(8,128)(2,1)} %shard_map.78.refs_4_.refs_0_), channel_id=1, source_target_pairs={{0,8},{1,9},{2,10},{3,11},{4,12},{5,13},{6,14},{7,15},{8,16},{9,17... | collective-permute-start | bytes 746504 | tf_op jit(solution)/shard_map/ppermute | solution.py:49
  72.7 9.7 %collective-permute-start.13 = (bf16[4,72,432]{2,1,0:T(8,128)(2,1)}, bf16[4,72,432]{2,1,0:T(8,128)(2,1)S(1)}, u32[]{:S(2)}, u32[]{:S(2)}) collective-permute-start(bf16[4,72,432]{2,1,0:T(8,128)(2,1)} %shard_map.78.refs_4_.refs_0_), channel_id=1, source_target_pairs={{8,0},{9,1},{10,2},{11,3},{12,4},{13,5},{14,6},{15,7},{16,8},{17,9... | collective-permute-start | bytes 746504 | tf_op jit(solution)/shard_map/ppermute | solution.py:49
  74.0 11.5 %collective-permute-start.14 = (bf16[4,72,432]{2,1,0:T(8,128)(2,1)S(1)}, bf16[4,72,432]{2,1,0:T(8,128)(2,1)S(1)}, u32[]{:S(2)}, u32[]{:S(2)}) collective-permute-start(bf16[4,72,432]{2,1,0:T(8,128)(2,1)S(1)} %collective-permute-done.12.refs_6_.refs_2_), channel_id=1, source_target_pairs={{8,0},{9,1},{10,2},{11,3},{12,4},{13,5},{14,6},{15,7},{16,24},{17,... | collective-permute-start | bytes 746504 | tf_op jit(solution)/shard_map/ppermute | solution.py:49
  111.4 28.5 %collective-permute-start.19 = (bf16[4,128,1152]{2,1,0:T(8,128)(2,1)}, bf16[4,128,1152]{2,1,0:T(8,128)(2,1)S(1)}, u32[]{:S(2)}, u32[]{:S(2)}) collective-permute-start(bf16[4,128,1152]{2,1,0:T(8,128)(2,1)} %get-tuple-element.24), channel_id=1, source_target_pairs={{0,2},{1,3},{2,0},{3,1},{4,6},{5,7},{6,4},{7,5},{8,10},{9,11},{10,... | collective-permute-start | bytes 3538952 | tf_op jit(solution)/shard_map/ppermute | solution.py:49
  111.4 12.0 %collective-permute-start.23 = (bf16[4,72,432]{2,1,0:T(8,128)(2,1)}, bf16[4,72,432]{2,1,0:T(8,128)(2,1)S(1)}, u32[]{:S(2)}, u32[]{:S(2)}) collective-permute-start(bf16[4,72,432]{2,1,0:T(8,128)(2,1)} %get-tuple-element.26), channel_id=1, source_target_pairs={{0,8},{1,9},{2,10},{3,11},{4,12},{5,13},{6,14},{7,15},{8,16},{9,17... | collective-permute-start | bytes 746504 | tf_op jit(solution)/shard_map/ppermute | solution.py:49
  111.4 23.9 %collective-permute-start.24 = (bf16[4,72,432]{2,1,0:T(8,128)(2,1)}, bf16[4,72,432]{2,1,0:T(8,128)(2,1)S(1)}, u32[]{:S(2)}, u32[]{:S(2)}) collective-permute-start(bf16[4,72,432]{2,1,0:T(8,128)(2,1)} %get-tuple-element.27), channel_id=1, source_target_pairs={{0,16},{1,17},{2,18},{3,19},{4,20},{5,21},{6,22},{7,23},{8,24},{9,... | collective-permute-start | bytes 746504 | tf_op jit(solution)/shard_map/ppermute | solution.py:49
  114.5 22.0 %collective-permute-start.25 = (bf16[4,72,432]{2,1,0:T(8,128)(2,1)}, bf16[4,72,432]{2,1,0:T(8,128)(2,1)}, u32[]{:S(2)}, u32[]{:S(2)}) collective-permute-start(bf16[4,72,432]{2,1,0:T(8,128)(2,1)} %get-tuple-element.28), channel_id=1, source_target_pairs={{0,24},{1,25},{2,26},{3,27},{4,28},{5,29},{6,30},{7,31},{8,0},{9,1... | collective-permute-start | bytes 746504 | tf_op jit(solution)/shard_map/ppermute | solution.py:49
  116.1 36.1 %collective-permute-start.33 = (bf16[72,1152]{1,0:T(8,128)(2,1)}, bf16[72,1152]{1,0:T(8,128)(2,1)}, u32[]{:S(2)}, u32[]{:S(2)}) collective-permute-start(bf16[72,1152]{1,0:T(8,128)(2,1)} %get-tuple-element.39), channel_id=1, source_target_pairs={{0,0},{1,3},{4,4},{5,7},{8,8},{9,11},{12,12},{13,15},{18,16},{19,1... | collective-permute-start | bytes 497672 | tf_op jit(solution)/shard_map/ppermute | solution.py:49
  123.5 28.9 %collective-permute-start.34 = (bf16[72,1152]{1,0:T(8,128)(2,1)}, bf16[72,1152]{1,0:T(8,128)(2,1)}, u32[]{:S(2)}, u32[]{:S(2)}) collective-permute-start(bf16[72,1152]{1,0:T(8,128)(2,1)} %get-tuple-element.42), channel_id=1, source_target_pairs={{0,8},{1,11},{4,12},{5,15},{10,16},{11,19},{14,20},{15,23},{18,24}... | collective-permute-start | bytes 497672 | tf_op jit(solution)/shard_map/ppermute | solution.py:49
  135.3 19.7 %collective-permute-start.35 = (bf16[72,1152]{1,0:T(8,128)(2,1)}, bf16[72,1152]{1,0:T(8,128)(2,1)}, u32[]{:S(2)}, u32[]{:S(2)}) collective-permute-start(bf16[72,1152]{1,0:T(8,128)(2,1)} %get-tuple-element.41), channel_id=1, source_target_pairs={{2,16},{3,19},{6,20},{7,23},{10,24},{11,27},{14,28},{15,31},{16,0}... | collective-permute-start | bytes 497672 | tf_op jit(solution)/shard_map/ppermute | solution.py:49
  136.6 19.8 %collective-permute-start.36 = (bf16[72,1152]{1,0:T(8,128)(2,1)}, bf16[72,1152]{1,0:T(8,128)(2,1)}, u32[]{:S(2)}, u32[]{:S(2)}) collective-permute-start(bf16[72,1152]{1,0:T(8,128)(2,1)} %get-tuple-element.40), channel_id=1, source_target_pairs={{2,24},{3,27},{6,28},{7,31},{8,0},{9,3},{12,4},{13,7},{16,8},{17,1... | collective-permute-start | bytes 497672 | tf_op jit(solution)/shard_map/ppermute | solution.py:49
  140.0 19.9 %collective-permute-start.27 = (bf16[72,432]{1,0:T(8,128)(2,1)}, bf16[72,432]{1,0:T(8,128)(2,1)S(1)}, u32[]{:S(2)}, u32[]{:S(2)}) collective-permute-start(bf16[72,432]{1,0:T(8,128)(2,1)} %get-tuple-element.30), channel_id=1, source_target_pairs={{0,2},{1,3},{2,0},{3,1},{4,6},{5,7},{6,4},{7,5},{8,10},{9,11},{10,... | collective-permute-start | bytes 186632 | tf_op jit(solution)/shard_map/ppermute | solution.py:49
  152.3 8.3 %collective-permute-start.28 = (bf16[72,432]{1,0:T(8,128)(2,1)S(1)}, bf16[72,432]{1,0:T(8,128)(2,1)S(1)}, u32[]{:S(2)}, u32[]{:S(2)}) collective-permute-start(bf16[72,432]{1,0:T(8,128)(2,1)S(1)} %copy-done.28), channel_id=1, source_target_pairs={{0,3},{1,2},{2,1},{3,0},{4,7},{5,6},{6,5},{7,4},{8,11},{9,10},{10,... | collective-permute-start | bytes 186632 | tf_op jit(solution)/shard_map/ppermute | solution.py:49
  155.0 8.3 %collective-permute-start.29 = (bf16[72,432]{1,0:T(8,128)(2,1)S(1)}, bf16[72,432]{1,0:T(8,128)(2,1)S(1)}, u32[]{:S(2)}, u32[]{:S(2)}) collective-permute-start(bf16[72,432]{1,0:T(8,128)(2,1)S(1)} %copy-done.27), channel_id=1, source_target_pairs={{0,4},{1,5},{2,6},{3,7},{4,0},{5,1},{6,2},{7,3},{8,12},{9,13},{10,... | collective-permute-start | bytes 186632 | tf_op jit(solution)/shard_map/ppermute | solution.py:49
  156.4 11.0 %collective-permute-start.30 = (bf16[72,432]{1,0:T(8,128)(2,1)S(1)}, bf16[72,432]{1,0:T(8,128)(2,1)}, u32[]{:S(2)}, u32[]{:S(2)}) collective-permute-start(bf16[72,432]{1,0:T(8,128)(2,1)S(1)} %copy-done.27), channel_id=1, source_target_pairs={{0,5},{1,4},{2,7},{3,6},{4,1},{5,0},{6,3},{7,2},{8,13},{9,12},{10,... | collective-permute-start | bytes 186632 | tf_op jit(solution)/shard_map/ppermute | solution.py:49
  158.5 24.5 %collective-permute-start.20 = (bf16[128,1152]{1,0:T(8,128)(2,1)S(1)}, bf16[128,1152]{1,0:T(8,128)(2,1)}, u32[]{:S(2)}, u32[]{:S(2)}) collective-permute-start(bf16[128,1152]{1,0:T(8,128)(2,1)S(1)} %get-tuple-element.36), channel_id=1, source_target_pairs={{0,4},{1,5},{2,6},{3,7},{4,0},{5,1},{6,2},{7,3},{8,12},{9,13},{10,... | collective-permute-start | bytes 884744 | tf_op jit(solution)/shard_map/ppermute | solution.py:49
  159.9 23.2 %collective-permute-start.21 = (bf16[128,1152]{1,0:T(8,128)(2,1)S(1)}, bf16[128,1152]{1,0:T(8,128)(2,1)}, u32[]{:S(2)}, u32[]{:S(2)}) collective-permute-start(bf16[128,1152]{1,0:T(8,128)(2,1)S(1)} %get-tuple-element.38), channel_id=1, source_target_pairs={{0,1},{1,0},{2,3},{3,2},{4,5},{5,4},{6,7},{7,6},{8,9},{9,8},{10,11... | collective-permute-start | bytes 884744 | tf_op jit(solution)/shard_map/ppermute | solution.py:49
  160.6 22.5 %collective-permute-start.22 = (bf16[128,1152]{1,0:T(8,128)(2,1)S(1)}, bf16[128,1152]{1,0:T(8,128)(2,1)}, u32[]{:S(2)}, u32[]{:S(2)}) collective-permute-start(bf16[128,1152]{1,0:T(8,128)(2,1)S(1)} %get-tuple-element.37), channel_id=1, source_target_pairs={{0,5},{1,4},{2,7},{3,6},{4,1},{5,0},{6,3},{7,2},{8,13},{9,12},{10,... | collective-permute-start | bytes 884744 | tf_op jit(solution)/shard_map/ppermute | solution.py:49
  164.0 14.5 %collective-permute-start.37 = (bf16[72,1152]{1,0:T(8,128)(2,1)S(1)}, bf16[72,1152]{1,0:T(8,128)(2,1)}, u32[]{:S(2)}, u32[]{:S(2)}) collective-permute-start(bf16[72,1152]{1,0:T(8,128)(2,1)S(1)} %add_convert_fusion.refs_8_), channel_id=1, source_target_pairs={{0,1},{3,2},{4,5},{7,6},{8,9},{11,10},{12,13},{15,14},{16,17},{19,... | collective-permute-start | bytes 497672 | tf_op jit(solution)/shard_map/ppermute | solution.py:49
  (35 other events, 343.2 us)
where the time goes:
time: 187 us; the launch traced here: 185 us
  starting transfers between devices  77.6 us (41%)
  waiting for transfers between devices  60 us (32%)
  Pallas kernels  36.3 us (19%)
  other arithmetic  7.02 us (4%)
  local copies, waits for them, and re-layouts  3 us (2%)
    ppermute x38, starting transfers between devices, send(): return lax.ppermute(value, BOTH, pairs)  77.6 us
    ppermute x38, waiting for transfers between devices, send(): return lax.ppermute(value, BOTH, pairs)  60 us
    pallas_call x1, Pallas kernels, local(): pl.pallas_call(functools.partial(attention_kernel, scale, 128, lines), ou...  20 us
    pallas_call x1, Pallas kernels, local(): own_part, other_part = input_call(at, dqkv, *planes)  5.09 us
    pallas_call x1, Pallas kernels, local(): pl.pallas_call(functools.partial(spread_kernel, dim), out_shape=shape_of(...  4.51 us
  transfers between devices with their start and end apart: 38, of which 15 were waited for; matrix products, arithmetic and copies ran while one was open for 3% of the time, Pallas kernels for 6%

commit v1 on v0

--- a/solution.py
+++ b/solution.py
@@ -15,6 +15,10 @@
 BOTH = ("pix", "rep")
 VMEM = pl.BlockSpec(memory_space=pltpu.VMEM)
 SMEM = pl.BlockSpec(memory_space=pltpu.SMEM)
+
+
+def room(mib):
+    return pltpu.CompilerParams(vmem_limit_bytes=mib << 20)
 
 
 def matmul(left, right, dims):
@@ -281,6 +285,7 @@
 
     pieces = pl.pallas_call(
         functools.partial(pack_kernel, dim),
+        compiler_params=room(8),
         out_shape=(shape_of(shard, 3 * wide),) * 4,
         in_specs=[SMEM, VMEM, VMEM, VMEM],
         out_specs=(VMEM,) * 4,
@@ -288,6 +293,7 @@
     pieces = [pieces[0]] + [grid.flip(pieces[n], n // 2, n % 2, 0) for n in range(1, 4)]
     plane = pl.pallas_call(
         plane_kernel,
+        compiler_params=room(8),
         out_shape=shape_of(4, shard, 3 * wide),
         in_specs=[SMEM] + [VMEM] * 4,
         out_specs=VMEM,
@@ -316,7 +322,8 @@
     ds, dc = gather_rows(drows)
 
     *grads_in, grad_out, dqkv = pl.pallas_call(
-        functools.partial(attention_kernel, scale, 128, lines),
+        functools.partial(attention_kernel, scale, BLOCK, lines),
+        compiler_params=room(28),
         out_shape=(shape_of(4, shard, 3 * wide),) * lines
         + (shape_of(wide, width), shape_of(total, 3 * wide)),
         in_specs=[SMEM] + [VMEM] * (4 + len(planes) + len(out_ws)),
@@ -335,6 +342,7 @@
 
     summed = pl.pallas_call(
         sum_kernel,
+        compiler_params=room(8),
         out_shape=(shape_of(shard, 3 * wide),) * 4,
         in_specs=[SMEM] + [VMEM] * lines,
         out_specs=(VMEM,) * 4,
@@ -373,6 +381,7 @@
 
     input_call = pl.pallas_call(
         functools.partial(input_kernel, lines),
+        compiler_params=room(20),
         out_shape=(shape_of(4, count, width),) * 2,
         in_specs=[SMEM] + [VMEM] * (1 + len(planes)),
         out_specs=(VMEM,) * 2,
@@ -387,12 +396,16 @@
     own_part, other_part = input_call(at, dqkv, *planes)
     pair = own_part.astype(jnp.float32) + grid.flip(other_part, 0, 1, 0).astype(jnp.float32)
     sent = pair.astype(jnp.bfloat16)
-    dinput = pair[0]
-    for i, (db, dy) in enumerate(((1, 0), (0, 1), (1, 1))):
-        dinput = dinput + grid.flip(sent[i + 1], db, 0, dy).astype(jnp.float32)
+    moves = [
+        grid.flip(sent[i + 1], db, 0, dy)
+        for i, (db, dy) in enumerate(((1, 0), (0, 1), (1, 1)))
+    ]
+    dinput = pair[0] + sum(move.astype(jnp.float32) for move in moves)
+    dinput = dinput.astype(jnp.bfloat16)
 
     grads = pl.pallas_call(
         functools.partial(spread_kernel, dim),
+        compiler_params=room(12),
         out_shape=shape_of(shard, 4 * width, dtype=jnp.float32),
         in_specs=[SMEM] + [VMEM] * 10,
         out_specs=VMEM,
@@ -401,7 +414,7 @@
     if grid.groups > 1:
         same = [[2 * g + y for g in range(grid.groups)] for y in range(2)]
         grads = lax.psum(grads, "rep", axis_index_groups=same)
-    return dinput.astype(jnp.bfloat16).reshape(tokens.shape), grads
+    return dinput.reshape(tokens.shape), grads
 
 
 def solution(mesh):

time: 187 us -> 172 us (0.920)
  Pallas kernels: 36.3 us -> 26.6 us
  waiting for transfers between devices: 60 us -> 67.2 us
  starting transfers between devices: 77.6 us -> 70.8 us
  other arithmetic: 7.02 us -> 3.98 us
  local copies, waits for them, and re-layouts: 3 us -> 0.81 us
    pallas_call x5, Pallas kernels: 31.2 us -> 22.7 us  [the longest x1 16 us: local(): pl.pallas_call(functools.partial(attention_kernel, scale, BLOCK, lines),...]
    ppermute x38, waiting for transfers between devices: 60 us -> 67.2 us  [send(): return lax.ppermute(value, BOTH, pairs)]
    ppermute x38, starting transfers between devices: 77.6 us -> 70.8 us  [send(): return lax.ppermute(value, BOTH, pairs)]
  transfers between devices with their start and end apart: 38 -> 38, of which waited for: 15 -> 15; matrix products, arithmetic and copies ran while one was open for 3% -> 2% of each run, Pallas kernels for 6% -> 4%
where the time goes in v1:
time: 172 us; the launch traced here: 170 us
  starting transfers between devices  70.8 us (41%)
  waiting for transfers between devices  67.2 us (39%)
  Pallas kernels  26.6 us (15%)
  other arithmetic  3.98 us (2%)
    ppermute x38, starting transfers between devices, send(): return lax.ppermute(value, BOTH, pairs)  70.8 us
    ppermute x38, waiting for transfers between devices, send(): return lax.ppermute(value, BOTH, pairs)  67.2 us
    pallas_call x1, Pallas kernels, local(): pl.pallas_call(functools.partial(attention_kernel, scale, BLOCK, lines),...  16 us
    pallas_call x1, Pallas kernels, local(): own_part, other_part = input_call(at, dqkv, *planes)  3.92 us
    pallas_call x1, Pallas kernels, local(): pl.pallas_call(functools.partial(spread_kernel, dim), compiler_params=roo...  3.79 us
  transfers between devices with their start and end apart: 38, of which 15 were waited for; matrix products, arithmetic and copies ran while one was open for 2% of the time, Pallas kernels for 4%

profile of v1, /device:TPU:0, one launch (start us, length us, event | category | flops | bytes accessed | tf_op | source)
XLA Modules:
  0.0 170.5 jit_solution(10724212697389547007)
XLA Ops:
  0.6 3.0 %collective-permute-start = (bf16[128,1152]{1,0:T(8,128)(2,1)}, bf16[128,1152]{1,0:T(8,128)(2,1)S(1)}, u32[]{:S(2)}, u32[]{:S(2)}) collective-permute-start(bf16[128,1152]{1,0:T(8,128)(2,1)} %bitcast.37), channel_id=1, source_target_pairs={{0,4},{1,5},{2,6},{3,7},{4,0},{5,1},{6,2},{7,3},{8,12},{9,13},{10,... | collective-permute-start | bytes 884744 | tf_op jit(solution)/shard_map/ppermute | solution.py:53
  5.2 1.9 %collective-permute-start.4 = (bf16[128,1152]{1,0:T(8,128)(2,1)}, bf16[128,1152]{1,0:T(8,128)(2,1)S(1)}, u32[]{:S(2)}, u32[]{:S(2)}) collective-permute-start(bf16[128,1152]{1,0:T(8,128)(2,1)} %bitcast.41), channel_id=1, source_target_pairs={{0,4},{1,5},{2,6},{3,7},{4,0},{5,1},{6,2},{7,3},{8,12},{9,13},{10,... | collective-permute-start | bytes 884744 | tf_op jit(solution)/shard_map/ppermute | solution.py:53
  8.7 3.1 %collective-permute-done = bf16[128,1152]{1,0:T(8,128)(2,1)S(1)} collective-permute-done((bf16[128,1152]{1,0:T(8,128)(2,1)}, bf16[128,1152]{1,0:T(8,128)(2,1)S(1)}, u32[]{:S(2)}, u32[]{:S(2)}) %collective-permute-start) | collective-permute-done | bytes 294944 | tf_op jit(solution)/shard_map/ppermute | solution.py:53
  11.7 3.0 %collective-permute-start.6 = (bf16[128,1152]{1,0:T(8,128)(2,1)}, bf16[128,1152]{1,0:T(8,128)(2,1)S(1)}, u32[]{:S(2)}, u32[]{:S(2)}) collective-permute-start(bf16[128,1152]{1,0:T(8,128)(2,1)} %bitcast.43), channel_id=1, source_target_pairs={{0,5},{1,4},{2,7},{3,6},{4,1},{5,0},{6,3},{7,2},{8,13},{9,12},{10,... | collective-permute-start | bytes 884744 | tf_op jit(solution)/shard_map/ppermute | solution.py:53
  14.7 5.4 %collective-permute-done.1 = bf16[128,1152]{1,0:T(8,128)(2,1)S(1)} collective-permute-done((bf16[128,1152]{1,0:T(8,128)(2,1)}, bf16[128,1152]{1,0:T(8,128)(2,1)S(1)}, u32[]{:S(2)}, u32[]{:S(2)}) %collective-permute-start.1) | collective-permute-done | bytes 294944 | tf_op jit(solution)/shard_map/ppermute | solution.py:53
  21.3 3.1 %collective-permute-done.4 = bf16[128,1152]{1,0:T(8,128)(2,1)S(1)} collective-permute-done((bf16[128,1152]{1,0:T(8,128)(2,1)}, bf16[128,1152]{1,0:T(8,128)(2,1)S(1)}, u32[]{:S(2)}, u32[]{:S(2)}) %collective-permute-start.4) | collective-permute-done | bytes 294944 | tf_op jit(solution)/shard_map/ppermute | solution.py:53
  24.4 6.9 %collective-permute-done.5 = bf16[128,1152]{1,0:T(8,128)(2,1)S(1)} collective-permute-done((bf16[128,1152]{1,0:T(8,128)(2,1)}, bf16[128,1152]{1,0:T(8,128)(2,1)S(1)}, u32[]{:S(2)}, u32[]{:S(2)}) %collective-permute-start.5) | collective-permute-done | bytes 294944 | tf_op jit(solution)/shard_map/ppermute | solution.py:53
  32.4 1.6 shard_map.77
  36.1 2.5 %collective-permute-done.10.refs_3_ = bf16[72,432]{1,0:T(8,128)(2,1)S(1)} collective-permute-done((bf16[72,432]{1,0:T(8,128)(2,1)S(1)}, bf16[72,432]{1,0:T(8,128)(2,1)S(1)}, u32[]{:S(2)}, u32[]{:S(2)}) %collective-permute-start.10) | collective-permute-done | bytes 62240 | tf_op jit(solution)/shard_map/ppermute | solution.py:53
  38.6 3.5 %collective-permute-start.16 = (bf16[72,1152]{1,0:T(8,128)(2,1)S(1)}, bf16[72,1152]{1,0:T(8,128)(2,1)S(1)}, u32[]{:S(2)}, u32[]{:S(2)}) collective-permute-start(bf16[72,1152]{1,0:T(8,128)(2,1)S(1)} %copy-done.6), channel_id=1, source_target_pairs={{0,8},{3,9},{4,12},{7,13},{8,16},{11,17},{12,20},{15,21},{16,26},{... | collective-permute-start | bytes 497672 | tf_op jit(solution)/shard_map/ppermute | solution.py:53
  43.4 3.1 %collective-permute-done.9.refs_2_ = bf16[72,432]{1,0:T(8,128)(2,1)S(1)} collective-permute-done((bf16[72,432]{1,0:T(8,128)(2,1)S(1)}, bf16[72,432]{1,0:T(8,128)(2,1)S(1)}, u32[]{:S(2)}, u32[]{:S(2)}) %collective-permute-start.9) | collective-permute-done | bytes 62240 | tf_op jit(solution)/shard_map/ppermute | solution.py:53
  47.1 2.4 %collective-permute-start.12 = (bf16[4,72,432]{2,1,0:T(8,128)(2,1)S(1)}, bf16[4,72,432]{2,1,0:T(8,128)(2,1)S(1)}, u32[]{:S(2)}, u32[]{:S(2)}) collective-permute-start(bf16[4,72,432]{2,1,0:T(8,128)(2,1)S(1)} %shard_map.78.refs_4_.refs_0_), channel_id=1, source_target_pairs={{0,16},{1,17},{2,18},{3,19},{4,20},{5,21},{6,22},{7,23},{8,24},{9,... | collective-permute-start | bytes 746504 | tf_op jit(solution)/shard_map/ppermute | solution.py:53
  49.4 2.5 %collective-permute-start.17 = (bf16[72,1152]{1,0:T(8,128)(2,1)S(1)}, bf16[72,1152]{1,0:T(8,128)(2,1)S(1)}, u32[]{:S(2)}, u32[]{:S(2)}) collective-permute-start(bf16[72,1152]{1,0:T(8,128)(2,1)S(1)} %copy-done.6), channel_id=1, source_target_pairs={{0,16},{3,17},{4,20},{7,21},{8,24},{11,25},{12,28},{15,29},{16,2},... | collective-permute-start | bytes 497672 | tf_op jit(solution)/shard_map/ppermute | solution.py:53
  52.0 2.9 %collective-permute-start.18 = (bf16[72,1152]{1,0:T(8,128)(2,1)S(1)}, bf16[72,1152]{1,0:T(8,128)(2,1)S(1)}, u32[]{:S(2)}, u32[]{:S(2)}) collective-permute-start(bf16[72,1152]{1,0:T(8,128)(2,1)S(1)} %copy-done.6), channel_id=1, source_target_pairs={{0,24},{3,25},{4,28},{7,29},{8,0},{11,1},{12,4},{15,5},{16,10},{19... | collective-permute-start | bytes 497672 | tf_op jit(solution)/shard_map/ppermute | solution.py:53
  55.5 13.7 %collective-permute-start.11 = (bf16[4,72,432]{2,1,0:T(8,128)(2,1)S(1)}, bf16[4,72,432]{2,1,0:T(8,128)(2,1)S(1)}, u32[]{:S(2)}, u32[]{:S(2)}) collective-permute-start(bf16[4,72,432]{2,1,0:T(8,128)(2,1)S(1)} %shard_map.78.refs_4_.refs_0_), channel_id=1, source_target_pairs={{0,8},{1,9},{2,10},{3,11},{4,12},{5,13},{6,14},{7,15},{8,16},{9,17... | collective-permute-start | bytes 746504 | tf_op jit(solution)/shard_map/ppermute | solution.py:53
  71.9 1.6 collective-permute-done.11.refs_5_.refs_1_
  73.5 5.3 %collective-permute-done.13.refs_7_.refs_3_ = bf16[4,72,432]{2,1,0:T(8,128)(2,1)S(1)} collective-permute-done((bf16[4,72,432]{2,1,0:T(8,128)(2,1)S(1)}, bf16[4,72,432]{2,1,0:T(8,128)(2,1)S(1)}, u32[]{:S(2)}, u32[]{:S(2)}) %collective-permute-start.13) | collective-permute-done | bytes 248864 | tf_op jit(solution)/shard_map/ppermute | solution.py:53
  78.8 3.2 %collective-permute-done.14.refs_8_.refs_4_ = bf16[4,72,432]{2,1,0:T(8,128)(2,1)S(1)} collective-permute-done((bf16[4,72,432]{2,1,0:T(8,128)(2,1)S(1)}, bf16[4,72,432]{2,1,0:T(8,128)(2,1)S(1)}, u32[]{:S(2)}, u32[]{:S(2)}) %collective-permute-start.14) | collective-permute-done | bytes 248864 | tf_op jit(solution)/shard_map/ppermute | solution.py:53
  82.0 16.0 %shard_map.79 = (bf16[4,72,432]{2,1,0:T(8,128)(2,1)S(1)}, bf16[4,72,432]{2,1,0:T(8,128)(2,1)S(1)}, bf16[4,72,432]{2,1,0:T(8,128)(2,1)S(1)}, bf16[4,72,432]{2,1,0...) custom-call(s32[4]{0:T(128)S(1)} %pad_add_fusion.at_ref, ...), custom_call_target="tpu_custom_call" | custom-call | flops 2717908992 | bytes 10485760 | tf_op jit(solution)/shard_map/pallas_call | solution.py:324
  98.0 3.9 %shard_map.80 = (bf16[4,128,1152]{2,1,0:T(8,128)(2,1)S(1)}, bf16[4,128,1152]{2,1,0:T(8,128)(2,1)}) custom-call(s32[4]{0:T(128)S(1)} %pad_add_fusion.at_ref, bf16[1024,432]{1,0:T(8,128)(2,1)S(1)} %get-tuple-element.22.dqkv_ref, bf16[4,72,432]{2,1,0:T(8,128)(2,1)S(1)} %shard_map.78.refs_4_.refs_0_, ...), custom_call_target="tpu_custom_call" | custom-call | flops 1019215872 | bytes 8388608 | tf_op jit(solution)/shard_map/pallas_call | solution.py:396
  102.1 3.3 %collective-permute-start.24 = (bf16[4,72,432]{2,1,0:T(8,128)(2,1)}, bf16[4,72,432]{2,1,0:T(8,128)(2,1)S(1)}, u32[]{:S(2)}, u32[]{:S(2)}) collective-permute-start(bf16[4,72,432]{2,1,0:T(8,128)(2,1)} %copy-done.3), channel_id=1, source_target_pairs={{0,16},{1,17},{2,18},{3,19},{4,20},{5,21},{6,22},{7,23},{8,24},{9,... | collective-permute-start | bytes 746504 | tf_op jit(solution)/shard_map/ppermute | solution.py:53
  106.7 7.5 %collective-permute-done.23.refs_1_ = bf16[4,72,432]{2,1,0:T(8,128)(2,1)S(1)} collective-permute-done((bf16[4,72,432]{2,1,0:T(8,128)(2,1)}, bf16[4,72,432]{2,1,0:T(8,128)(2,1)S(1)}, u32[]{:S(2)}, u32[]{:S(2)}) %collective-permute-start.23) | collective-permute-done | bytes 248864 | tf_op jit(solution)/shard_map/ppermute | solution.py:53
  114.1 1.9 %collective-permute-start.34 = (bf16[72,1152]{1,0:T(8,128)(2,1)S(1)}, bf16[72,1152]{1,0:T(8,128)(2,1)S(1)}, u32[]{:S(2)}, u32[]{:S(2)}) collective-permute-start(bf16[72,1152]{1,0:T(8,128)(2,1)S(1)} %get-tuple-element.42), channel_id=1, source_target_pairs={{0,8},{1,11},{4,12},{5,15},{10,16},{11,19},{14,20},{15,23},{18,24}... | collective-permute-start | bytes 497672 | tf_op jit(solution)/shard_map/ppermute | solution.py:53
  116.0 10.1 %collective-permute-done.24.refs_2_ = bf16[4,72,432]{2,1,0:T(8,128)(2,1)S(1)} collective-permute-done((bf16[4,72,432]{2,1,0:T(8,128)(2,1)}, bf16[4,72,432]{2,1,0:T(8,128)(2,1)S(1)}, u32[]{:S(2)}, u32[]{:S(2)}) %collective-permute-start.24) | collective-permute-done | bytes 248864 | tf_op jit(solution)/shard_map/ppermute | solution.py:53
  129.4 8.2 %collective-permute-start.27 = (bf16[72,432]{1,0:T(8,128)(2,1)S(1)}, bf16[72,432]{1,0:T(8,128)(2,1)S(1)}, u32[]{:S(2)}, u32[]{:S(2)}) collective-permute-start(bf16[72,432]{1,0:T(8,128)(2,1)S(1)} %get-tuple-element.30), channel_id=1, source_target_pairs={{0,2},{1,3},{2,0},{3,1},{4,6},{5,7},{6,4},{7,5},{8,10},{9,11},{10,... | collective-permute-start | bytes 186632 | tf_op jit(solution)/shard_map/ppermute | solution.py:53
  137.6 1.6 fusion.2
  143.2 2.2 %collective-permute-done.26.refs_1_ = bf16[72,432]{1,0:T(8,128)(2,1)S(1)} collective-permute-done((bf16[72,432]{1,0:T(8,128)(2,1)S(1)}, bf16[72,432]{1,0:T(8,128)(2,1)S(1)}, u32[]{:S(2)}, u32[]{:S(2)}) %collective-permute-start.26) | collective-permute-done | bytes 62240 | tf_op jit(solution)/shard_map/ppermute | solution.py:53
  146.8 2.1 %collective-permute-start.22 = (bf16[128,1152]{1,0:T(8,128)(2,1)S(1)}, bf16[128,1152]{1,0:T(8,128)(2,1)S(1)}, u32[]{:S(2)}, u32[]{:S(2)}) collective-permute-start(bf16[128,1152]{1,0:T(8,128)(2,1)S(1)} %get-tuple-element.37), channel_id=1, source_target_pairs={{0,5},{1,4},{2,7},{3,6},{4,1},{5,0},{6,3},{7,2},{8,13},{9,12},{10,... | collective-permute-start | bytes 884744 | tf_op jit(solution)/shard_map/ppermute | solution.py:53
  149.0 2.6 %collective-permute-start.37 = (bf16[72,1152]{1,0:T(8,128)(2,1)S(1)}, bf16[72,1152]{1,0:T(8,128)(2,1)S(1)}, u32[]{:S(2)}, u32[]{:S(2)}) collective-permute-start(bf16[72,1152]{1,0:T(8,128)(2,1)S(1)} %add_convert_fusion.refs_8_), channel_id=1, source_target_pairs={{0,1},{3,2},{4,5},{7,6},{8,9},{11,10},{12,13},{15,14},{16,17},{19,... | collective-permute-start | bytes 497672 | tf_op jit(solution)/shard_map/ppermute | solution.py:53
  151.7 9.4 %collective-permute-done.31.refs_6_ = bf16[72,432]{1,0:T(8,128)(2,1)S(1)} collective-permute-done((bf16[72,432]{1,0:T(8,128)(2,1)S(1)}, bf16[72,432]{1,0:T(8,128)(2,1)S(1)}, u32[]{:S(2)}, u32[]{:S(2)}) %collective-permute-start.31) | collective-permute-done | bytes 62240 | tf_op jit(solution)/shard_map/ppermute | solution.py:53
  162.5 3.3 %collective-permute-done.32.refs_7_ = bf16[72,432]{1,0:T(8,128)(2,1)S(1)} collective-permute-done((bf16[72,432]{1,0:T(8,128)(2,1)S(1)}, bf16[72,432]{1,0:T(8,128)(2,1)S(1)}, u32[]{:S(2)}, u32[]{:S(2)}) %collective-permute-start.32) | collective-permute-done | bytes 62240 | tf_op jit(solution)/shard_map/ppermute | solution.py:53
  165.8 3.8 %shard_map.82 = f32[72,4608]{1,0:T(8,128)} custom-call(s32[4]{0:T(128)S(1)} %pad_add_fusion.at_ref, bf16[72,432]{1,0:T(8,128)(2,1)S(1)} %get-tuple-element.29.refs_0_, bf16[72,432]{1,0:T(8,128)(2,1)S(1)} %collective-permute-done.26.refs_1_, bf16[72,432]{1,0:T(8,128)(2,1)S(1)} %collective-permute-done.27.refs_2_, ...), custom_call_target="tpu_custom_call" | custom-call | tf_op jit(solution)/shard_map/pallas_call | solution.py:406
  (72 shorter events, 24.9 us)
Async XLA Ops:
  0.6 11.1 %collective-permute-start = (bf16[128,1152]{1,0:T(8,128)(2,1)}, bf16[128,1152]{1,0:T(8,128)(2,1)S(1)}, u32[]{:S(2)}, u32[]{:S(2)}) collective-permute-start(bf16[128,1152]{1,0:T(8,128)(2,1)} %bitcast.37), channel_id=1, source_target_pairs={{0,4},{1,5},{2,6},{3,7},{4,0},{5,1},{6,2},{7,3},{8,12},{9,13},{10,... | collective-permute-start | bytes 884744 | tf_op jit(solution)/shard_map/ppermute | solution.py:53
  3.7 16.4 %collective-permute-start.1 = (bf16[128,1152]{1,0:T(8,128)(2,1)}, bf16[128,1152]{1,0:T(8,128)(2,1)S(1)}, u32[]{:S(2)}, u32[]{:S(2)}) collective-permute-start(bf16[128,1152]{1,0:T(8,128)(2,1)} %bitcast.38), channel_id=1, source_target_pairs={{0,1},{1,0},{2,3},{3,2},{4,5},{5,4},{6,7},{7,6},{8,9},{9,8},{10,11... | collective-permute-start | bytes 884744 | tf_op jit(solution)/shard_map/ppermute | solution.py:53
  5.2 14.9 %collective-permute-start.2 = (bf16[128,1152]{1,0:T(8,128)(2,1)}, bf16[128,1152]{1,0:T(8,128)(2,1)S(1)}, u32[]{:S(2)}, u32[]{:S(2)}) collective-permute-start(bf16[128,1152]{1,0:T(8,128)(2,1)} %bitcast.39), channel_id=1, source_target_pairs={{0,5},{1,4},{2,7},{3,6},{4,1},{5,0},{6,3},{7,2},{8,13},{9,12},{10,... | collective-permute-start | bytes 884744 | tf_op jit(solution)/shard_map/ppermute | solution.py:53
  5.2 19.2 %collective-permute-start.4 = (bf16[128,1152]{1,0:T(8,128)(2,1)}, bf16[128,1152]{1,0:T(8,128)(2,1)S(1)}, u32[]{:S(2)}, u32[]{:S(2)}) collective-permute-start(bf16[128,1152]{1,0:T(8,128)(2,1)} %bitcast.41), channel_id=1, source_target_pairs={{0,4},{1,5},{2,6},{3,7},{4,0},{5,1},{6,2},{7,3},{8,12},{9,13},{10,... | collective-permute-start | bytes 884744 | tf_op jit(solution)/shard_map/ppermute | solution.py:53
  7.2 24.1 %collective-permute-start.5 = (bf16[128,1152]{1,0:T(8,128)(2,1)}, bf16[128,1152]{1,0:T(8,128)(2,1)S(1)}, u32[]{:S(2)}, u32[]{:S(2)}) collective-permute-start(bf16[128,1152]{1,0:T(8,128)(2,1)} %bitcast.42), channel_id=1, source_target_pairs={{0,1},{1,0},{2,3},{3,2},{4,5},{5,4},{6,7},{7,6},{8,9},{9,8},{10,11... | collective-permute-start | bytes 884744 | tf_op jit(solution)/shard_map/ppermute | solution.py:53
  11.7 19.6 %collective-permute-start.6 = (bf16[128,1152]{1,0:T(8,128)(2,1)}, bf16[128,1152]{1,0:T(8,128)(2,1)S(1)}, u32[]{:S(2)}, u32[]{:S(2)}) collective-permute-start(bf16[128,1152]{1,0:T(8,128)(2,1)} %bitcast.43), channel_id=1, source_target_pairs={{0,5},{1,4},{2,7},{3,6},{4,1},{5,0},{6,3},{7,2},{8,13},{9,12},{10,... | collective-permute-start | bytes 884744 | tf_op jit(solution)/shard_map/ppermute | solution.py:53
  21.3 60.7 %collective-permute-start.3 = (bf16[4,128,1152]{2,1,0:T(8,128)(2,1)S(1)}, bf16[4,128,1152]{2,1,0:T(8,128)(2,1)}, u32[]{:S(2)}, u32[]{:S(2)}) collective-permute-start(bf16[4,128,1152]{2,1,0:T(8,128)(2,1)S(1)} %pad_maximum_fusion.refs_0_), channel_id=1, source_target_pairs={{0,2},{1,3},{2,0},{3,1},{4,6},{5,7},{6,4},{7,5},{8,10},{9,11},{10,... | collective-permute-start | bytes 3538952 | tf_op jit(solution)/shard_map/ppermute | solution.py:53
  31.5 50.4 %collective-permute-start.7 = (bf16[4,128,1152]{2,1,0:T(8,128)(2,1)S(1)}, bf16[4,128,1152]{2,1,0:T(8,128)(2,1)}, u32[]{:S(2)}, u32[]{:S(2)}) collective-permute-start(bf16[4,128,1152]{2,1,0:T(8,128)(2,1)S(1)} %pad_maximum_fusion.1.refs_2_), channel_id=1, source_target_pairs={{0,2},{1,3},{2,0},{3,1},{4,6},{5,7},{6,4},{7,5},{8,10},{9,11},{10,... | collective-permute-start | bytes 3538952 | tf_op jit(solution)/shard_map/ppermute | solution.py:53
  35.4 14.0 %collective-permute-start.15 = (bf16[72,1152]{1,0:T(8,128)(2,1)S(1)}, bf16[72,1152]{1,0:T(8,128)(2,1)S(1)}, u32[]{:S(2)}, u32[]{:S(2)}) collective-permute-start(bf16[72,1152]{1,0:T(8,128)(2,1)S(1)} %copy-done.6), channel_id=1, source_target_pairs={{0,0},{3,1},{4,4},{7,5},{8,8},{11,9},{12,12},{15,13},{16,18},{19,1... | collective-permute-start | bytes 497672 | tf_op jit(solution)/shard_map/ppermute | solution.py:53
  38.6 13.4 %collective-permute-start.16 = (bf16[72,1152]{1,0:T(8,128)(2,1)S(1)}, bf16[72,1152]{1,0:T(8,128)(2,1)S(1)}, u32[]{:S(2)}, u32[]{:S(2)}) collective-permute-start(bf16[72,1152]{1,0:T(8,128)(2,1)S(1)} %copy-done.6), channel_id=1, source_target_pairs={{0,8},{3,9},{4,12},{7,13},{8,16},{11,17},{12,20},{15,21},{16,26},{... | collective-permute-start | bytes 497672 | tf_op jit(solution)/shard_map/ppermute | solution.py:53
  47.1 23.5 %collective-permute-start.12 = (bf16[4,72,432]{2,1,0:T(8,128)(2,1)S(1)}, bf16[4,72,432]{2,1,0:T(8,128)(2,1)S(1)}, u32[]{:S(2)}, u32[]{:S(2)}) collective-permute-start(bf16[4,72,432]{2,1,0:T(8,128)(2,1)S(1)} %shard_map.78.refs_4_.refs_0_), channel_id=1, source_target_pairs={{0,16},{1,17},{2,18},{3,19},{4,20},{5,21},{6,22},{7,23},{8,24},{9,... | collective-permute-start | bytes 746504 | tf_op jit(solution)/shard_map/ppermute | solution.py:53
  52.0 17.3 %collective-permute-start.18 = (bf16[72,1152]{1,0:T(8,128)(2,1)S(1)}, bf16[72,1152]{1,0:T(8,128)(2,1)S(1)}, u32[]{:S(2)}, u32[]{:S(2)}) collective-permute-start(bf16[72,1152]{1,0:T(8,128)(2,1)S(1)} %copy-done.6), channel_id=1, source_target_pairs={{0,24},{3,25},{4,28},{7,29},{8,0},{11,1},{12,4},{15,5},{16,10},{19... | collective-permute-start | bytes 497672 | tf_op jit(solution)/shard_map/ppermute | solution.py:53
  55.5 18.0 %collective-permute-start.11 = (bf16[4,72,432]{2,1,0:T(8,128)(2,1)S(1)}, bf16[4,72,432]{2,1,0:T(8,128)(2,1)S(1)}, u32[]{:S(2)}, u32[]{:S(2)}) collective-permute-start(bf16[4,72,432]{2,1,0:T(8,128)(2,1)S(1)} %shard_map.78.refs_4_.refs_0_), channel_id=1, source_target_pairs={{0,8},{1,9},{2,10},{3,11},{4,12},{5,13},{6,14},{7,15},{8,16},{9,17... | collective-permute-start | bytes 746504 | tf_op jit(solution)/shard_map/ppermute | solution.py:53
  69.3 9.5 %collective-permute-start.13 = (bf16[4,72,432]{2,1,0:T(8,128)(2,1)S(1)}, bf16[4,72,432]{2,1,0:T(8,128)(2,1)S(1)}, u32[]{:S(2)}, u32[]{:S(2)}) collective-permute-start(bf16[4,72,432]{2,1,0:T(8,128)(2,1)S(1)} %shard_map.78.refs_4_.refs_0_), channel_id=1, source_target_pairs={{8,0},{9,1},{10,2},{11,3},{12,4},{13,5},{14,6},{15,7},{16,8},{17,9... | collective-permute-start | bytes 746504 | tf_op jit(solution)/shard_map/ppermute | solution.py:53
  70.6 11.4 %collective-permute-start.14 = (bf16[4,72,432]{2,1,0:T(8,128)(2,1)S(1)}, bf16[4,72,432]{2,1,0:T(8,128)(2,1)S(1)}, u32[]{:S(2)}, u32[]{:S(2)}) collective-permute-start(bf16[4,72,432]{2,1,0:T(8,128)(2,1)S(1)} %collective-permute-done.12.refs_6_.refs_2_), channel_id=1, source_target_pairs={{8,0},{9,1},{10,2},{11,3},{12,4},{13,5},{14,6},{15,7},{16,24},{17,... | collective-permute-start | bytes 746504 | tf_op jit(solution)/shard_map/ppermute | solution.py:53
  102.0 27.5 %collective-permute-start.19 = (bf16[4,128,1152]{2,1,0:T(8,128)(2,1)}, bf16[4,128,1152]{2,1,0:T(8,128)(2,1)}, u32[]{:S(2)}, u32[]{:S(2)}) collective-permute-start(bf16[4,128,1152]{2,1,0:T(8,128)(2,1)} %get-tuple-element.24), channel_id=1, source_target_pairs={{0,2},{1,3},{2,0},{3,1},{4,6},{5,7},{6,4},{7,5},{8,10},{9,11},{10,... | collective-permute-start | bytes 3538952 | tf_op jit(solution)/shard_map/ppermute | solution.py:53
  102.0 12.1 %collective-permute-start.23 = (bf16[4,72,432]{2,1,0:T(8,128)(2,1)}, bf16[4,72,432]{2,1,0:T(8,128)(2,1)S(1)}, u32[]{:S(2)}, u32[]{:S(2)}) collective-permute-start(bf16[4,72,432]{2,1,0:T(8,128)(2,1)} %copy-done.4), channel_id=1, source_target_pairs={{0,8},{1,9},{2,10},{3,11},{4,12},{5,13},{6,14},{7,15},{8,16},{9,17... | collective-permute-start | bytes 746504 | tf_op jit(solution)/shard_map/ppermute | solution.py:53
  102.1 24.0 %collective-permute-start.24 = (bf16[4,72,432]{2,1,0:T(8,128)(2,1)}, bf16[4,72,432]{2,1,0:T(8,128)(2,1)S(1)}, u32[]{:S(2)}, u32[]{:S(2)}) collective-permute-start(bf16[4,72,432]{2,1,0:T(8,128)(2,1)} %copy-done.3), channel_id=1, source_target_pairs={{0,16},{1,17},{2,18},{3,19},{4,20},{5,21},{6,22},{7,23},{8,24},{9,... | collective-permute-start | bytes 746504 | tf_op jit(solution)/shard_map/ppermute | solution.py:53
  105.4 22.0 %collective-permute-start.25 = (bf16[4,72,432]{2,1,0:T(8,128)(2,1)S(1)}, bf16[4,72,432]{2,1,0:T(8,128)(2,1)S(1)}, u32[]{:S(2)}, u32[]{:S(2)}) collective-permute-start(bf16[4,72,432]{2,1,0:T(8,128)(2,1)S(1)} %get-tuple-element.28), channel_id=1, source_target_pairs={{0,24},{1,25},{2,26},{3,27},{4,28},{5,29},{6,30},{7,31},{8,0},{9,1... | collective-permute-start | bytes 746504 | tf_op jit(solution)/shard_map/ppermute | solution.py:53
  106.0 33.2 %collective-permute-start.33 = (bf16[72,1152]{1,0:T(8,128)(2,1)S(1)}, bf16[72,1152]{1,0:T(8,128)(2,1)S(1)}, u32[]{:S(2)}, u32[]{:S(2)}) collective-permute-start(bf16[72,1152]{1,0:T(8,128)(2,1)S(1)} %get-tuple-element.39), channel_id=1, source_target_pairs={{0,0},{1,3},{4,4},{5,7},{8,8},{9,11},{12,12},{13,15},{18,16},{19,1... | collective-permute-start | bytes 497672 | tf_op jit(solution)/shard_map/ppermute | solution.py:53
  114.1 25.5 %collective-permute-start.34 = (bf16[72,1152]{1,0:T(8,128)(2,1)S(1)}, bf16[72,1152]{1,0:T(8,128)(2,1)S(1)}, u32[]{:S(2)}, u32[]{:S(2)}) collective-permute-start(bf16[72,1152]{1,0:T(8,128)(2,1)S(1)} %get-tuple-element.42), channel_id=1, source_target_pairs={{0,8},{1,11},{4,12},{5,15},{10,16},{11,19},{14,20},{15,23},{18,24}... | collective-permute-start | bytes 497672 | tf_op jit(solution)/shard_map/ppermute | solution.py:53
  126.1 14.9 %collective-permute-start.35 = (bf16[72,1152]{1,0:T(8,128)(2,1)S(1)}, bf16[72,1152]{1,0:T(8,128)(2,1)S(1)}, u32[]{:S(2)}, u32[]{:S(2)}) collective-permute-start(bf16[72,1152]{1,0:T(8,128)(2,1)S(1)} %get-tuple-element.41), channel_id=1, source_target_pairs={{2,16},{3,19},{6,20},{7,23},{10,24},{11,27},{14,28},{15,31},{16,0}... | collective-permute-start | bytes 497672 | tf_op jit(solution)/shard_map/ppermute | solution.py:53
  127.4 14.9 %collective-permute-start.36 = (bf16[72,1152]{1,0:T(8,128)(2,1)S(1)}, bf16[72,1152]{1,0:T(8,128)(2,1)S(1)}, u32[]{:S(2)}, u32[]{:S(2)}) collective-permute-start(bf16[72,1152]{1,0:T(8,128)(2,1)S(1)} %get-tuple-element.40), channel_id=1, source_target_pairs={{2,24},{3,27},{6,28},{7,31},{8,0},{9,3},{12,4},{13,7},{16,8},{17,1... | collective-permute-start | bytes 497672 | tf_op jit(solution)/shard_map/ppermute | solution.py:53
  129.4 17.3 %collective-permute-start.27 = (bf16[72,432]{1,0:T(8,128)(2,1)S(1)}, bf16[72,432]{1,0:T(8,128)(2,1)S(1)}, u32[]{:S(2)}, u32[]{:S(2)}) collective-permute-start(bf16[72,432]{1,0:T(8,128)(2,1)S(1)} %get-tuple-element.30), channel_id=1, source_target_pairs={{0,2},{1,3},{2,0},{3,1},{4,6},{5,7},{6,4},{7,5},{8,10},{9,11},{10,... | collective-permute-start | bytes 186632 | tf_op jit(solution)/shard_map/ppermute | solution.py:53
  139.2 7.6 %collective-permute-start.28 = (bf16[72,432]{1,0:T(8,128)(2,1)S(1)}, bf16[72,432]{1,0:T(8,128)(2,1)S(1)}, u32[]{:S(2)}, u32[]{:S(2)}) collective-permute-start(bf16[72,432]{1,0:T(8,128)(2,1)S(1)} %get-tuple-element.30), channel_id=1, source_target_pairs={{0,3},{1,2},{2,1},{3,0},{4,7},{5,6},{6,5},{7,4},{8,11},{9,10},{10,... | collective-permute-start | bytes 186632 | tf_op jit(solution)/shard_map/ppermute | solution.py:53
  141.0 8.0 %collective-permute-start.29 = (bf16[72,432]{1,0:T(8,128)(2,1)S(1)}, bf16[72,432]{1,0:T(8,128)(2,1)S(1)}, u32[]{:S(2)}, u32[]{:S(2)}) collective-permute-start(bf16[72,432]{1,0:T(8,128)(2,1)S(1)} %get-tuple-element.31), channel_id=1, source_target_pairs={{0,4},{1,5},{2,6},{3,7},{4,0},{5,1},{6,2},{7,3},{8,12},{9,13},{10,... | collective-permute-start | bytes 186632 | tf_op jit(solution)/shard_map/ppermute | solution.py:53
  142.3 9.3 %collective-permute-start.30 = (bf16[72,432]{1,0:T(8,128)(2,1)S(1)}, bf16[72,432]{1,0:T(8,128)(2,1)S(1)}, u32[]{:S(2)}, u32[]{:S(2)}) collective-permute-start(bf16[72,432]{1,0:T(8,128)(2,1)S(1)} %get-tuple-element.31), channel_id=1, source_target_pairs={{0,5},{1,4},{2,7},{3,6},{4,1},{5,0},{6,3},{7,2},{8,13},{9,12},{10,... | collective-permute-start | bytes 186632 | tf_op jit(solution)/shard_map/ppermute | solution.py:53
  145.4 24.2 %collective-permute-start.20 = (bf16[128,1152]{1,0:T(8,128)(2,1)S(1)}, bf16[128,1152]{1,0:T(8,128)(2,1)S(1)}, u32[]{:S(2)}, u32[]{:S(2)}) collective-permute-start(bf16[128,1152]{1,0:T(8,128)(2,1)S(1)} %get-tuple-element.36), channel_id=1, source_target_pairs={{0,4},{1,5},{2,6},{3,7},{4,0},{5,1},{6,2},{7,3},{8,12},{9,13},{10,... | collective-permute-start | bytes 884744 | tf_op jit(solution)/shard_map/ppermute | solution.py:53
  146.7 22.9 %collective-permute-start.21 = (bf16[128,1152]{1,0:T(8,128)(2,1)S(1)}, bf16[128,1152]{1,0:T(8,128)(2,1)S(1)}, u32[]{:S(2)}, u32[]{:S(2)}) collective-permute-start(bf16[128,1152]{1,0:T(8,128)(2,1)S(1)} %get-tuple-element.38), channel_id=1, source_target_pairs={{0,1},{1,0},{2,3},{3,2},{4,5},{5,4},{6,7},{7,6},{8,9},{9,8},{10,11... | collective-permute-start | bytes 884744 | tf_op jit(solution)/shard_map/ppermute | solution.py:53
  146.8 22.8 %collective-permute-start.22 = (bf16[128,1152]{1,0:T(8,128)(2,1)S(1)}, bf16[128,1152]{1,0:T(8,128)(2,1)S(1)}, u32[]{:S(2)}, u32[]{:S(2)}) collective-permute-start(bf16[128,1152]{1,0:T(8,128)(2,1)S(1)} %get-tuple-element.37), channel_id=1, source_target_pairs={{0,5},{1,4},{2,7},{3,6},{4,1},{5,0},{6,3},{7,2},{8,13},{9,12},{10,... | collective-permute-start | bytes 884744 | tf_op jit(solution)/shard_map/ppermute | solution.py:53
  149.0 16.8 %collective-permute-start.37 = (bf16[72,1152]{1,0:T(8,128)(2,1)S(1)}, bf16[72,1152]{1,0:T(8,128)(2,1)S(1)}, u32[]{:S(2)}, u32[]{:S(2)}) collective-permute-start(bf16[72,1152]{1,0:T(8,128)(2,1)S(1)} %add_convert_fusion.refs_8_), channel_id=1, source_target_pairs={{0,1},{3,2},{4,5},{7,6},{8,9},{11,10},{12,13},{15,14},{16,17},{19,... | collective-permute-start | bytes 497672 | tf_op jit(solution)/shard_map/ppermute | solution.py:53
  151.6 9.5 %collective-permute-start.31 = (bf16[72,432]{1,0:T(8,128)(2,1)S(1)}, bf16[72,432]{1,0:T(8,128)(2,1)S(1)}, u32[]{:S(2)}, u32[]{:S(2)}) collective-permute-start(bf16[72,432]{1,0:T(8,128)(2,1)S(1)} %get-tuple-element.32), channel_id=1, source_target_pairs={{0,6},{1,7},{2,4},{3,5},{4,2},{5,3},{6,0},{7,1},{8,14},{9,15},{10,... | collective-permute-start | bytes 186632 | tf_op jit(solution)/shard_map/ppermute | solution.py:53
  (13 other events, 59.2 us)

commit v2 on v1

--- a/solution.py
+++ b/solution.py
@@ -85,9 +85,32 @@
             found[1], found[last], found[lines] = up, down, ends
         return [found[s] for s in range(len(found))]
 
+    def scatter_lines(self, values):
+        lines = self.lines
+        if lines != 4:
+            return [values[0]] + [self.shift(values[s], s) for s in range(1, lines)]
+
+        def way(hops):
+            return lambda a, b, c, g, y: (hops[a], b, c, g, y) if a in hops else None
+
+        relay = self.send(values[4], way({0: 1, 3: 2}))
+        terms = [
+            values[0],
+            self.send(values[2], way({0: 2, 3: 1})),
+            self.send(values[1], way({0: 1, 1: 2, 2: 3})),
+            self.send(values[3], way({1: 0, 2: 1, 3: 2})),
+        ]
+        both = values[2].astype(jnp.float32) + relay.astype(jnp.float32)
+        return terms + [self.send(both.astype(jnp.bfloat16), way({1: 3, 2: 0}))]
+
 
 def pack_kernel(dim, at_ref, *refs):
-    weights, outs = refs[:3], refs[3:]
+    sources, outs, weights, sems = refs[:3], refs[3:7], refs[7:10], refs[10]
+    copies = [pltpu.make_async_copy(sources[w], weights[w], sems.at[w]) for w in range(3)]
+    for copy in copies:
+        copy.start()
+    for copy in copies:
+        copy.wait()
     even, b_here, c_here = at_ref[3] == 0, at_ref[1], at_ref[2]
     values = [ref[...] for ref in weights]
     for b in range(2):
@@ -110,24 +133,35 @@
 def plane_kernel(at_ref, *refs):
     *pieces, out_ref = refs
     here = 2 * at_ref[1] + at_ref[2]
+    wide = pieces[0].shape[1]
     for n, piece in enumerate(pieces):
-        out_ref[here ^ n] = piece[...]
+        index = here ^ n
+        for side in range(2):
+
+            @pl.when(index % 2 == side)
+            def _(side=side, piece=piece, index=index):
+                out_ref[index // 2, :, side * wide : (side + 1) * wide] = piece[...]
 
 
 def sum_kernel(at_ref, *refs):
     parts, outs = refs[: len(refs) - 4], refs[len(refs) - 4 :]
     here = 2 * at_ref[1] + at_ref[2]
+    wide = outs[0].shape[1]
     for n, out in enumerate(outs):
-        out[...] = sum(p[here ^ n].astype(jnp.float32) for p in parts).astype(jnp.bfloat16)
-
-
-def attend(query, keyed, valued, dattn, scale):
-    rows = query.shape[0]
-    site = lambda axis: lax.broadcasted_iota(jnp.int32, (rows, rows), axis) // FRAMES
-    scores = matmul(query, keyed, ((1,), (1,))) * scale
-    scores = jnp.where(site(0) == site(1), scores, -1e30)
+        index = here ^ n
+        for side in range(2):
+
+            @pl.when(index % 2 == side)
+            def _(side=side, out=out, index=index):
+                cut = slice(side * wide, (side + 1) * wide)
+                total = sum(p[index // 2, :, cut].astype(jnp.float32) for p in parts)
+                out[...] = total.astype(jnp.bfloat16)
+
+
+def attend(query, keyed, valued, dattn, scale, bias):
+    scores = matmul(query, keyed, ((1,), (1,))) * scale + bias
     expo = jnp.exp(scores - jnp.max(scores, axis=1, keepdims=True))
-    probs = expo / jnp.sum(expo, axis=1, keepdims=True)
+    probs = expo * (1.0 / jnp.sum(expo, axis=1, keepdims=True))
     probs_b = probs.astype(jnp.bfloat16)
     attended = matmul(probs_b, valued, ((1,), (0,)))
     dvalue = matmul(probs_b, dattn, ((0,), (0,)))
@@ -142,7 +176,8 @@
 def full_weights(lines, at_ref, planes, loose, full):
     def store(plane, line):
         for n in range(4):
-            loose[4 * line + n] = plane[n]
+            side = (n % 2) * loose.shape[2]
+            loose[4 * line + n] = plane[n // 2, :, side : side + loose.shape[2]]
 
     last = lines - 1
     for s in range(lines):
@@ -158,12 +193,13 @@
         full[p * shard : (p + 1) * shard, :] = loose[p]
 
 
-def attention_kernel(scale, sub, lines, at_ref, *refs):
+def attention_kernel(scale, lines, at_ref, *refs):
     xs, xc, ds, dc = refs[:4]
     moved = 4 + lines + (lines > 2)
-    planes, out_ws = refs[4:moved], refs[moved : len(refs) - lines - 7]
-    grads_in = refs[len(refs) - lines - 7 : len(refs) - 7]
-    grad_out, dqkv_ref, full, loose, out_w, att, grads = refs[len(refs) - 7 :]
+    sent = lines + (lines == 4)
+    planes, out_ws = refs[4:moved], refs[moved : len(refs) - sent - 8]
+    grads_in = refs[len(refs) - sent - 8 : len(refs) - 8]
+    grad_out, dqkv_ref, full, loose, out_w, att, grads, bias = refs[len(refs) - 8 :]
     shard, wide = loose.shape[1:]
     dim = wide // (3 * KEPT)
     width = xs.shape[-1]
@@ -179,6 +215,8 @@
                 def _(k=k, held=held):
                     out_w[k * dim : (k + 1) * dim, :] = held[...]
 
+    site = lambda axis: lax.broadcasted_iota(jnp.int32, (BLOCK, BLOCK), axis) // FRAMES
+    bias[...] = jnp.where(site(0) == site(1), 0.0, -1e30)
     half = xs.shape[0] * xs.shape[1]
     each = BLOCK // xs.shape[1]
     for part, (x_ref, d_ref) in enumerate(((xs, ds), (xc, dc))):
@@ -189,19 +227,22 @@
             qkv = matmul(x, full[...], ((1,), (0,))).astype(jnp.bfloat16)
             da = matmul(d, out_w[...], ((1,), (1,))).astype(jnp.bfloat16)
             row = pl.multiple_of(part * half + j * BLOCK, BLOCK)
-            for low in range(0, BLOCK, sub):
-                outs = []
-                for k in range(KEPT):
-                    cut = lambda v, n: v[low : low + sub, n * dim : (n + 1) * dim]
-                    outs.append(
-                        attend(
-                            cut(qkv, k), cut(qkv, KEPT + k), cut(qkv, 2 * KEPT + k), cut(da, k), scale
-                        )
-                    )
-                att[pl.ds(row + low, sub), :] = jnp.concatenate([o[0] for o in outs], axis=1)
-                dqkv_ref[pl.ds(row + low, sub), :] = jnp.concatenate(
-                    [outs[k][n] for n in (1, 2, 3) for k in range(KEPT)], axis=1
+            cut = lambda v, n: v[:, n * dim : (n + 1) * dim]
+            outs = [
+                attend(
+                    cut(qkv, k),
+                    cut(qkv, KEPT + k),
+                    cut(qkv, 2 * KEPT + k),
+                    cut(da, k),
+                    scale,
+                    bias[...],
                 )
+                for k in range(KEPT)
+            ]
+            att[pl.ds(row, BLOCK), :] = jnp.concatenate([o[0] for o in outs], axis=1)
+            dqkv_ref[pl.ds(row, BLOCK), :] = jnp.concatenate(
+                [outs[k][n] for n in (1, 2, 3) for k in range(KEPT)], axis=1
+            )
             return 0
 
         lax.fori_loop(0, half // BLOCK, block, 0)
@@ -221,8 +262,10 @@
         loose[p] = grads[p * shard : (p + 1) * shard, :].astype(jnp.bfloat16)
     for s, out in enumerate(grads_in):
         line = lax.rem(at_ref[0] + s, lines)
+        if s == lines:
+            line = jnp.where(at_ref[0] == 0, lines - 1, 0)
         for n in range(4):
-            out[n] = loose[4 * line + n]
+            out[n // 2, :, (n % 2) * wide : (n % 2 + 1) * wide] = loose[4 * line + n]
 
 
 def input_kernel(lines, at_ref, dqkv_ref, *refs):
@@ -243,23 +286,28 @@
 
 def spread_kernel(dim, at_ref, *refs):
     *pieces, kept_ref, moved_ref, out_ref, table = refs
-    width = HEADS * dim
-    for n, piece in enumerate(pieces):
-        db, dc, dy = n // 4, (n // 2) % 2, n % 2
-        b = lax.rem(at_ref[1] + db, 2)
-        c = lax.rem(at_ref[2] + dc, 2)
-        y = lax.rem(at_ref[3] + dy, 2)
-        table[4 * b + 2 * c + y] = piece[...].astype(jnp.float32)
-    for b in range(2):
-        for c in range(2):
-            first, second = table[4 * b + 2 * c], table[4 * b + 2 * c + 1]
-            for w in range(3):
-                for k in range(KEPT):
-                    piece = slice((w * KEPT + k) * dim, (w * KEPT + k + 1) * dim)
-                    low = w * width + (8 * c + 4 * k + 2 * b) * dim
-                    both = jnp.concatenate([first[:, piece], second[:, piece]], axis=1)
-                    out_ref[:, low : low + 2 * dim] = both
-    out_ref[:, 3 * width :] = kept_ref[...].astype(jnp.float32) + moved_ref[...].astype(jnp.float32)
+    step = pl.program_id(0)
+
+    @pl.when(step == 0)
+    def _():
+        for n, piece in enumerate(pieces):
+            db, dc, dy = n // 4, (n // 2) % 2, n % 2
+            b = lax.rem(at_ref[1] + db, 2)
+            c = lax.rem(at_ref[2] + dc, 2)
+            y = lax.rem(at_ref[3] + dy, 2)
+            table[4 * b + 2 * c + y] = piece[...]
+        out_ref[...] = kept_ref[...].astype(jnp.float32) + moved_ref[...].astype(jnp.float32)
+
+    for w in range(3):
+
+        @pl.when(step == w + 1)
+        def _(w=w):
+            heads = []
+            for h in range(HEADS):
+                c, k, b, y = h // 8, (h // 4) % 2, (h // 2) % 2, h % 2
+                low = (w * KEPT + k) * dim
+                heads.append(table[4 * b + 2 * c + y, :, low : low + dim].astype(jnp.float32))
+            out_ref[...] = jnp.concatenate(heads, axis=1)
 
 
 def local(pix, rep, tokens, out_grad, query_weight, key_weight, value_weight, output_weight):
@@ -287,14 +335,16 @@
         functools.partial(pack_kernel, dim),
         compiler_params=room(8),
         out_shape=(shape_of(shard, 3 * wide),) * 4,
-        in_specs=[SMEM, VMEM, VMEM, VMEM],
+        in_specs=[SMEM] + [pl.BlockSpec(memory_space=pltpu.HBM)] * 3,
         out_specs=(VMEM,) * 4,
+        scratch_shapes=[pltpu.VMEM((shard, width), jnp.bfloat16)] * 3
+        + [pltpu.SemaphoreType.DMA((3,))],
     )(at, query_weight, key_weight, value_weight)
     pieces = [pieces[0]] + [grid.flip(pieces[n], n // 2, n % 2, 0) for n in range(1, 4)]
     plane = pl.pallas_call(
         plane_kernel,
         compiler_params=room(8),
-        out_shape=shape_of(4, shard, 3 * wide),
+        out_shape=shape_of(2, shard, 6 * wide),
         in_specs=[SMEM] + [VMEM] * 4,
         out_specs=VMEM,
     )(at, *pieces)
@@ -321,32 +371,35 @@
         out_ws = [out_w]
     ds, dc = gather_rows(drows)
 
+    sent = lines + (lines == 4)
     *grads_in, grad_out, dqkv = pl.pallas_call(
-        functools.partial(attention_kernel, scale, BLOCK, lines),
+        functools.partial(attention_kernel, scale, lines),
         compiler_params=room(28),
-        out_shape=(shape_of(4, shard, 3 * wide),) * lines
+        out_shape=(shape_of(2, shard, 6 * wide),) * sent
         + (shape_of(wide, width), shape_of(total, 3 * wide)),
         in_specs=[SMEM] + [VMEM] * (4 + len(planes) + len(out_ws)),
-        out_specs=(VMEM,) * (lines + 2),
+        out_specs=(VMEM,) * (sent + 2),
         scratch_shapes=[
             pltpu.VMEM((width, 3 * wide), jnp.bfloat16),
             pltpu.VMEM((pix, shard, 3 * wide), jnp.bfloat16),
             pltpu.VMEM((wide, width), jnp.bfloat16),
             pltpu.VMEM((total, wide), jnp.bfloat16),
             pltpu.VMEM((width, 3 * wide), jnp.float32),
+            pltpu.VMEM((BLOCK, BLOCK), jnp.float32),
         ],
         cost_estimate=pl.CostEstimate(
             flops=8 * total * width * wide * 2, bytes_accessed=10 << 20, transcendentals=total * 32
         ),
     )(at, xs, xc, ds, dc, *planes, *out_ws)
 
+    parts = grid.scatter_lines(grads_in)
     summed = pl.pallas_call(
         sum_kernel,
         compiler_params=room(8),
         out_shape=(shape_of(shard, 3 * wide),) * 4,
-        in_specs=[SMEM] + [VMEM] * lines,
+        in_specs=[SMEM] + [VMEM] * len(parts),
         out_specs=(VMEM,) * 4,
-    )(at, grads_in[0], *[grid.shift(grads_in[s], s) for s in range(1, lines)])
+    )(at, *parts)
     square = []
     for n in range(8):
         block = summed[n // 2]
@@ -407,9 +460,10 @@
         functools.partial(spread_kernel, dim),
         compiler_params=room(12),
         out_shape=shape_of(shard, 4 * width, dtype=jnp.float32),
+        grid=(4,),
         in_specs=[SMEM] + [VMEM] * 10,
-        out_specs=VMEM,
-        scratch_shapes=[pltpu.VMEM((8, shard, 3 * wide), jnp.float32)],
+        out_specs=pl.BlockSpec((shard, width), lambda i: (0, (i + 3) % 4)),
+        scratch_shapes=[pltpu.VMEM((8, shard, 3 * wide), jnp.bfloat16)],
     )(at, *square, kept, moved)
     if grid.groups > 1:
         same = [[2 * g + y for g in range(grid.groups)] for y in range(2)]

time: 172 us -> 166 us (0.965)
  waiting for transfers between devices: 67.2 us -> 58.4 us
  starting transfers between devices: 70.8 us -> 73 us
    ppermute x38 -> x40, waiting for transfers between devices: 67.2 us -> 58.4 us  [send(): return lax.ppermute(value, BOTH, pairs)]
    ppermute x38 -> x40, starting transfers between devices: 70.8 us -> 73 us  [send(): return lax.ppermute(value, BOTH, pairs)]
  transfers between devices with their start and end apart: 38 -> 40, of which waited for: 15 -> 18; matrix products, arithmetic and copies ran while one was open for 2% -> 2% of each run, Pallas kernels for 4% -> 4%
where the time goes in v2:
time: 166 us; the launch traced here: 165 us
  starting transfers between devices  73 us (44%)
  waiting for transfers between devices  58.4 us (35%)
  Pallas kernels  28 us (17%)
  other arithmetic  4.03 us (2%)
    ppermute x40, starting transfers between devices, send(): return lax.ppermute(value, BOTH, pairs)  73 us
    ppermute x40, waiting for transfers between devices, send(): return lax.ppermute(value, BOTH, pairs)  58.4 us
    pallas_call x1, Pallas kernels, local(): pl.pallas_call(functools.partial(attention_kernel, scale, lines), compile...  17.3 us
    pallas_call x1, Pallas kernels, local(): own_part, other_part = input_call(at, dqkv, *planes)  4.2 us
  transfers between devices with their start and end apart: 40, of which 18 were waited for; matrix products, arithmetic and copies ran while one was open for 2% of the time, Pallas kernels for 4%

profile of v2, /device:TPU:0, one launch (start us, length us, event | category | flops | bytes accessed | tf_op | source)
XLA Modules:
  0.0 165.4 jit_solution(14009151685768352718)
XLA Ops:
  0.6 3.0 %collective-permute-start = (bf16[128,1152]{1,0:T(8,128)(2,1)}, bf16[128,1152]{1,0:T(8,128)(2,1)S(1)}, u32[]{:S(2)}, u32[]{:S(2)}) collective-permute-start(bf16[128,1152]{1,0:T(8,128)(2,1)} %bitcast.37), channel_id=1, source_target_pairs={{0,4},{1,5},{2,6},{3,7},{4,0},{5,1},{6,2},{7,3},{8,12},{9,13},{10,... | collective-permute-start | bytes 884744 | tf_op jit(solution)/shard_map/ppermute | solution.py:53
  5.2 1.9 %collective-permute-start.4 = (bf16[128,1152]{1,0:T(8,128)(2,1)}, bf16[128,1152]{1,0:T(8,128)(2,1)S(1)}, u32[]{:S(2)}, u32[]{:S(2)}) collective-permute-start(bf16[128,1152]{1,0:T(8,128)(2,1)} %bitcast.41), channel_id=1, source_target_pairs={{0,4},{1,5},{2,6},{3,7},{4,0},{5,1},{6,2},{7,3},{8,12},{9,13},{10,... | collective-permute-start | bytes 884744 | tf_op jit(solution)/shard_map/ppermute | solution.py:53
  8.7 3.1 %collective-permute-done = bf16[128,1152]{1,0:T(8,128)(2,1)S(1)} collective-permute-done((bf16[128,1152]{1,0:T(8,128)(2,1)}, bf16[128,1152]{1,0:T(8,128)(2,1)S(1)}, u32[]{:S(2)}, u32[]{:S(2)}) %collective-permute-start) | collective-permute-done | bytes 294944 | tf_op jit(solution)/shard_map/ppermute | solution.py:53
  11.7 3.0 %collective-permute-start.6 = (bf16[128,1152]{1,0:T(8,128)(2,1)}, bf16[128,1152]{1,0:T(8,128)(2,1)S(1)}, u32[]{:S(2)}, u32[]{:S(2)}) collective-permute-start(bf16[128,1152]{1,0:T(8,128)(2,1)} %bitcast.43), channel_id=1, source_target_pairs={{0,5},{1,4},{2,7},{3,6},{4,1},{5,0},{6,3},{7,2},{8,13},{9,12},{10,... | collective-permute-start | bytes 884744 | tf_op jit(solution)/shard_map/ppermute | solution.py:53
  14.7 5.4 %collective-permute-done.1 = bf16[128,1152]{1,0:T(8,128)(2,1)S(1)} collective-permute-done((bf16[128,1152]{1,0:T(8,128)(2,1)}, bf16[128,1152]{1,0:T(8,128)(2,1)S(1)}, u32[]{:S(2)}, u32[]{:S(2)}) %collective-permute-start.1) | collective-permute-done | bytes 294944 | tf_op jit(solution)/shard_map/ppermute | solution.py:53
  21.3 3.1 %collective-permute-done.4 = bf16[128,1152]{1,0:T(8,128)(2,1)S(1)} collective-permute-done((bf16[128,1152]{1,0:T(8,128)(2,1)}, bf16[128,1152]{1,0:T(8,128)(2,1)S(1)}, u32[]{:S(2)}, u32[]{:S(2)}) %collective-permute-start.4) | collective-permute-done | bytes 294944 | tf_op jit(solution)/shard_map/ppermute | solution.py:53
  24.4 6.9 %collective-permute-done.5 = bf16[128,1152]{1,0:T(8,128)(2,1)S(1)} collective-permute-done((bf16[128,1152]{1,0:T(8,128)(2,1)}, bf16[128,1152]{1,0:T(8,128)(2,1)S(1)}, u32[]{:S(2)}, u32[]{:S(2)}) %collective-permute-start.5) | collective-permute-done | bytes 294944 | tf_op jit(solution)/shard_map/ppermute | solution.py:53
  32.4 2.3 %shard_map.77 = (bf16[72,432]{1,0:T(8,128)(2,1)S(1)}, bf16[72,432]{1,0:T(8,128)(2,1)S(1)}, bf16[72,432]{1,0:T(8,128)(2,1)S(1)}, bf16[72,432]{1,0:T(8,128)(2,1)S(1)}) custom-call(s32[4]{0:T(128)S(1)} %pad_add_fusion.at_ref, bf16[72,1152]{1,0:T(8,128)(2,1)S(1)} %copy-done, bf16[72,1152]{1,0:T(8,128)(2,1)S(1)} %copy-done.1, bf16[72,1152]{1,0:T(8,128)(2,1)S(1)} %copy-done.2), custom_call_target="tpu_custom_call" | custom-call | tf_op jit(solution)/shard_map/pallas_call | solution.py:334
  36.8 2.5 %collective-permute-done.10.refs_3_ = bf16[72,432]{1,0:T(8,128)(2,1)S(1)} collective-permute-done((bf16[72,432]{1,0:T(8,128)(2,1)S(1)}, bf16[72,432]{1,0:T(8,128)(2,1)S(1)}, u32[]{:S(2)}, u32[]{:S(2)}) %collective-permute-start.10) | collective-permute-done | bytes 62240 | tf_op jit(solution)/shard_map/ppermute | solution.py:53
  39.3 3.5 %collective-permute-start.16 = (bf16[72,1152]{1,0:T(8,128)(2,1)S(1)}, bf16[72,1152]{1,0:T(8,128)(2,1)S(1)}, u32[]{:S(2)}, u32[]{:S(2)}) collective-permute-start(bf16[72,1152]{1,0:T(8,128)(2,1)S(1)} %copy-done.6), channel_id=1, source_target_pairs={{0,8},{3,9},{4,12},{7,13},{8,16},{11,17},{12,20},{15,21},{16,26},{... | collective-permute-start | bytes 497672 | tf_op jit(solution)/shard_map/ppermute | solution.py:53
  44.1 3.1 %collective-permute-done.9.refs_2_ = bf16[72,432]{1,0:T(8,128)(2,1)S(1)} collective-permute-done((bf16[72,432]{1,0:T(8,128)(2,1)S(1)}, bf16[72,432]{1,0:T(8,128)(2,1)S(1)}, u32[]{:S(2)}, u32[]{:S(2)}) %collective-permute-start.9) | collective-permute-done | bytes 62240 | tf_op jit(solution)/shard_map/ppermute | solution.py:53
  48.0 2.4 %collective-permute-start.12 = (bf16[2,72,864]{2,1,0:T(8,128)(2,1)S(1)}, bf16[2,72,864]{2,1,0:T(8,128)(2,1)S(1)}, u32[]{:S(2)}, u32[]{:S(2)}) collective-permute-start(bf16[2,72,864]{2,1,0:T(8,128)(2,1)S(1)} %shard_map.78.refs_4_.refs_0_), channel_id=1, source_target_pairs={{0,16},{1,17},{2,18},{3,19},{4,20},{5,21},{6,22},{7,23},{8,24},{9,... | collective-permute-start | bytes 746504 | tf_op jit(solution)/shard_map/ppermute | solution.py:53
  50.3 2.5 %collective-permute-start.17 = (bf16[72,1152]{1,0:T(8,128)(2,1)S(1)}, bf16[72,1152]{1,0:T(8,128)(2,1)S(1)}, u32[]{:S(2)}, u32[]{:S(2)}) collective-permute-start(bf16[72,1152]{1,0:T(8,128)(2,1)S(1)} %copy-done.6), channel_id=1, source_target_pairs={{0,16},{3,17},{4,20},{7,21},{8,24},{11,25},{12,28},{15,29},{16,2},... | collective-permute-start | bytes 497672 | tf_op jit(solution)/shard_map/ppermute | solution.py:53
  52.9 2.9 %collective-permute-start.18 = (bf16[72,1152]{1,0:T(8,128)(2,1)S(1)}, bf16[72,1152]{1,0:T(8,128)(2,1)S(1)}, u32[]{:S(2)}, u32[]{:S(2)}) collective-permute-start(bf16[72,1152]{1,0:T(8,128)(2,1)S(1)} %copy-done.6), channel_id=1, source_target_pairs={{0,24},{3,25},{4,28},{7,29},{8,0},{11,1},{12,4},{15,5},{16,10},{19... | collective-permute-start | bytes 497672 | tf_op jit(solution)/shard_map/ppermute | solution.py:53
  56.0 12.9 %collective-permute-start.11 = (bf16[2,72,864]{2,1,0:T(8,128)(2,1)S(1)}, bf16[2,72,864]{2,1,0:T(8,128)(2,1)S(1)}, u32[]{:S(2)}, u32[]{:S(2)}) collective-permute-start(bf16[2,72,864]{2,1,0:T(8,128)(2,1)S(1)} %shard_map.78.refs_4_.refs_0_), channel_id=1, source_target_pairs={{0,8},{1,9},{2,10},{3,11},{4,12},{5,13},{6,14},{7,15},{8,16},{9,17... | collective-permute-start | bytes 746504 | tf_op jit(solution)/shard_map/ppermute | solution.py:53
  72.8 4.4 %collective-permute-done.13.refs_7_.refs_3_ = bf16[2,72,864]{2,1,0:T(8,128)(2,1)S(1)} collective-permute-done((bf16[2,72,864]{2,1,0:T(8,128)(2,1)S(1)}, bf16[2,72,864]{2,1,0:T(8,128)(2,1)S(1)}, u32[]{:S(2)}, u32[]{:S(2)}) %collective-permute-start.13) | collective-permute-done | bytes 248864 | tf_op jit(solution)/shard_map/ppermute | solution.py:53
  77.2 2.8 %collective-permute-done.14.refs_8_.refs_4_ = bf16[2,72,864]{2,1,0:T(8,128)(2,1)S(1)} collective-permute-done((bf16[2,72,864]{2,1,0:T(8,128)(2,1)S(1)}, bf16[2,72,864]{2,1,0:T(8,128)(2,1)S(1)}, u32[]{:S(2)}, u32[]{:S(2)}) %collective-permute-start.14) | collective-permute-done | bytes 248864 | tf_op jit(solution)/shard_map/ppermute | solution.py:53
  80.0 17.3 %shard_map.79 = (bf16[2,72,864]{2,1,0:T(8,128)(2,1)S(1)}, bf16[2,72,864]{2,1,0:T(8,128)(2,1)}, bf16[2,72,864]{2,1,0:T(8,128)(2,1)S(1)}, bf16[2,72,864]{2,1,0:T(8...) custom-call(s32[4]{0:T(128)S(1)} %pad_add_fusion.at_ref, ...), custom_call_target="tpu_custom_call" | custom-call | flops 2717908992 | bytes 10485760 | tf_op jit(solution)/shard_map/pallas_call | solution.py:375
  97.2 4.2 %shard_map.80 = (bf16[4,128,1152]{2,1,0:T(8,128)(2,1)S(1)}, bf16[4,128,1152]{2,1,0:T(8,128)(2,1)}) custom-call(s32[4]{0:T(128)S(1)} %pad_add_fusion.at_ref, bf16[1024,432]{1,0:T(8,128)(2,1)S(1)} %get-tuple-element.23.dqkv_ref, bf16[2,72,864]{2,1,0:T(8,128)(2,1)S(1)} %shard_map.78.refs_4_.refs_0_, ...), custom_call_target="tpu_custom_call" | custom-call | flops 1019215872 | bytes 8388608 | tf_op jit(solution)/shard_map/pallas_call | solution.py:449
  102.3 1.9 %collective-permute-start.36 = (bf16[72,1152]{1,0:T(8,128)(2,1)S(1)}, bf16[72,1152]{1,0:T(8,128)(2,1)S(1)}, u32[]{:S(2)}, u32[]{:S(2)}) collective-permute-start(bf16[72,1152]{1,0:T(8,128)(2,1)S(1)} %get-tuple-element.44), channel_id=1, source_target_pairs={{0,8},{1,11},{4,12},{5,15},{10,16},{11,19},{14,20},{15,23},{18,24}... | collective-permute-start | bytes 497672 | tf_op jit(solution)/shard_map/ppermute | solution.py:53
  106.8 4.6 %collective-permute-start.26 = (bf16[2,72,864]{2,1,0:T(8,128)(2,1)S(1)}, bf16[2,72,864]{2,1,0:T(8,128)(2,1)S(1)}, u32[]{:S(2)}, u32[]{:S(2)}) collective-permute-start(bf16[2,72,864]{2,1,0:T(8,128)(2,1)S(1)} %copy-done.4), channel_id=1, source_target_pairs={{0,8},{1,9},{2,10},{3,11},{4,12},{5,13},{6,14},{7,15},{24,16},{25,... | collective-permute-start | bytes 746504 | tf_op jit(solution)/shard_map/ppermute | solution.py:53
  112.3 1.9 %collective-permute-start.23 = (bf16[2,72,864]{2,1,0:T(8,128)(2,1)S(1)}, bf16[2,72,864]{2,1,0:T(8,128)(2,1)S(1)}, u32[]{:S(2)}, u32[]{:S(2)}) collective-permute-start(bf16[2,72,864]{2,1,0:T(8,128)(2,1)S(1)} %get-tuple-element.27), channel_id=1, source_target_pairs={{0,16},{1,17},{2,18},{3,19},{4,20},{5,21},{6,22},{7,23},{24,8},{25... | collective-permute-start | bytes 746504 | tf_op jit(solution)/shard_map/ppermute | solution.py:53
  115.7 1.5 collective-permute-start.24
  118.7 7.7 %collective-permute-start.39 = (bf16[72,1152]{1,0:T(8,128)(2,1)S(1)}, bf16[72,1152]{1,0:T(8,128)(2,1)S(1)}, u32[]{:S(2)}, u32[]{:S(2)}) collective-permute-start(bf16[72,1152]{1,0:T(8,128)(2,1)S(1)} %add_convert_fusion.1.refs_8_), channel_id=1, source_target_pairs={{0,1},{3,2},{4,5},{7,6},{8,9},{11,10},{12,13},{15,14},{16,17},{19,... | collective-permute-start | bytes 497672 | tf_op jit(solution)/shard_map/ppermute | solution.py:53
  127.8 1.6 fusion.2
  130.0 3.2 %collective-permute-start.21 = (bf16[128,1152]{1,0:T(8,128)(2,1)S(1)}, bf16[128,1152]{1,0:T(8,128)(2,1)S(1)}, u32[]{:S(2)}, u32[]{:S(2)}) collective-permute-start(bf16[128,1152]{1,0:T(8,128)(2,1)S(1)} %get-tuple-element.40), channel_id=1, source_target_pairs={{0,1},{1,0},{2,3},{3,2},{4,5},{5,4},{6,7},{7,6},{8,9},{9,8},{10,11... | collective-permute-start | bytes 884744 | tf_op jit(solution)/shard_map/ppermute | solution.py:53
  133.2 4.8 %collective-permute-done.27.refs_4_ = bf16[2,72,864]{2,1,0:T(8,128)(2,1)S(1)} collective-permute-done((bf16[2,72,864]{2,1,0:T(8,128)(2,1)S(1)}, bf16[2,72,864]{2,1,0:T(8,128)(2,1)S(1)}, u32[]{:S(2)}, u32[]{:S(2)}) %collective-permute-start.27) | collective-permute-done | bytes 248864 | tf_op jit(solution)/shard_map/ppermute | solution.py:53
  140.1 7.7 %collective-permute-done.28.refs_1_ = bf16[72,432]{1,0:T(8,128)(2,1)S(1)} collective-permute-done((bf16[72,432]{1,0:T(8,128)(2,1)S(1)}, bf16[72,432]{1,0:T(8,128)(2,1)S(1)}, u32[]{:S(2)}, u32[]{:S(2)}) %collective-permute-start.28) | collective-permute-done | bytes 62240 | tf_op jit(solution)/shard_map/ppermute | solution.py:53
  149.1 2.5 %collective-permute-done.30.refs_3_ = bf16[72,432]{1,0:T(8,128)(2,1)S(1)} collective-permute-done((bf16[72,432]{1,0:T(8,128)(2,1)S(1)}, bf16[72,432]{1,0:T(8,128)(2,1)S(1)}, u32[]{:S(2)}, u32[]{:S(2)}) %collective-permute-start.30) | collective-permute-done | bytes 62240 | tf_op jit(solution)/shard_map/ppermute | solution.py:53
  153.6 3.3 %collective-permute-done.32.refs_5_ = bf16[72,432]{1,0:T(8,128)(2,1)S(1)} collective-permute-done((bf16[72,432]{1,0:T(8,128)(2,1)S(1)}, bf16[72,432]{1,0:T(8,128)(2,1)S(1)}, u32[]{:S(2)}, u32[]{:S(2)}) %collective-permute-start.32) | collective-permute-done | bytes 62240 | tf_op jit(solution)/shard_map/ppermute | solution.py:53
  157.6 4.4 %collective-permute-done.34.refs_7_ = bf16[72,432]{1,0:T(8,128)(2,1)S(1)} collective-permute-done((bf16[72,432]{1,0:T(8,128)(2,1)S(1)}, bf16[72,432]{1,0:T(8,128)(2,1)S(1)}, u32[]{:S(2)}, u32[]{:S(2)}) %collective-permute-start.34) | collective-permute-done | bytes 62240 | tf_op jit(solution)/shard_map/ppermute | solution.py:53
  162.0 2.6 %shard_map.82 = f32[72,4608]{1,0:T(8,128)} custom-call(s32[4]{0:T(128)S(1)} %pad_add_fusion.at_ref, bf16[72,432]{1,0:T(8,128)(2,1)S(1)} %get-tuple-element.31.refs_0_, bf16[72,432]{1,0:T(8,128)(2,1)S(1)} %collective-permute-done.28.refs_1_, bf16[72,432]{1,0:T(8,128)(2,1)S(1)} %collective-permute-done.29.refs_2_, ...), custom_call_target="tpu_custom_call" | custom-call | tf_op jit(solution)/shard_map/pallas_call | solution.py:459
  (77 shorter events, 29.6 us)
Async XLA Ops:
  0.6 11.1 %collective-permute-start = (bf16[128,1152]{1,0:T(8,128)(2,1)}, bf16[128,1152]{1,0:T(8,128)(2,1)S(1)}, u32[]{:S(2)}, u32[]{:S(2)}) collective-permute-start(bf16[128,1152]{1,0:T(8,128)(2,1)} %bitcast.37), channel_id=1, source_target_pairs={{0,4},{1,5},{2,6},{3,7},{4,0},{5,1},{6,2},{7,3},{8,12},{9,13},{10,... | collective-permute-start | bytes 884744 | tf_op jit(solution)/shard_map/ppermute | solution.py:53
  3.7 16.4 %collective-permute-start.1 = (bf16[128,1152]{1,0:T(8,128)(2,1)}, bf16[128,1152]{1,0:T(8,128)(2,1)S(1)}, u32[]{:S(2)}, u32[]{:S(2)}) collective-permute-start(bf16[128,1152]{1,0:T(8,128)(2,1)} %bitcast.38), channel_id=1, source_target_pairs={{0,1},{1,0},{2,3},{3,2},{4,5},{5,4},{6,7},{7,6},{8,9},{9,8},{10,11... | collective-permute-start | bytes 884744 | tf_op jit(solution)/shard_map/ppermute | solution.py:53
  5.2 14.9 %collective-permute-start.2 = (bf16[128,1152]{1,0:T(8,128)(2,1)}, bf16[128,1152]{1,0:T(8,128)(2,1)S(1)}, u32[]{:S(2)}, u32[]{:S(2)}) collective-permute-start(bf16[128,1152]{1,0:T(8,128)(2,1)} %bitcast.39), channel_id=1, source_target_pairs={{0,5},{1,4},{2,7},{3,6},{4,1},{5,0},{6,3},{7,2},{8,13},{9,12},{10,... | collective-permute-start | bytes 884744 | tf_op jit(solution)/shard_map/ppermute | solution.py:53
  5.2 19.2 %collective-permute-start.4 = (bf16[128,1152]{1,0:T(8,128)(2,1)}, bf16[128,1152]{1,0:T(8,128)(2,1)S(1)}, u32[]{:S(2)}, u32[]{:S(2)}) collective-permute-start(bf16[128,1152]{1,0:T(8,128)(2,1)} %bitcast.41), channel_id=1, source_target_pairs={{0,4},{1,5},{2,6},{3,7},{4,0},{5,1},{6,2},{7,3},{8,12},{9,13},{10,... | collective-permute-start | bytes 884744 | tf_op jit(solution)/shard_map/ppermute | solution.py:53
  7.2 24.1 %collective-permute-start.5 = (bf16[128,1152]{1,0:T(8,128)(2,1)}, bf16[128,1152]{1,0:T(8,128)(2,1)S(1)}, u32[]{:S(2)}, u32[]{:S(2)}) collective-permute-start(bf16[128,1152]{1,0:T(8,128)(2,1)} %bitcast.42), channel_id=1, source_target_pairs={{0,1},{1,0},{2,3},{3,2},{4,5},{5,4},{6,7},{7,6},{8,9},{9,8},{10,11... | collective-permute-start | bytes 884744 | tf_op jit(solution)/shard_map/ppermute | solution.py:53
  11.7 19.6 %collective-permute-start.6 = (bf16[128,1152]{1,0:T(8,128)(2,1)}, bf16[128,1152]{1,0:T(8,128)(2,1)S(1)}, u32[]{:S(2)}, u32[]{:S(2)}) collective-permute-start(bf16[128,1152]{1,0:T(8,128)(2,1)} %bitcast.43), channel_id=1, source_target_pairs={{0,5},{1,4},{2,7},{3,6},{4,1},{5,0},{6,3},{7,2},{8,13},{9,12},{10,... | collective-permute-start | bytes 884744 | tf_op jit(solution)/shard_map/ppermute | solution.py:53
  21.3 58.7 %collective-permute-start.3 = (bf16[4,128,1152]{2,1,0:T(8,128)(2,1)S(1)}, bf16[4,128,1152]{2,1,0:T(8,128)(2,1)}, u32[]{:S(2)}, u32[]{:S(2)}) collective-permute-start(bf16[4,128,1152]{2,1,0:T(8,128)(2,1)S(1)} %pad_maximum_fusion.refs_0_), channel_id=1, source_target_pairs={{0,2},{1,3},{2,0},{3,1},{4,6},{5,7},{6,4},{7,5},{8,10},{9,11},{10,... | collective-permute-start | bytes 3538952 | tf_op jit(solution)/shard_map/ppermute | solution.py:53
  31.5 48.4 %collective-permute-start.7 = (bf16[4,128,1152]{2,1,0:T(8,128)(2,1)S(1)}, bf16[4,128,1152]{2,1,0:T(8,128)(2,1)}, u32[]{:S(2)}, u32[]{:S(2)}) collective-permute-start(bf16[4,128,1152]{2,1,0:T(8,128)(2,1)S(1)} %pad_maximum_fusion.1.refs_2_), channel_id=1, source_target_pairs={{0,2},{1,3},{2,0},{3,1},{4,6},{5,7},{6,4},{7,5},{8,10},{9,11},{10,... | collective-permute-start | bytes 3538952 | tf_op jit(solution)/shard_map/ppermute | solution.py:53
  35.4 7.4 %collective-permute-start.8 = (bf16[72,432]{1,0:T(8,128)(2,1)S(1)}, bf16[72,432]{1,0:T(8,128)(2,1)S(1)}, u32[]{:S(2)}, u32[]{:S(2)}) collective-permute-start(bf16[72,432]{1,0:T(8,128)(2,1)S(1)} %get-tuple-element.20), channel_id=1, source_target_pairs={{0,2},{1,3},{2,0},{3,1},{4,6},{5,7},{6,4},{7,5},{8,10},{9,11},{10,... | collective-permute-start | bytes 186632 | tf_op jit(solution)/shard_map/ppermute | solution.py:53
  36.1 14.2 %collective-permute-start.15 = (bf16[72,1152]{1,0:T(8,128)(2,1)S(1)}, bf16[72,1152]{1,0:T(8,128)(2,1)S(1)}, u32[]{:S(2)}, u32[]{:S(2)}) collective-permute-start(bf16[72,1152]{1,0:T(8,128)(2,1)S(1)} %copy-done.6), channel_id=1, source_target_pairs={{0,0},{3,1},{4,4},{7,5},{8,8},{11,9},{12,12},{15,13},{16,18},{19,1... | collective-permute-start | bytes 497672 | tf_op jit(solution)/shard_map/ppermute | solution.py:53
  39.3 13.6 %collective-permute-start.16 = (bf16[72,1152]{1,0:T(8,128)(2,1)S(1)}, bf16[72,1152]{1,0:T(8,128)(2,1)S(1)}, u32[]{:S(2)}, u32[]{:S(2)}) collective-permute-start(bf16[72,1152]{1,0:T(8,128)(2,1)S(1)} %copy-done.6), channel_id=1, source_target_pairs={{0,8},{3,9},{4,12},{7,13},{8,16},{11,17},{12,20},{15,21},{16,26},{... | collective-permute-start | bytes 497672 | tf_op jit(solution)/shard_map/ppermute | solution.py:53
  48.0 22.3 %collective-permute-start.12 = (bf16[2,72,864]{2,1,0:T(8,128)(2,1)S(1)}, bf16[2,72,864]{2,1,0:T(8,128)(2,1)S(1)}, u32[]{:S(2)}, u32[]{:S(2)}) collective-permute-start(bf16[2,72,864]{2,1,0:T(8,128)(2,1)S(1)} %shard_map.78.refs_4_.refs_0_), channel_id=1, source_target_pairs={{0,16},{1,17},{2,18},{3,19},{4,20},{5,21},{6,22},{7,23},{8,24},{9,... | collective-permute-start | bytes 746504 | tf_op jit(solution)/shard_map/ppermute | solution.py:53
  50.3 5.7 %collective-permute-start.17 = (bf16[72,1152]{1,0:T(8,128)(2,1)S(1)}, bf16[72,1152]{1,0:T(8,128)(2,1)S(1)}, u32[]{:S(2)}, u32[]{:S(2)}) collective-permute-start(bf16[72,1152]{1,0:T(8,128)(2,1)S(1)} %copy-done.6), channel_id=1, source_target_pairs={{0,16},{3,17},{4,20},{7,21},{8,24},{11,25},{12,28},{15,29},{16,2},... | collective-permute-start | bytes 497672 | tf_op jit(solution)/shard_map/ppermute | solution.py:53
  52.9 16.1 %collective-permute-start.18 = (bf16[72,1152]{1,0:T(8,128)(2,1)S(1)}, bf16[72,1152]{1,0:T(8,128)(2,1)S(1)}, u32[]{:S(2)}, u32[]{:S(2)}) collective-permute-start(bf16[72,1152]{1,0:T(8,128)(2,1)S(1)} %copy-done.6), channel_id=1, source_target_pairs={{0,24},{3,25},{4,28},{7,29},{8,0},{11,1},{12,4},{15,5},{16,10},{19... | collective-permute-start | bytes 497672 | tf_op jit(solution)/shard_map/ppermute | solution.py:53
  56.0 16.8 %collective-permute-start.11 = (bf16[2,72,864]{2,1,0:T(8,128)(2,1)S(1)}, bf16[2,72,864]{2,1,0:T(8,128)(2,1)S(1)}, u32[]{:S(2)}, u32[]{:S(2)}) collective-permute-start(bf16[2,72,864]{2,1,0:T(8,128)(2,1)S(1)} %shard_map.78.refs_4_.refs_0_), channel_id=1, source_target_pairs={{0,8},{1,9},{2,10},{3,11},{4,12},{5,13},{6,14},{7,15},{8,16},{9,17... | collective-permute-start | bytes 746504 | tf_op jit(solution)/shard_map/ppermute | solution.py:53
  69.0 8.2 %collective-permute-start.13 = (bf16[2,72,864]{2,1,0:T(8,128)(2,1)S(1)}, bf16[2,72,864]{2,1,0:T(8,128)(2,1)S(1)}, u32[]{:S(2)}, u32[]{:S(2)}) collective-permute-start(bf16[2,72,864]{2,1,0:T(8,128)(2,1)S(1)} %shard_map.78.refs_4_.refs_0_), channel_id=1, source_target_pairs={{8,0},{9,1},{10,2},{11,3},{12,4},{13,5},{14,6},{15,7},{16,8},{17,9... | collective-permute-start | bytes 746504 | tf_op jit(solution)/shard_map/ppermute | solution.py:53
  70.3 9.7 %collective-permute-start.14 = (bf16[2,72,864]{2,1,0:T(8,128)(2,1)S(1)}, bf16[2,72,864]{2,1,0:T(8,128)(2,1)S(1)}, u32[]{:S(2)}, u32[]{:S(2)}) collective-permute-start(bf16[2,72,864]{2,1,0:T(8,128)(2,1)S(1)} %collective-permute-done.12.refs_6_.refs_2_), channel_id=1, source_target_pairs={{8,0},{9,1},{10,2},{11,3},{12,4},{13,5},{14,6},{15,7},{16,24},{17,... | collective-permute-start | bytes 746504 | tf_op jit(solution)/shard_map/ppermute | solution.py:53
  101.4 25.0 %collective-permute-start.19 = (bf16[4,128,1152]{2,1,0:T(8,128)(2,1)}, bf16[4,128,1152]{2,1,0:T(8,128)(2,1)}, u32[]{:S(2)}, u32[]{:S(2)}) collective-permute-start(bf16[4,128,1152]{2,1,0:T(8,128)(2,1)} %get-tuple-element.25), channel_id=1, source_target_pairs={{0,2},{1,3},{2,0},{3,1},{4,6},{5,7},{6,4},{7,5},{8,10},{9,11},{10,... | collective-permute-start | bytes 3538952 | tf_op jit(solution)/shard_map/ppermute | solution.py:53
  102.3 10.1 %collective-permute-start.36 = (bf16[72,1152]{1,0:T(8,128)(2,1)S(1)}, bf16[72,1152]{1,0:T(8,128)(2,1)S(1)}, u32[]{:S(2)}, u32[]{:S(2)}) collective-permute-start(bf16[72,1152]{1,0:T(8,128)(2,1)S(1)} %get-tuple-element.44), channel_id=1, source_target_pairs={{0,8},{1,11},{4,12},{5,15},{10,16},{11,19},{14,20},{15,23},{18,24}... | collective-permute-start | bytes 497672 | tf_op jit(solution)/shard_map/ppermute | solution.py:53
  104.2 11.5 %collective-permute-start.37 = (bf16[72,1152]{1,0:T(8,128)(2,1)S(1)}, bf16[72,1152]{1,0:T(8,128)(2,1)S(1)}, u32[]{:S(2)}, u32[]{:S(2)}) collective-permute-start(bf16[72,1152]{1,0:T(8,128)(2,1)S(1)} %get-tuple-element.43), channel_id=1, source_target_pairs={{2,16},{3,19},{6,20},{7,23},{10,24},{11,27},{14,28},{15,31},{16,0}... | collective-permute-start | bytes 497672 | tf_op jit(solution)/shard_map/ppermute | solution.py:53
  105.5 11.7 %collective-permute-start.38 = (bf16[72,1152]{1,0:T(8,128)(2,1)S(1)}, bf16[72,1152]{1,0:T(8,128)(2,1)S(1)}, u32[]{:S(2)}, u32[]{:S(2)}) collective-permute-start(bf16[72,1152]{1,0:T(8,128)(2,1)S(1)} %get-tuple-element.42), channel_id=1, source_target_pairs={{2,24},{3,27},{6,28},{7,31},{8,0},{9,3},{12,4},{13,7},{16,8},{17,1... | collective-permute-start | bytes 497672 | tf_op jit(solution)/shard_map/ppermute | solution.py:53
  106.8 11.8 %collective-permute-start.26 = (bf16[2,72,864]{2,1,0:T(8,128)(2,1)S(1)}, bf16[2,72,864]{2,1,0:T(8,128)(2,1)S(1)}, u32[]{:S(2)}, u32[]{:S(2)}) collective-permute-start(bf16[2,72,864]{2,1,0:T(8,128)(2,1)S(1)} %copy-done.4), channel_id=1, source_target_pairs={{0,8},{1,9},{2,10},{3,11},{4,12},{5,13},{6,14},{7,15},{24,16},{25,... | collective-permute-start | bytes 746504 | tf_op jit(solution)/shard_map/ppermute | solution.py:53
  112.3 17.1 %collective-permute-start.23 = (bf16[2,72,864]{2,1,0:T(8,128)(2,1)S(1)}, bf16[2,72,864]{2,1,0:T(8,128)(2,1)S(1)}, u32[]{:S(2)}, u32[]{:S(2)}) collective-permute-start(bf16[2,72,864]{2,1,0:T(8,128)(2,1)S(1)} %get-tuple-element.27), channel_id=1, source_target_pairs={{0,16},{1,17},{2,18},{3,19},{4,20},{5,21},{6,22},{7,23},{24,8},{25... | collective-permute-start | bytes 746504 | tf_op jit(solution)/shard_map/ppermute | solution.py:53
  115.7 14.3 %collective-permute-start.24 = (bf16[2,72,864]{2,1,0:T(8,128)(2,1)}, bf16[2,72,864]{2,1,0:T(8,128)(2,1)S(1)}, u32[]{:S(2)}, u32[]{:S(2)}) collective-permute-start(bf16[2,72,864]{2,1,0:T(8,128)(2,1)} %get-tuple-element.28), channel_id=1, source_target_pairs={{0,8},{1,9},{2,10},{3,11},{4,12},{5,13},{6,14},{7,15},{8,16},{9,17... | collective-permute-start | bytes 746504 | tf_op jit(solution)/shard_map/ppermute | solution.py:53
  117.3 15.9 %collective-permute-start.25 = (bf16[2,72,864]{2,1,0:T(8,128)(2,1)S(1)}, bf16[2,72,864]{2,1,0:T(8,128)(2,1)S(1)}, u32[]{:S(2)}, u32[]{:S(2)}) collective-permute-start(bf16[2,72,864]{2,1,0:T(8,128)(2,1)S(1)} %get-tuple-element.29), channel_id=1, source_target_pairs={{8,0},{9,1},{10,2},{11,3},{12,4},{13,5},{14,6},{15,7},{16,8},{17,9... | collective-permute-start | bytes 746504 | tf_op jit(solution)/shard_map/ppermute | solution.py:53
  118.7 21.5 %collective-permute-start.39 = (bf16[72,1152]{1,0:T(8,128)(2,1)S(1)}, bf16[72,1152]{1,0:T(8,128)(2,1)S(1)}, u32[]{:S(2)}, u32[]{:S(2)}) collective-permute-start(bf16[72,1152]{1,0:T(8,128)(2,1)S(1)} %add_convert_fusion.1.refs_8_), channel_id=1, source_target_pairs={{0,1},{3,2},{4,5},{7,6},{8,9},{11,10},{12,13},{15,14},{16,17},{19,... | collective-permute-start | bytes 497672 | tf_op jit(solution)/shard_map/ppermute | solution.py:53
  126.5 11.5 %collective-permute-start.27 = (bf16[2,72,864]{2,1,0:T(8,128)(2,1)S(1)}, bf16[2,72,864]{2,1,0:T(8,128)(2,1)S(1)}, u32[]{:S(2)}, u32[]{:S(2)}) collective-permute-start(bf16[2,72,864]{2,1,0:T(8,128)(2,1)S(1)} %add_convert_fusion), channel_id=1, source_target_pairs={{8,24},{9,25},{10,26},{11,27},{12,28},{13,29},{14,30},{15,31},{16,... | collective-permute-start | bytes 746504 | tf_op jit(solution)/shard_map/ppermute | solution.py:53
  129.4 35.2 %collective-permute-start.20 = (bf16[128,1152]{1,0:T(8,128)(2,1)S(1)}, bf16[128,1152]{1,0:T(8,128)(2,1)S(1)}, u32[]{:S(2)}, u32[]{:S(2)}) collective-permute-start(bf16[128,1152]{1,0:T(8,128)(2,1)S(1)} %get-tuple-element.38), channel_id=1, source_target_pairs={{0,4},{1,5},{2,6},{3,7},{4,0},{5,1},{6,2},{7,3},{8,12},{9,13},{10,... | collective-permute-start | bytes 884744 | tf_op jit(solution)/shard_map/ppermute | solution.py:53
  130.0 34.6 %collective-permute-start.21 = (bf16[128,1152]{1,0:T(8,128)(2,1)S(1)}, bf16[128,1152]{1,0:T(8,128)(2,1)S(1)}, u32[]{:S(2)}, u32[]{:S(2)}) collective-permute-start(bf16[128,1152]{1,0:T(8,128)(2,1)S(1)} %get-tuple-element.40), channel_id=1, source_target_pairs={{0,1},{1,0},{2,3},{3,2},{4,5},{5,4},{6,7},{7,6},{8,9},{9,8},{10,11... | collective-permute-start | bytes 884744 | tf_op jit(solution)/shard_map/ppermute | solution.py:53
  133.2 31.4 %collective-permute-start.22 = (bf16[128,1152]{1,0:T(8,128)(2,1)S(1)}, bf16[128,1152]{1,0:T(8,128)(2,1)S(1)}, u32[]{:S(2)}, u32[]{:S(2)}) collective-permute-start(bf16[128,1152]{1,0:T(8,128)(2,1)S(1)} %get-tuple-element.39), channel_id=1, source_target_pairs={{0,5},{1,4},{2,7},{3,6},{4,1},{5,0},{6,3},{7,2},{8,13},{9,12},{10,... | collective-permute-start | bytes 884744 | tf_op jit(solution)/shard_map/ppermute | solution.py:53
  138.9 8.9 %collective-permute-start.28 = (bf16[72,432]{1,0:T(8,128)(2,1)S(1)}, bf16[72,432]{1,0:T(8,128)(2,1)S(1)}, u32[]{:S(2)}, u32[]{:S(2)}) collective-permute-start(bf16[72,432]{1,0:T(8,128)(2,1)S(1)} %get-tuple-element.31.refs_0_), channel_id=1, source_target_pairs={{0,1},{1,0},{2,3},{3,2},{4,5},{5,4},{6,7},{7,6},{8,9},{9,8},{10,11... | collective-permute-start | bytes 186632 | tf_op jit(solution)/shard_map/ppermute | solution.py:53
  140.1 7.7 %collective-permute-start.29 = (bf16[72,432]{1,0:T(8,128)(2,1)S(1)}, bf16[72,432]{1,0:T(8,128)(2,1)S(1)}, u32[]{:S(2)}, u32[]{:S(2)}) collective-permute-start(bf16[72,432]{1,0:T(8,128)(2,1)S(1)} %get-tuple-element.32), channel_id=1, source_target_pairs={{0,2},{1,3},{2,0},{3,1},{4,6},{5,7},{6,4},{7,5},{8,10},{9,11},{10,... | collective-permute-start | bytes 186632 | tf_op jit(solution)/shard_map/ppermute | solution.py:53
  (15 other events, 66.8 us)

commit v3 on v2

--- a/solution.py
+++ b/solution.py
@@ -143,11 +143,11 @@
                 out_ref[index // 2, :, side * wide : (side + 1) * wide] = piece[...]
 
 
-def sum_kernel(at_ref, *refs):
-    parts, outs = refs[: len(refs) - 4], refs[len(refs) - 4 :]
+def sum_kernel(terms, at_ref, *refs):
+    parts, heads, outs = refs[:terms], refs[terms : len(refs) - 6], refs[len(refs) - 6 :]
     here = 2 * at_ref[1] + at_ref[2]
     wide = outs[0].shape[1]
-    for n, out in enumerate(outs):
+    for n, out in enumerate(outs[:4]):
         index = here ^ n
         for side in range(2):
 
@@ -156,6 +156,12 @@
                 cut = slice(side * wide, (side + 1) * wide)
                 total = sum(p[index // 2, :, cut].astype(jnp.float32) for p in parts)
                 out[...] = total.astype(jnp.bfloat16)
+
+    kept, other = outs[4:]
+    kept[...] = sum(h[...].astype(jnp.float32) for h in heads).astype(kept.dtype)
+    width = kept.shape[1]
+    other[:, :width] = kept[...]
+    other[:, width:] = outs[0][...]
 
 
 def attend(query, keyed, valued, dattn, scale, bias):
@@ -197,9 +203,11 @@
     xs, xc, ds, dc = refs[:4]
     moved = 4 + lines + (lines > 2)
     sent = lines + (lines == 4)
-    planes, out_ws = refs[4:moved], refs[moved : len(refs) - sent - 8]
-    grads_in = refs[len(refs) - sent - 8 : len(refs) - 8]
-    grad_out, dqkv_ref, full, loose, out_w, att, grads, bias = refs[len(refs) - 8 :]
+    owed = lines if len(refs) > moved + 1 + sent + 9 else 1
+    planes, out_ws = refs[4:moved], refs[moved : moved + owed]
+    grads_in = refs[moved + owed : moved + owed + sent]
+    grads_out = refs[moved + owed + sent : moved + 2 * owed + sent]
+    dqkv_ref, full, loose, out_w, att, grads, bias = refs[moved + 2 * owed + sent :]
     shard, wide = loose.shape[1:]
     dim = wide // (3 * KEPT)
     width = xs.shape[-1]
@@ -245,19 +253,24 @@
             )
             return 0
 
-        lax.fori_loop(0, half // BLOCK, block, 0)
+        lax.fori_loop(0, half // BLOCK, block, 0, unroll=True)
 
     def columns(m, _):
         at = pl.multiple_of(m * 128, 128)
         first = matmul(att[:half, :], ds[:, :, pl.ds(at, 128)].reshape(half, 128), ((0,), (0,)))
         second = matmul(att[half:, :], dc[:, :, pl.ds(at, 128)].reshape(half, 128), ((0,), (0,)))
-        grad_out[:, pl.ds(at, 128)] = (first + second).astype(jnp.bfloat16)
+        term = (first + second).astype(jnp.bfloat16)
+        if owed == 1:
+            grads_out[0][:, pl.ds(at, 128)] = term
+        for s in range(owed if owed > 1 else 0):
+            upper = lax.rem(at_ref[0] + s, lines) != KEPT * at_ref[2]
+            grads_out[s][:, pl.ds(at, 128)] = jnp.where(upper, term[dim:], term[:dim])
         first = matmul(xs[:, :, pl.ds(at, 128)].reshape(half, 128), dqkv_ref[:half, :], ((0,), (0,)))
         second = matmul(xc[:, :, pl.ds(at, 128)].reshape(half, 128), dqkv_ref[half:, :], ((0,), (0,)))
         grads[pl.ds(at, 128), :] = first + second
         return 0
 
-    lax.fori_loop(0, width // 128, columns, 0)
+    lax.fori_loop(0, width // 128, columns, 0, unroll=True)
     for p in range(4 * lines):
         loose[p] = grads[p * shard : (p + 1) * shard, :].astype(jnp.bfloat16)
     for s, out in enumerate(grads_in):
@@ -268,9 +281,7 @@
             out[n // 2, :, (n % 2) * wide : (n % 2 + 1) * wide] = loose[4 * line + n]
 
 
-def input_kernel(lines, at_ref, dqkv_ref, *refs):
-    *planes, own_ref, other_ref, full, loose = refs
-    full_weights(lines, at_ref, planes, loose, full)
+def input_kernel(dqkv_ref, full, own_ref, other_ref):
     chunks, count, width = own_ref.shape
     each = BLOCK // count
     for part, out in enumerate((own_ref, other_ref)):
@@ -281,11 +292,11 @@
             out[pl.ds(each * j, each)] = value.astype(jnp.bfloat16).reshape(each, count, width)
             return 0
 
-        lax.fori_loop(0, chunks // each, block, 0)
+        lax.fori_loop(0, chunks // each, block, 0, unroll=True)
 
 
 def spread_kernel(dim, at_ref, *refs):
-    *pieces, kept_ref, moved_ref, out_ref, table = refs
+    *pieces, kept_ref, out_ref, table = refs
     step = pl.program_id(0)
 
     @pl.when(step == 0)
@@ -295,8 +306,9 @@
             b = lax.rem(at_ref[1] + db, 2)
             c = lax.rem(at_ref[2] + dc, 2)
             y = lax.rem(at_ref[3] + dy, 2)
-            table[4 * b + 2 * c + y] = piece[...]
-        out_ref[...] = kept_ref[...].astype(jnp.float32) + moved_ref[...].astype(jnp.float32)
+            table[4 * b + 2 * c + y] = piece[:, piece.shape[1] - table.shape[2] :]
+        moved = pieces[1][:, : out_ref.shape[1]].astype(jnp.float32)
+        out_ref[...] = kept_ref[...].astype(jnp.float32) + moved
 
     for w in range(3):
 
@@ -339,7 +351,7 @@
         out_specs=(VMEM,) * 4,
         scratch_shapes=[pltpu.VMEM((shard, width), jnp.bfloat16)] * 3
         + [pltpu.SemaphoreType.DMA((3,))],
-    )(at, query_weight, key_weight, value_weight)
+    )(at, *[pltpu.with_memory_space_constraint(v, pltpu.HBM) for v in (query_weight, key_weight, value_weight)])
     pieces = [pieces[0]] + [grid.flip(pieces[n], n // 2, n % 2, 0) for n in range(1, 4)]
     plane = pl.pallas_call(
         plane_kernel,
@@ -372,15 +384,17 @@
     ds, dc = gather_rows(drows)
 
     sent = lines + (lines == 4)
-    *grads_in, grad_out, dqkv = pl.pallas_call(
+    owed = len(out_ws)
+    head_rows = dim if one_head else wide
+    *results, dqkv, full = pl.pallas_call(
         functools.partial(attention_kernel, scale, lines),
         compiler_params=room(28),
         out_shape=(shape_of(2, shard, 6 * wide),) * sent
-        + (shape_of(wide, width), shape_of(total, 3 * wide)),
+        + (shape_of(head_rows, width),) * owed
+        + (shape_of(total, 3 * wide), shape_of(width, 3 * wide)),
         in_specs=[SMEM] + [VMEM] * (4 + len(planes) + len(out_ws)),
-        out_specs=(VMEM,) * (sent + 2),
+        out_specs=(VMEM,) * (sent + owed + 2),
         scratch_shapes=[
-            pltpu.VMEM((width, 3 * wide), jnp.bfloat16),
             pltpu.VMEM((pix, shard, 3 * wide), jnp.bfloat16),
             pltpu.VMEM((wide, width), jnp.bfloat16),
             pltpu.VMEM((total, wide), jnp.bfloat16),
@@ -392,68 +406,57 @@
         ),
     )(at, xs, xc, ds, dc, *planes, *out_ws)
 
+    grads_in, grads_out = results[:sent], results[sent:]
     parts = grid.scatter_lines(grads_in)
-    summed = pl.pallas_call(
-        sum_kernel,
-        compiler_params=room(8),
-        out_shape=(shape_of(shard, 3 * wide),) * 4,
-        in_specs=[SMEM] + [VMEM] * len(parts),
-        out_specs=(VMEM,) * 4,
-    )(at, *parts)
-    square = []
-    for n in range(8):
-        block = summed[n // 2]
-        square.append(grid.flip(block, n // 4, (n // 2) % 2, n % 2) if n else block)
-
     if one_head:
-        blocks = grad_out.reshape(KEPT, dim, width)
-        partial = [
+        heads = [
             grid.send(
-                lax.dynamic_index_in_dim(
-                    blocks, jnp.clip((a + s) % lines - span * c, 0, KEPT - 1), 0, keepdims=False
-                ),
+                grads_out[s],
                 lambda a, b, c, g, y: (
                     ((a + s) % lines, b, y, g, y) if ((a + s) % lines) // span == c else None
                 ),
             )
             for s in range(lines)
         ]
-        kept = sum(p.astype(jnp.float32) for p in partial).astype(jnp.bfloat16)
-        moved = grid.send(kept, lambda a, b, c, g, y: (a, b, c, g, y ^ 1) if c == y else None)
     else:
         whole = jnp.zeros((2, KEPT, 2, 2, dim, width), jnp.float32)
         whole = lax.dynamic_update_slice(
             whole,
-            grad_out.astype(jnp.float32).reshape(1, KEPT, 1, 1, dim, width),
+            grads_out[0].astype(jnp.float32).reshape(1, KEPT, 1, 1, dim, width),
             (c, 0, b, y, 0, 0),
         ).reshape(width, width)
-        pairs = [[2 * g, 2 * g + 1] for g in range(grid.groups)]
-        whole = lax.psum(whole, "rep", axis_index_groups=pairs)
-        kept = lax.psum_scatter(whole, "pix", scatter_dimension=0, tiled=True)
-        moved = jnp.zeros_like(kept)
+        heads = [lax.psum_scatter(whole, "pix", scatter_dimension=0, tiled=True)]
+    *summed, kept, other = pl.pallas_call(
+        functools.partial(sum_kernel, len(parts)),
+        compiler_params=room(10),
+        out_shape=(shape_of(shard, 3 * wide),) * 4
+        + (shape_of(shard, width), shape_of(shard, width + 3 * wide)),
+        in_specs=[SMEM] + [VMEM] * (len(parts) + len(heads)),
+        out_specs=(VMEM,) * 6,
+    )(at, *parts, *heads)
+    square = []
+    for n in range(8):
+        block = other if n == 1 else summed[n // 2]
+        square.append(grid.flip(block, n // 4, (n // 2) % 2, n % 2) if n else block)
 
     input_call = pl.pallas_call(
-        functools.partial(input_kernel, lines),
+        input_kernel,
         compiler_params=room(20),
         out_shape=(shape_of(4, count, width),) * 2,
-        in_specs=[SMEM] + [VMEM] * (1 + len(planes)),
+        in_specs=[VMEM] * 2,
         out_specs=(VMEM,) * 2,
-        scratch_shapes=[
-            pltpu.VMEM((width, 3 * wide), jnp.bfloat16),
-            pltpu.VMEM((pix, shard, 3 * wide), jnp.bfloat16),
-        ],
         cost_estimate=pl.CostEstimate(
             flops=6 * total * width * wide, bytes_accessed=8 << 20, transcendentals=0
         ),
     )
-    own_part, other_part = input_call(at, dqkv, *planes)
-    pair = own_part.astype(jnp.float32) + grid.flip(other_part, 0, 1, 0).astype(jnp.float32)
-    sent = pair.astype(jnp.bfloat16)
+    own_part, other_part = input_call(dqkv, full)
+    swapped = grid.flip(other_part, 0, 1, 0)
+    pair = lambda i: own_part[i].astype(jnp.float32) + swapped[i].astype(jnp.float32)
     moves = [
-        grid.flip(sent[i + 1], db, 0, dy)
+        grid.flip(pair(i + 1).astype(jnp.bfloat16), db, 0, dy)
         for i, (db, dy) in enumerate(((1, 0), (0, 1), (1, 1)))
     ]
-    dinput = pair[0] + sum(move.astype(jnp.float32) for move in moves)
+    dinput = pair(0) + sum(move.astype(jnp.float32) for move in moves)
     dinput = dinput.astype(jnp.bfloat16)
 
     grads = pl.pallas_call(
@@ -461,10 +464,10 @@
         compiler_params=room(12),
         out_shape=shape_of(shard, 4 * width, dtype=jnp.float32),
         grid=(4,),
-        in_specs=[SMEM] + [VMEM] * 10,
+        in_specs=[SMEM] + [VMEM] * 9,
         out_specs=pl.BlockSpec((shard, width), lambda i: (0, (i + 3) % 4)),
         scratch_shapes=[pltpu.VMEM((8, shard, 3 * wide), jnp.bfloat16)],
-    )(at, *square, kept, moved)
+    )(at, *square, kept)
     if grid.groups > 1:
         same = [[2 * g + y for g in range(grid.groups)] for y in range(2)]
         grads = lax.psum(grads, "rep", axis_index_groups=same)

time: 166 us -> 166 us (level)
  waiting for transfers between devices: 58.4 us -> 70.9 us
  Pallas kernels: 28 us -> 22.3 us
  starting transfers between devices: 73 us -> 68.4 us
    ppermute x40 -> x39, waiting for transfers between devices: 58.4 us -> 70.9 us  [send(): return lax.ppermute(value, BOTH, pairs)]
    ppermute x40 -> x39, starting transfers between devices: 73 us -> 68.4 us  [send(): return lax.ppermute(value, BOTH, pairs)]
    pallas_call x1, Pallas kernels: 17.3 us -> 13.7 us  [local(): pl.pallas_call(functools.partial(attention_kernel, scale, lines), compile...]
    pallas_call x2, Pallas kernels: 5.15 us -> 2.65 us  [the longest x1 1.55 us: local(): own_part, other_part = input_call(dqkv, full)]
  transfers between devices with their start and end apart: 40 -> 39, of which waited for: 18 -> 17; matrix products, arithmetic and copies ran while one was open for 2% -> 1% of each run, Pallas kernels for 4% -> 4%
where the time goes in v3:
time: 166 us; the launch traced here: 165 us
  waiting for transfers between devices  70.9 us (43%)
  starting transfers between devices  68.4 us (41%)
  Pallas kernels  22.3 us (13%)
  other arithmetic  2.61 us (2%)
    ppermute x39, waiting for transfers between devices, send(): return lax.ppermute(value, BOTH, pairs)  70.9 us
    ppermute x39, starting transfers between devices, send(): return lax.ppermute(value, BOTH, pairs)  68.4 us
    pallas_call x1, Pallas kernels, local(): pl.pallas_call(functools.partial(attention_kernel, scale, lines), compile...  13.7 us
  transfers between devices with their start and end apart: 39, of which 17 were waited for; matrix products, arithmetic and copies ran while one was open for 1% of the time, Pallas kernels for 4%

profile of v3, /device:TPU:0, one launch (start us, length us, event | category | flops | bytes accessed | tf_op | source)
XLA Modules:
  0.0 165.1 jit_solution(5066895188115965194)
XLA Ops:
  0.6 4.0 %collective-permute-start.6 = (bf16[128,1152]{1,0:T(8,128)(2,1)}, bf16[128,1152]{1,0:T(8,128)(2,1)S(1)}, u32[]{:S(2)}, u32[]{:S(2)}) collective-permute-start(bf16[128,1152]{1,0:T(8,128)(2,1)} %bitcast.25), channel_id=1, source_target_pairs={{0,5},{1,4},{2,7},{3,6},{4,1},{5,0},{6,3},{7,2},{8,13},{9,12},{10,... | collective-permute-start | bytes 884744 | tf_op jit(solution)/shard_map/ppermute | solution.py:53
  5.3 2.8 %collective-permute-start.2 = (bf16[128,1152]{1,0:T(8,128)(2,1)}, bf16[128,1152]{1,0:T(8,128)(2,1)S(1)}, u32[]{:S(2)}, u32[]{:S(2)}) collective-permute-start(bf16[128,1152]{1,0:T(8,128)(2,1)} %bitcast.29), channel_id=1, source_target_pairs={{0,5},{1,4},{2,7},{3,6},{4,1},{5,0},{6,3},{7,2},{8,13},{9,12},{10,... | collective-permute-start | bytes 884744 | tf_op jit(solution)/shard_map/ppermute | solution.py:53
  8.6 4.1 %collective-permute-done.6 = bf16[128,1152]{1,0:T(8,128)(2,1)S(1)} collective-permute-done((bf16[128,1152]{1,0:T(8,128)(2,1)}, bf16[128,1152]{1,0:T(8,128)(2,1)S(1)}, u32[]{:S(2)}, u32[]{:S(2)}) %collective-permute-start.6) | collective-permute-done | bytes 294944 | tf_op jit(solution)/shard_map/ppermute | solution.py:53
  12.7 2.0 %collective-permute-start = (bf16[128,1152]{1,0:T(8,128)(2,1)}, bf16[128,1152]{1,0:T(8,128)(2,1)S(1)}, u32[]{:S(2)}, u32[]{:S(2)}) collective-permute-start(bf16[128,1152]{1,0:T(8,128)(2,1)} %bitcast.31), channel_id=1, source_target_pairs={{0,4},{1,5},{2,6},{3,7},{4,0},{5,1},{6,2},{7,3},{8,12},{9,13},{10,... | collective-permute-start | bytes 884744 | tf_op jit(solution)/shard_map/ppermute | solution.py:53
  14.7 4.4 %collective-permute-done.5 = bf16[128,1152]{1,0:T(8,128)(2,1)S(1)} collective-permute-done((bf16[128,1152]{1,0:T(8,128)(2,1)}, bf16[128,1152]{1,0:T(8,128)(2,1)S(1)}, u32[]{:S(2)}, u32[]{:S(2)}) %collective-permute-start.5) | collective-permute-done | bytes 294944 | tf_op jit(solution)/shard_map/ppermute | solution.py:53
  20.8 4.6 %collective-permute-done.2 = bf16[128,1152]{1,0:T(8,128)(2,1)S(1)} collective-permute-done((bf16[128,1152]{1,0:T(8,128)(2,1)}, bf16[128,1152]{1,0:T(8,128)(2,1)S(1)}, u32[]{:S(2)}, u32[]{:S(2)}) %collective-permute-start.2) | collective-permute-done | bytes 294944 | tf_op jit(solution)/shard_map/ppermute | solution.py:53
  25.4 5.4 %collective-permute-done.1 = bf16[128,1152]{1,0:T(8,128)(2,1)S(1)} collective-permute-done((bf16[128,1152]{1,0:T(8,128)(2,1)}, bf16[128,1152]{1,0:T(8,128)(2,1)S(1)}, u32[]{:S(2)}, u32[]{:S(2)}) %collective-permute-start.1) | collective-permute-done | bytes 294944 | tf_op jit(solution)/shard_map/ppermute | solution.py:53
  31.5 2.7 %shard_map.77 = (bf16[72,432]{1,0:T(8,128)(2,1)S(1)}, bf16[72,432]{1,0:T(8,128)(2,1)S(1)}, bf16[72,432]{1,0:T(8,128)(2,1)S(1)}, bf16[72,432]{1,0:T(8,128)(2,1)S(1)}) custom-call(s32[4]{0:T(128)S(1)} %pad_add_fusion.at_ref, bf16[72,1152]{1,0:T(8,128)(2,1)} %refs_0_.1, bf16[72,1152]{1,0:T(8,128)(2,1)} %refs_1_.1, bf16[72,1152]{1,0:T(8,128)(2,1)} %refs_2_.1), custom_call_target="tpu_custom_call" | custom-call | tf_op jit(solution)/shard_map/pallas_call | solution.py:346
  36.2 3.5 %collective-permute-start.16 = (bf16[72,1152]{1,0:T(8,128)(2,1)}, bf16[72,1152]{1,0:T(8,128)(2,1)S(1)}, u32[]{:S(2)}, u32[]{:S(2)}) collective-permute-start(bf16[72,1152]{1,0:T(8,128)(2,1)} %param.11), channel_id=1, source_target_pairs={{0,8},{3,9},{4,12},{7,13},{8,16},{11,17},{12,20},{15,21},{16,26},{... | collective-permute-start | bytes 497672 | tf_op jit(solution)/shard_map/ppermute | solution.py:53
  39.7 1.6 collective-permute-start.15
  41.3 3.8 %collective-permute-done.10.refs_3_ = bf16[72,432]{1,0:T(8,128)(2,1)S(1)} collective-permute-done((bf16[72,432]{1,0:T(8,128)(2,1)S(1)}, bf16[72,432]{1,0:T(8,128)(2,1)S(1)}, u32[]{:S(2)}, u32[]{:S(2)}) %collective-permute-start.10) | collective-permute-done | bytes 62240 | tf_op jit(solution)/shard_map/ppermute | solution.py:53
  45.9 1.9 %collective-permute-start.12 = (bf16[2,72,864]{2,1,0:T(8,128)(2,1)S(1)}, bf16[2,72,864]{2,1,0:T(8,128)(2,1)S(1)}, u32[]{:S(2)}, u32[]{:S(2)}) collective-permute-start(bf16[2,72,864]{2,1,0:T(8,128)(2,1)S(1)} %shard_map.78.refs_4_), channel_id=1, source_target_pairs={{0,16},{1,17},{2,18},{3,19},{4,20},{5,21},{6,22},{7,23},{8,24},{9,... | collective-permute-start | bytes 746504 | tf_op jit(solution)/shard_map/ppermute | solution.py:53
  47.7 4.0 %collective-permute-start.18 = (bf16[72,1152]{1,0:T(8,128)(2,1)}, bf16[72,1152]{1,0:T(8,128)(2,1)S(1)}, u32[]{:S(2)}, u32[]{:S(2)}) collective-permute-start(bf16[72,1152]{1,0:T(8,128)(2,1)} %param.11), channel_id=1, source_target_pairs={{0,24},{3,25},{4,28},{7,29},{8,0},{11,1},{12,4},{15,5},{16,10},{19... | collective-permute-start | bytes 497672 | tf_op jit(solution)/shard_map/ppermute | solution.py:53
  53.3 3.7 %collective-permute-done.18.refs_12_ = bf16[72,1152]{1,0:T(8,128)(2,1)S(1)} collective-permute-done((bf16[72,1152]{1,0:T(8,128)(2,1)}, bf16[72,1152]{1,0:T(8,128)(2,1)S(1)}, u32[]{:S(2)}, u32[]{:S(2)}) %collective-permute-start.18) | collective-permute-done | bytes 165920 | tf_op jit(solution)/shard_map/ppermute | solution.py:53
  58.2 8.7 %collective-permute-start.11 = (bf16[2,72,864]{2,1,0:T(8,128)(2,1)S(1)}, bf16[2,72,864]{2,1,0:T(8,128)(2,1)S(1)}, u32[]{:S(2)}, u32[]{:S(2)}) collective-permute-start(bf16[2,72,864]{2,1,0:T(8,128)(2,1)S(1)} %shard_map.78.refs_4_), channel_id=1, source_target_pairs={{0,8},{1,9},{2,10},{3,11},{4,12},{5,13},{6,14},{7,15},{8,16},{9,17... | collective-permute-start | bytes 746504 | tf_op jit(solution)/shard_map/ppermute | solution.py:53
  68.2 4.6 %collective-permute-done.11.refs_5_ = bf16[2,72,864]{2,1,0:T(8,128)(2,1)S(1)} collective-permute-done((bf16[2,72,864]{2,1,0:T(8,128)(2,1)S(1)}, bf16[2,72,864]{2,1,0:T(8,128)(2,1)S(1)}, u32[]{:S(2)}, u32[]{:S(2)}) %collective-permute-start.11) | collective-permute-done | bytes 248864 | tf_op jit(solution)/shard_map/ppermute | solution.py:53
  72.9 4.1 %collective-permute-done.14.refs_8_ = bf16[2,72,864]{2,1,0:T(8,128)(2,1)S(1)} collective-permute-done((bf16[2,72,864]{2,1,0:T(8,128)(2,1)S(1)}, bf16[2,72,864]{2,1,0:T(8,128)(2,1)S(1)}, u32[]{:S(2)}, u32[]{:S(2)}) %collective-permute-start.14) | collective-permute-done | bytes 248864 | tf_op jit(solution)/shard_map/ppermute | solution.py:53
  77.0 13.7 %shard_map.79 = (bf16[2,72,864]{2,1,0:T(8,128)(2,1)S(1)}, bf16[2,72,864]{2,1,0:T(8,128)(2,1)S(1)}, bf16[2,72,864]{2,1,0:T(8,128)(2,1)S(1)}, bf16[2,72,864]{2,1,0...) custom-call(s32[4]{0:T(128)S(1)} %pad_add_fusion.at_ref, ...), custom_call_target="tpu_custom_call" | custom-call | flops 2717908992 | bytes 10485760 | tf_op jit(solution)/shard_map/pallas_call | solution.py:389
  90.7 1.6 shard_map.80
  94.5 1.9 %collective-permute-start.29 = (bf16[72,1152]{1,0:T(8,128)(2,1)S(1)}, bf16[72,1152]{1,0:T(8,128)(2,1)S(1)}, u32[]{:S(2)}, u32[]{:S(2)}) collective-permute-start(bf16[72,1152]{1,0:T(8,128)(2,1)S(1)} %get-tuple-element.39), channel_id=1, source_target_pairs={{0,8},{1,11},{4,12},{5,15},{10,16},{11,19},{14,20},{15,23},{18,24}... | collective-permute-start | bytes 497672 | tf_op jit(solution)/shard_map/ppermute | solution.py:53
  97.7 2.3 %collective-permute-done.26 = bf16[2,72,864]{2,1,0:T(8,128)(2,1)S(1)} collective-permute-done((bf16[2,72,864]{2,1,0:T(8,128)(2,1)S(1)}, bf16[2,72,864]{2,1,0:T(8,128)(2,1)S(1)}, u32[]{:S(2)}, u32[]{:S(2)}) %collective-permute-start.26) | collective-permute-done | bytes 248864 | tf_op jit(solution)/shard_map/ppermute | solution.py:53
  101.4 8.3 %collective-permute-start.23 = (bf16[2,72,864]{2,1,0:T(8,128)(2,1)S(1)}, bf16[2,72,864]{2,1,0:T(8,128)(2,1)S(1)}, u32[]{:S(2)}, u32[]{:S(2)}) collective-permute-start(bf16[2,72,864]{2,1,0:T(8,128)(2,1)S(1)} %get-tuple-element.34), channel_id=1, source_target_pairs={{0,16},{1,17},{2,18},{3,19},{4,20},{5,21},{6,22},{7,23},{24,8},{25... | collective-permute-start | bytes 746504 | tf_op jit(solution)/shard_map/ppermute | solution.py:53
  113.7 6.4 %collective-permute-done.24.refs_2_ = bf16[2,72,864]{2,1,0:T(8,128)(2,1)S(1)} collective-permute-done((bf16[2,72,864]{2,1,0:T(8,128)(2,1)S(1)}, bf16[2,72,864]{2,1,0:T(8,128)(2,1)S(1)}, u32[]{:S(2)}, u32[]{:S(2)}) %collective-permute-start.24) | collective-permute-done | bytes 248864 | tf_op jit(solution)/shard_map/ppermute | solution.py:53
  120.0 8.4 %collective-permute-done.27.refs_4_ = bf16[2,72,864]{2,1,0:T(8,128)(2,1)S(1)} collective-permute-done((bf16[2,72,864]{2,1,0:T(8,128)(2,1)S(1)}, bf16[2,72,864]{2,1,0:T(8,128)(2,1)S(1)}, u32[]{:S(2)}, u32[]{:S(2)}) %collective-permute-start.27) | collective-permute-done | bytes 248864 | tf_op jit(solution)/shard_map/ppermute | solution.py:53
  129.6 2.2 %collective-permute-start.34 = (bf16[72,432]{1,0:T(8,128)(2,1)S(1)}, bf16[72,432]{1,0:T(8,128)(2,1)S(1)}, u32[]{:S(2)}, u32[]{:S(2)}) collective-permute-start(bf16[72,432]{1,0:T(8,128)(2,1)S(1)} %get-tuple-element.44), channel_id=1, source_target_pairs={{0,3},{1,2},{2,1},{3,0},{4,7},{5,6},{6,5},{7,4},{8,11},{9,10},{10,... | collective-permute-start | bytes 186632 | tf_op jit(solution)/shard_map/ppermute | solution.py:53
  135.7 2.0 %collective-permute-start.36 = (bf16[72,432]{1,0:T(8,128)(2,1)S(1)}, bf16[72,432]{1,0:T(8,128)(2,1)S(1)}, u32[]{:S(2)}, u32[]{:S(2)}) collective-permute-start(bf16[72,432]{1,0:T(8,128)(2,1)S(1)} %get-tuple-element.45), channel_id=1, source_target_pairs={{0,5},{1,4},{2,7},{3,6},{4,1},{5,0},{6,3},{7,2},{8,13},{9,12},{10,... | collective-permute-start | bytes 186632 | tf_op jit(solution)/shard_map/ppermute | solution.py:53
  138.5 10.4 %collective-permute-done.36.refs_5_ = bf16[72,432]{1,0:T(8,128)(2,1)S(1)} collective-permute-done((bf16[72,432]{1,0:T(8,128)(2,1)S(1)}, bf16[72,432]{1,0:T(8,128)(2,1)S(1)}, u32[]{:S(2)}, u32[]{:S(2)}) %collective-permute-start.36) | collective-permute-done | bytes 62240 | tf_op jit(solution)/shard_map/ppermute | solution.py:53
  150.1 3.0 %collective-permute-done.35.refs_4_ = bf16[72,432]{1,0:T(8,128)(2,1)S(1)} collective-permute-done((bf16[72,432]{1,0:T(8,128)(2,1)S(1)}, bf16[72,432]{1,0:T(8,128)(2,1)S(1)}, u32[]{:S(2)}, u32[]{:S(2)}) %collective-permute-start.35) | collective-permute-done | bytes 62240 | tf_op jit(solution)/shard_map/ppermute | solution.py:53
  153.2 2.1 %collective-permute-start.38 = (bf16[72,432]{1,0:T(8,128)(2,1)S(1)}, bf16[72,432]{1,0:T(8,128)(2,1)S(1)}, u32[]{:S(2)}, u32[]{:S(2)}) collective-permute-start(bf16[72,432]{1,0:T(8,128)(2,1)S(1)} %get-tuple-element.46), channel_id=1, source_target_pairs={{0,7},{1,6},{2,5},{3,4},{4,3},{5,2},{6,1},{7,0},{8,15},{9,14},{10,... | collective-permute-start | bytes 186632 | tf_op jit(solution)/shard_map/ppermute | solution.py:53
  155.3 2.5 %collective-permute-done.38.refs_7_ = bf16[72,432]{1,0:T(8,128)(2,1)S(1)} collective-permute-done((bf16[72,432]{1,0:T(8,128)(2,1)S(1)}, bf16[72,432]{1,0:T(8,128)(2,1)S(1)}, u32[]{:S(2)}, u32[]{:S(2)}) %collective-permute-start.38) | collective-permute-done | bytes 62240 | tf_op jit(solution)/shard_map/ppermute | solution.py:53
  159.4 2.3 %collective-permute-done.37.refs_6_ = bf16[72,432]{1,0:T(8,128)(2,1)S(1)} collective-permute-done((bf16[72,432]{1,0:T(8,128)(2,1)S(1)}, bf16[72,432]{1,0:T(8,128)(2,1)S(1)}, u32[]{:S(2)}, u32[]{:S(2)}) %collective-permute-start.37) | collective-permute-done | bytes 62240 | tf_op jit(solution)/shard_map/ppermute | solution.py:53
  161.7 2.5 %shard_map.82 = f32[72,4608]{1,0:T(8,128)} custom-call(s32[4]{0:T(128)S(1)} %pad_add_fusion.at_ref, bf16[72,432]{1,0:T(8,128)(2,1)S(1)} %get-tuple-element.42.refs_0_, bf16[72,1584]{1,0:T(8,128)(2,1)S(1)} %collective-permute-done.32.refs_1_, bf16[72,432]{1,0:T(8,128)(2,1)S(1)} %collective-permute-done.33.refs_2_, ...), custom_call_target="tpu_custom_call" | custom-call | tf_op jit(solution)/shard_map/pallas_call | solution.py:462
  (60 shorter events, 28.7 us)
Async XLA Ops:
  0.6 12.1 %collective-permute-start.6 = (bf16[128,1152]{1,0:T(8,128)(2,1)}, bf16[128,1152]{1,0:T(8,128)(2,1)S(1)}, u32[]{:S(2)}, u32[]{:S(2)}) collective-permute-start(bf16[128,1152]{1,0:T(8,128)(2,1)} %bitcast.25), channel_id=1, source_target_pairs={{0,5},{1,4},{2,7},{3,6},{4,1},{5,0},{6,3},{7,2},{8,13},{9,12},{10,... | collective-permute-start | bytes 884744 | tf_op jit(solution)/shard_map/ppermute | solution.py:53
  4.6 14.5 %collective-permute-start.5 = (bf16[128,1152]{1,0:T(8,128)(2,1)}, bf16[128,1152]{1,0:T(8,128)(2,1)S(1)}, u32[]{:S(2)}, u32[]{:S(2)}) collective-permute-start(bf16[128,1152]{1,0:T(8,128)(2,1)} %bitcast.26), channel_id=1, source_target_pairs={{0,1},{1,0},{2,3},{3,2},{4,5},{5,4},{6,7},{7,6},{8,9},{9,8},{10,11... | collective-permute-start | bytes 884744 | tf_op jit(solution)/shard_map/ppermute | solution.py:53
  5.1 14.5 %collective-permute-start.4 = (bf16[128,1152]{1,0:T(8,128)(2,1)}, bf16[128,1152]{1,0:T(8,128)(2,1)S(1)}, u32[]{:S(2)}, u32[]{:S(2)}) collective-permute-start(bf16[128,1152]{1,0:T(8,128)(2,1)} %bitcast.27), channel_id=1, source_target_pairs={{0,4},{1,5},{2,6},{3,7},{4,0},{5,1},{6,2},{7,3},{8,12},{9,13},{10,... | collective-permute-start | bytes 884744 | tf_op jit(solution)/shard_map/ppermute | solution.py:53
  5.3 20.2 %collective-permute-start.2 = (bf16[128,1152]{1,0:T(8,128)(2,1)}, bf16[128,1152]{1,0:T(8,128)(2,1)S(1)}, u32[]{:S(2)}, u32[]{:S(2)}) collective-permute-start(bf16[128,1152]{1,0:T(8,128)(2,1)} %bitcast.29), channel_id=1, source_target_pairs={{0,5},{1,4},{2,7},{3,6},{4,1},{5,0},{6,3},{7,2},{8,13},{9,12},{10,... | collective-permute-start | bytes 884744 | tf_op jit(solution)/shard_map/ppermute | solution.py:53
  8.1 22.7 %collective-permute-start.1 = (bf16[128,1152]{1,0:T(8,128)(2,1)}, bf16[128,1152]{1,0:T(8,128)(2,1)S(1)}, u32[]{:S(2)}, u32[]{:S(2)}) collective-permute-start(bf16[128,1152]{1,0:T(8,128)(2,1)} %bitcast.30), channel_id=1, source_target_pairs={{0,1},{1,0},{2,3},{3,2},{4,5},{5,4},{6,7},{7,6},{8,9},{9,8},{10,11... | collective-permute-start | bytes 884744 | tf_op jit(solution)/shard_map/ppermute | solution.py:53
  12.7 18.4 %collective-permute-start = (bf16[128,1152]{1,0:T(8,128)(2,1)}, bf16[128,1152]{1,0:T(8,128)(2,1)S(1)}, u32[]{:S(2)}, u32[]{:S(2)}) collective-permute-start(bf16[128,1152]{1,0:T(8,128)(2,1)} %bitcast.31), channel_id=1, source_target_pairs={{0,4},{1,5},{2,6},{3,7},{4,0},{5,1},{6,2},{7,3},{8,12},{9,13},{10,... | collective-permute-start | bytes 884744 | tf_op jit(solution)/shard_map/ppermute | solution.py:53
  20.8 56.2 %collective-permute-start.7 = (bf16[4,128,1152]{2,1,0:T(8,128)(2,1)S(1)}, bf16[4,128,1152]{2,1,0:T(8,128)(2,1)S(1)}, u32[]{:S(2)}, u32[]{:S(2)}) collective-permute-start(bf16[4,128,1152]{2,1,0:T(8,128)(2,1)S(1)} %pad_maximum_fusion.1.refs_2_), channel_id=1, source_target_pairs={{0,2},{1,3},{2,0},{3,1},{4,6},{5,7},{6,4},{7,5},{8,10},{9,11},{10,... | collective-permute-start | bytes 3538952 | tf_op jit(solution)/shard_map/ppermute | solution.py:53
  31.3 45.7 %collective-permute-start.3 = (bf16[4,128,1152]{2,1,0:T(8,128)(2,1)S(1)}, bf16[4,128,1152]{2,1,0:T(8,128)(2,1)}, u32[]{:S(2)}, u32[]{:S(2)}) collective-permute-start(bf16[4,128,1152]{2,1,0:T(8,128)(2,1)S(1)} %pad_maximum_fusion.refs_0_), channel_id=1, source_target_pairs={{0,2},{1,3},{2,0},{3,1},{4,6},{5,7},{6,4},{7,5},{8,10},{9,11},{10,... | collective-permute-start | bytes 3538952 | tf_op jit(solution)/shard_map/ppermute | solution.py:53
  34.7 6.6 %collective-permute-start.9 = (bf16[72,432]{1,0:T(8,128)(2,1)S(1)}, bf16[72,432]{1,0:T(8,128)(2,1)S(1)}, u32[]{:S(2)}, u32[]{:S(2)}) collective-permute-start(bf16[72,432]{1,0:T(8,128)(2,1)S(1)} %get-tuple-element.27), channel_id=1, source_target_pairs={{0,4},{1,5},{2,6},{3,7},{4,0},{5,1},{6,2},{7,3},{8,12},{9,13},{10,... | collective-permute-start | bytes 186632 | tf_op jit(solution)/shard_map/ppermute | solution.py:53
  36.2 11.5 %collective-permute-start.16 = (bf16[72,1152]{1,0:T(8,128)(2,1)}, bf16[72,1152]{1,0:T(8,128)(2,1)S(1)}, u32[]{:S(2)}, u32[]{:S(2)}) collective-permute-start(bf16[72,1152]{1,0:T(8,128)(2,1)} %param.11), channel_id=1, source_target_pairs={{0,8},{3,9},{4,12},{7,13},{8,16},{11,17},{12,20},{15,21},{16,26},{... | collective-permute-start | bytes 497672 | tf_op jit(solution)/shard_map/ppermute | solution.py:53
  39.7 12.1 %collective-permute-start.15 = (bf16[72,1152]{1,0:T(8,128)(2,1)}, bf16[72,1152]{1,0:T(8,128)(2,1)S(1)}, u32[]{:S(2)}, u32[]{:S(2)}) collective-permute-start(bf16[72,1152]{1,0:T(8,128)(2,1)} %param.11), channel_id=1, source_target_pairs={{0,0},{3,1},{4,4},{7,5},{8,8},{11,9},{12,12},{15,13},{16,18},{19,1... | collective-permute-start | bytes 497672 | tf_op jit(solution)/shard_map/ppermute | solution.py:53
  45.9 21.1 %collective-permute-start.12 = (bf16[2,72,864]{2,1,0:T(8,128)(2,1)S(1)}, bf16[2,72,864]{2,1,0:T(8,128)(2,1)S(1)}, u32[]{:S(2)}, u32[]{:S(2)}) collective-permute-start(bf16[2,72,864]{2,1,0:T(8,128)(2,1)S(1)} %shard_map.78.refs_4_), channel_id=1, source_target_pairs={{0,16},{1,17},{2,18},{3,19},{4,20},{5,21},{6,22},{7,23},{8,24},{9,... | collective-permute-start | bytes 746504 | tf_op jit(solution)/shard_map/ppermute | solution.py:53
  47.7 9.2 %collective-permute-start.18 = (bf16[72,1152]{1,0:T(8,128)(2,1)}, bf16[72,1152]{1,0:T(8,128)(2,1)S(1)}, u32[]{:S(2)}, u32[]{:S(2)}) collective-permute-start(bf16[72,1152]{1,0:T(8,128)(2,1)} %param.11), channel_id=1, source_target_pairs={{0,24},{3,25},{4,28},{7,29},{8,0},{11,1},{12,4},{15,5},{16,10},{19... | collective-permute-start | bytes 497672 | tf_op jit(solution)/shard_map/ppermute | solution.py:53
  51.8 6.4 %collective-permute-start.17 = (bf16[72,1152]{1,0:T(8,128)(2,1)}, bf16[72,1152]{1,0:T(8,128)(2,1)S(1)}, u32[]{:S(2)}, u32[]{:S(2)}) collective-permute-start(bf16[72,1152]{1,0:T(8,128)(2,1)} %param.11), channel_id=1, source_target_pairs={{0,16},{3,17},{4,20},{7,21},{8,24},{11,25},{12,28},{15,29},{16,2},... | collective-permute-start | bytes 497672 | tf_op jit(solution)/shard_map/ppermute | solution.py:53
  56.9 11.3 %collective-permute-start.13 = (bf16[2,72,864]{2,1,0:T(8,128)(2,1)S(1)}, bf16[2,72,864]{2,1,0:T(8,128)(2,1)S(1)}, u32[]{:S(2)}, u32[]{:S(2)}) collective-permute-start(bf16[2,72,864]{2,1,0:T(8,128)(2,1)S(1)} %shard_map.78.refs_4_), channel_id=1, source_target_pairs={{8,0},{9,1},{10,2},{11,3},{12,4},{13,5},{14,6},{15,7},{16,8},{17,9... | collective-permute-start | bytes 746504 | tf_op jit(solution)/shard_map/ppermute | solution.py:53
  58.2 14.6 %collective-permute-start.11 = (bf16[2,72,864]{2,1,0:T(8,128)(2,1)S(1)}, bf16[2,72,864]{2,1,0:T(8,128)(2,1)S(1)}, u32[]{:S(2)}, u32[]{:S(2)}) collective-permute-start(bf16[2,72,864]{2,1,0:T(8,128)(2,1)S(1)} %shard_map.78.refs_4_), channel_id=1, source_target_pairs={{0,8},{1,9},{2,10},{3,11},{4,12},{5,13},{6,14},{7,15},{8,16},{9,17... | collective-permute-start | bytes 746504 | tf_op jit(solution)/shard_map/ppermute | solution.py:53
  66.9 10.1 %collective-permute-start.14 = (bf16[2,72,864]{2,1,0:T(8,128)(2,1)S(1)}, bf16[2,72,864]{2,1,0:T(8,128)(2,1)S(1)}, u32[]{:S(2)}, u32[]{:S(2)}) collective-permute-start(bf16[2,72,864]{2,1,0:T(8,128)(2,1)S(1)} %collective-permute-done.12.refs_6_), channel_id=1, source_target_pairs={{8,0},{9,1},{10,2},{11,3},{12,4},{13,5},{14,6},{15,7},{16,24},{17,... | collective-permute-start | bytes 746504 | tf_op jit(solution)/shard_map/ppermute | solution.py:53
  92.2 39.5 %collective-permute-start.19 = (bf16[4,128,1152]{2,1,0:T(8,128)(2,1)S(1)}, bf16[4,128,1152]{2,1,0:T(8,128)(2,1)S(1)}, u32[]{:S(2)}, u32[]{:S(2)}) collective-permute-start(bf16[4,128,1152]{2,1,0:T(8,128)(2,1)S(1)} %get-tuple-element.32), channel_id=1, source_target_pairs={{0,2},{1,3},{2,0},{3,1},{4,6},{5,7},{6,4},{7,5},{8,10},{9,11},{10,... | collective-permute-start | bytes 3538952 | tf_op jit(solution)/shard_map/ppermute | solution.py:53
  92.3 7.7 %collective-permute-start.26 = (bf16[2,72,864]{2,1,0:T(8,128)(2,1)S(1)}, bf16[2,72,864]{2,1,0:T(8,128)(2,1)S(1)}, u32[]{:S(2)}, u32[]{:S(2)}) collective-permute-start(bf16[2,72,864]{2,1,0:T(8,128)(2,1)S(1)} %get-tuple-element.37), channel_id=1, source_target_pairs={{0,8},{1,9},{2,10},{3,11},{4,12},{5,13},{6,14},{7,15},{24,16},{25,... | collective-permute-start | bytes 746504 | tf_op jit(solution)/shard_map/ppermute | solution.py:53
  93.8 7.6 %collective-permute-start.28 = (bf16[72,1152]{1,0:T(8,128)(2,1)S(1)}, bf16[72,1152]{1,0:T(8,128)(2,1)S(1)}, u32[]{:S(2)}, u32[]{:S(2)}) collective-permute-start(bf16[72,1152]{1,0:T(8,128)(2,1)S(1)} %get-tuple-element.38), channel_id=1, source_target_pairs={{0,0},{1,3},{4,4},{5,7},{8,8},{9,11},{12,12},{13,15},{18,16},{19,1... | collective-permute-start | bytes 497672 | tf_op jit(solution)/shard_map/ppermute | solution.py:53
  94.5 15.2 %collective-permute-start.29 = (bf16[72,1152]{1,0:T(8,128)(2,1)S(1)}, bf16[72,1152]{1,0:T(8,128)(2,1)S(1)}, u32[]{:S(2)}, u32[]{:S(2)}) collective-permute-start(bf16[72,1152]{1,0:T(8,128)(2,1)S(1)} %get-tuple-element.39), channel_id=1, source_target_pairs={{0,8},{1,11},{4,12},{5,15},{10,16},{11,19},{14,20},{15,23},{18,24}... | collective-permute-start | bytes 497672 | tf_op jit(solution)/shard_map/ppermute | solution.py:53
  96.4 14.6 %collective-permute-start.30 = (bf16[72,1152]{1,0:T(8,128)(2,1)S(1)}, bf16[72,1152]{1,0:T(8,128)(2,1)S(1)}, u32[]{:S(2)}, u32[]{:S(2)}) collective-permute-start(bf16[72,1152]{1,0:T(8,128)(2,1)S(1)} %get-tuple-element.40), channel_id=1, source_target_pairs={{2,16},{3,19},{6,20},{7,23},{10,24},{11,27},{14,28},{15,31},{16,0}... | collective-permute-start | bytes 497672 | tf_op jit(solution)/shard_map/ppermute | solution.py:53
  100.0 12.4 %collective-permute-start.31 = (bf16[72,1152]{1,0:T(8,128)(2,1)S(1)}, bf16[72,1152]{1,0:T(8,128)(2,1)S(1)}, u32[]{:S(2)}, u32[]{:S(2)}) collective-permute-start(bf16[72,1152]{1,0:T(8,128)(2,1)S(1)} %get-tuple-element.41), channel_id=1, source_target_pairs={{2,24},{3,27},{6,28},{7,31},{8,0},{9,3},{12,4},{13,7},{16,8},{17,1... | collective-permute-start | bytes 497672 | tf_op jit(solution)/shard_map/ppermute | solution.py:53
  101.4 18.7 %collective-permute-start.23 = (bf16[2,72,864]{2,1,0:T(8,128)(2,1)S(1)}, bf16[2,72,864]{2,1,0:T(8,128)(2,1)S(1)}, u32[]{:S(2)}, u32[]{:S(2)}) collective-permute-start(bf16[2,72,864]{2,1,0:T(8,128)(2,1)S(1)} %get-tuple-element.34), channel_id=1, source_target_pairs={{0,16},{1,17},{2,18},{3,19},{4,20},{5,21},{6,22},{7,23},{24,8},{25... | collective-permute-start | bytes 746504 | tf_op jit(solution)/shard_map/ppermute | solution.py:53
  109.7 10.3 %collective-permute-start.24 = (bf16[2,72,864]{2,1,0:T(8,128)(2,1)S(1)}, bf16[2,72,864]{2,1,0:T(8,128)(2,1)S(1)}, u32[]{:S(2)}, u32[]{:S(2)}) collective-permute-start(bf16[2,72,864]{2,1,0:T(8,128)(2,1)S(1)} %get-tuple-element.35), channel_id=1, source_target_pairs={{0,8},{1,9},{2,10},{3,11},{4,12},{5,13},{6,14},{7,15},{8,16},{9,17... | collective-permute-start | bytes 746504 | tf_op jit(solution)/shard_map/ppermute | solution.py:53
  111.0 9.0 %collective-permute-start.25 = (bf16[2,72,864]{2,1,0:T(8,128)(2,1)S(1)}, bf16[2,72,864]{2,1,0:T(8,128)(2,1)S(1)}, u32[]{:S(2)}, u32[]{:S(2)}) collective-permute-start(bf16[2,72,864]{2,1,0:T(8,128)(2,1)S(1)} %get-tuple-element.36), channel_id=1, source_target_pairs={{8,0},{9,1},{10,2},{11,3},{12,4},{13,5},{14,6},{15,7},{16,8},{17,9... | collective-permute-start | bytes 746504 | tf_op jit(solution)/shard_map/ppermute | solution.py:53
  112.4 16.1 %collective-permute-start.27 = (bf16[2,72,864]{2,1,0:T(8,128)(2,1)S(1)}, bf16[2,72,864]{2,1,0:T(8,128)(2,1)S(1)}, u32[]{:S(2)}, u32[]{:S(2)}) collective-permute-start(bf16[2,72,864]{2,1,0:T(8,128)(2,1)S(1)} %add_convert_fusion.3), channel_id=1, source_target_pairs={{8,24},{9,25},{10,26},{11,27},{12,28},{13,29},{14,30},{15,31},{16,... | collective-permute-start | bytes 746504 | tf_op jit(solution)/shard_map/ppermute | solution.py:53
  132.0 32.2 %collective-permute-start.20 = (bf16[128,1152]{1,0:T(8,128)(2,1)S(1)}, bf16[128,1152]{1,0:T(8,128)(2,1)S(1)}, u32[]{:S(2)}, u32[]{:S(2)}) collective-permute-start(bf16[128,1152]{1,0:T(8,128)(2,1)S(1)} %get-tuple-element.48), channel_id=1, source_target_pairs={{0,4},{1,5},{2,6},{3,7},{4,0},{5,1},{6,2},{7,3},{8,12},{9,13},{10,... | collective-permute-start | bytes 884744 | tf_op jit(solution)/shard_map/ppermute | solution.py:53
  133.4 30.9 %collective-permute-start.22 = (bf16[128,1152]{1,0:T(8,128)(2,1)S(1)}, bf16[128,1152]{1,0:T(8,128)(2,1)S(1)}, u32[]{:S(2)}, u32[]{:S(2)}) collective-permute-start(bf16[128,1152]{1,0:T(8,128)(2,1)S(1)} %get-tuple-element.49), channel_id=1, source_target_pairs={{0,5},{1,4},{2,7},{3,6},{4,1},{5,0},{6,3},{7,2},{8,13},{9,12},{10,... | collective-permute-start | bytes 884744 | tf_op jit(solution)/shard_map/ppermute | solution.py:53
  134.4 29.8 %collective-permute-start.21 = (bf16[128,1152]{1,0:T(8,128)(2,1)S(1)}, bf16[128,1152]{1,0:T(8,128)(2,1)S(1)}, u32[]{:S(2)}, u32[]{:S(2)}) collective-permute-start(bf16[128,1152]{1,0:T(8,128)(2,1)S(1)} %get-tuple-element.50), channel_id=1, source_target_pairs={{0,1},{1,0},{2,3},{3,2},{4,5},{5,4},{6,7},{7,6},{8,9},{9,8},{10,11... | collective-permute-start | bytes 884744 | tf_op jit(solution)/shard_map/ppermute | solution.py:53
  135.7 13.2 %collective-permute-start.36 = (bf16[72,432]{1,0:T(8,128)(2,1)S(1)}, bf16[72,432]{1,0:T(8,128)(2,1)S(1)}, u32[]{:S(2)}, u32[]{:S(2)}) collective-permute-start(bf16[72,432]{1,0:T(8,128)(2,1)S(1)} %get-tuple-element.45), channel_id=1, source_target_pairs={{0,5},{1,4},{2,7},{3,6},{4,1},{5,0},{6,3},{7,2},{8,13},{9,12},{10,... | collective-permute-start | bytes 186632 | tf_op jit(solution)/shard_map/ppermute | solution.py:53
  137.7 24.0 %collective-permute-start.32 = (bf16[72,1584]{1,0:T(8,128)(2,1)S(1)}, bf16[72,1584]{1,0:T(8,128)(2,1)S(1)}, u32[]{:S(2)}, u32[]{:S(2)}) collective-permute-start(bf16[72,1584]{1,0:T(8,128)(2,1)S(1)} %get-tuple-element.43), channel_id=1, source_target_pairs={{0,1},{1,0},{2,3},{3,2},{4,5},{5,4},{6,7},{7,6},{8,9},{9,8},{10,11... | collective-permute-start | bytes 684296 | tf_op jit(solution)/shard_map/ppermute | solution.py:53
  (8 other events, 41.9 us)

commit v4 on v3

--- a/solution.py
+++ b/solution.py
@@ -199,20 +199,30 @@
         full[p * shard : (p + 1) * shard, :] = loose[p]
 
 
-def attention_kernel(scale, lines, at_ref, *refs):
-    xs, xc, ds, dc = refs[:4]
-    moved = 4 + lines + (lines > 2)
+def project_kernel(lines, at_ref, *refs):
+    xs, xc = refs[:2]
+    planes, (qkv_ref, full, loose) = refs[2:-3], refs[-3:]
+    full_weights(lines, at_ref, planes, loose, full)
+    half = xs.shape[0] * xs.shape[1]
+    each = BLOCK // xs.shape[1]
+    for part, x_ref in enumerate((xs, xc)):
+        for j in range(half // BLOCK):
+            x = x_ref[each * j : each * (j + 1)].reshape(BLOCK, xs.shape[-1])
+            row = part * half + j * BLOCK
+            value = matmul(x, full[...], ((1,), (0,)))
+            qkv_ref[row : row + BLOCK, :] = value.astype(jnp.bfloat16)
+
+
+def attention_kernel(scale, lines, owed, at_ref, *refs):
+    xs, xc, ds, dc, qkv_ref = refs[:5]
     sent = lines + (lines == 4)
-    owed = lines if len(refs) > moved + 1 + sent + 9 else 1
-    planes, out_ws = refs[4:moved], refs[moved : moved + owed]
-    grads_in = refs[moved + owed : moved + owed + sent]
-    grads_out = refs[moved + owed + sent : moved + 2 * owed + sent]
-    dqkv_ref, full, loose, out_w, att, grads, bias = refs[moved + 2 * owed + sent :]
+    out_ws, grads_in = refs[5 : 5 + owed], refs[5 + owed : 5 + owed + sent]
+    grads_out = refs[5 + owed + sent : 5 + 2 * owed + sent]
+    dqkv_ref, loose, out_w, att, grads, bias = refs[5 + 2 * owed + sent :]
     shard, wide = loose.shape[1:]
     dim = wide // (3 * KEPT)
     width = xs.shape[-1]
-    full_weights(lines, at_ref, planes, loose, full)
-    if len(out_ws) == 1:
+    if owed == 1:
         out_w[...] = out_ws[0][...]
     else:
         for s, held in enumerate(out_ws):
@@ -227,14 +237,13 @@
     bias[...] = jnp.where(site(0) == site(1), 0.0, -1e30)
     half = xs.shape[0] * xs.shape[1]
     each = BLOCK // xs.shape[1]
-    for part, (x_ref, d_ref) in enumerate(((xs, ds), (xc, dc))):
-
-        def block(j, _, part=part, x_ref=x_ref, d_ref=d_ref):
-            x = x_ref[pl.ds(each * j, each)].reshape(BLOCK, width)
+    for part, d_ref in enumerate((ds, dc)):
+
+        def block(j, _, part=part, d_ref=d_ref):
             d = d_ref[pl.ds(each * j, each)].reshape(BLOCK, width)
-            qkv = matmul(x, full[...], ((1,), (0,))).astype(jnp.bfloat16)
             da = matmul(d, out_w[...], ((1,), (1,))).astype(jnp.bfloat16)
             row = pl.multiple_of(part * half + j * BLOCK, BLOCK)
+            qkv = qkv_ref[pl.ds(row, BLOCK), :]
             cut = lambda v, n: v[:, n * dim : (n + 1) * dim]
             outs = [
                 attend(
@@ -386,14 +395,26 @@
     sent = lines + (lines == 4)
     owed = len(out_ws)
     head_rows = dim if one_head else wide
-    *results, dqkv, full = pl.pallas_call(
-        functools.partial(attention_kernel, scale, lines),
+    project = pl.pallas_call(
+        functools.partial(project_kernel, lines),
+        compiler_params=room(16),
+        out_shape=(shape_of(total, 3 * wide), shape_of(width, 3 * wide)),
+        in_specs=[SMEM] + [VMEM] * (2 + len(planes)),
+        out_specs=(VMEM,) * 2,
+        scratch_shapes=[pltpu.VMEM((pix, shard, 3 * wide), jnp.bfloat16)],
+        cost_estimate=pl.CostEstimate(
+            flops=6 * total * width * wide, bytes_accessed=6 << 20, transcendentals=0
+        ),
+    )
+    qkv, full = project(at, xs, xc, *planes)
+    *results, dqkv = pl.pallas_call(
+        functools.partial(attention_kernel, scale, lines, owed),
         compiler_params=room(28),
         out_shape=(shape_of(2, shard, 6 * wide),) * sent
         + (shape_of(head_rows, width),) * owed
-        + (shape_of(total, 3 * wide), shape_of(width, 3 * wide)),
-        in_specs=[SMEM] + [VMEM] * (4 + len(planes) + len(out_ws)),
-        out_specs=(VMEM,) * (sent + owed + 2),
+        + (shape_of(total, 3 * wide),),
+        in_specs=[SMEM] + [VMEM] * (5 + owed),
+        out_specs=(VMEM,) * (sent + owed + 1),
         scratch_shapes=[
             pltpu.VMEM((pix, shard, 3 * wide), jnp.bfloat16),
             pltpu.VMEM((wide, width), jnp.bfloat16),
@@ -402,9 +423,9 @@
             pltpu.VMEM((BLOCK, BLOCK), jnp.float32),
         ],
         cost_estimate=pl.CostEstimate(
-            flops=8 * total * width * wide * 2, bytes_accessed=10 << 20, transcendentals=total * 32
+            flops=12 * total * width * wide, bytes_accessed=10 << 20, transcendentals=total * 512
         ),
-    )(at, xs, xc, ds, dc, *planes, *out_ws)
+    )(at, xs, xc, ds, dc, qkv, *out_ws)
 
     grads_in, grads_out = results[:sent], results[sent:]
     parts = grid.scatter_lines(grads_in)

time: 166 us -> 164 us (0.988)
  starting transfers between devices: 68.4 us -> 63.4 us
  waiting for transfers between devices: 70.9 us -> 74.7 us
    ppermute x39, starting transfers between devices: 68.4 us -> 63.4 us  [send(): return lax.ppermute(value, BOTH, pairs)]
    ppermute x39, waiting for transfers between devices: 70.9 us -> 74.7 us  [send(): return lax.ppermute(value, BOTH, pairs)]
    pallas_call x1 -> x2, Pallas kernels: 13.7 us -> 13.3 us  [the longest x1 10.8 us: local(): pl.pallas_call(functools.partial(attention_kernel, scale, lines, owed), c...]
  transfers between devices with their start and end apart: 39 -> 39, of which waited for: 17 -> 21; matrix products, arithmetic and copies ran while one was open for 1% -> 1% of each run, Pallas kernels for 4% -> 6%
where the time goes in v4:
time: 164 us
  waiting for transfers between devices  74.7 us (46%)
  starting transfers between devices  63.4 us (39%)
  Pallas kernels  22 us (13%)
  other arithmetic  2.61 us (2%)
    ppermute x39, waiting for transfers between devices, send(): return lax.ppermute(value, BOTH, pairs)  74.7 us
    ppermute x39, starting transfers between devices, send(): return lax.ppermute(value, BOTH, pairs)  63.4 us
    pallas_call x1, Pallas kernels, local(): pl.pallas_call(functools.partial(attention_kernel, scale, lines, owed), c...  10.8 us
  transfers between devices with their start and end apart: 39, of which 21 were waited for; matrix products, arithmetic and copies ran while one was open for 1% of the time, Pallas kernels for 6%

profile of v4, /device:TPU:0, one launch (start us, length us, event | category | flops | bytes accessed | tf_op | source)
XLA Modules:
  0.0 163.7 jit_solution(4145749377399376579)
XLA Ops:
  0.6 4.0 %collective-permute-start.2 = (bf16[128,1152]{1,0:T(8,128)(2,1)}, bf16[128,1152]{1,0:T(8,128)(2,1)S(1)}, u32[]{:S(2)}, u32[]{:S(2)}) collective-permute-start(bf16[128,1152]{1,0:T(8,128)(2,1)} %bitcast.25), channel_id=1, source_target_pairs={{0,5},{1,4},{2,7},{3,6},{4,1},{5,0},{6,3},{7,2},{8,13},{9,12},{10,... | collective-permute-start | bytes 884744 | tf_op jit(solution)/shard_map/ppermute | solution.py:53
  5.3 2.8 %collective-permute-start.6 = (bf16[128,1152]{1,0:T(8,128)(2,1)}, bf16[128,1152]{1,0:T(8,128)(2,1)S(1)}, u32[]{:S(2)}, u32[]{:S(2)}) collective-permute-start(bf16[128,1152]{1,0:T(8,128)(2,1)} %bitcast.29), channel_id=1, source_target_pairs={{0,5},{1,4},{2,7},{3,6},{4,1},{5,0},{6,3},{7,2},{8,13},{9,12},{10,... | collective-permute-start | bytes 884744 | tf_op jit(solution)/shard_map/ppermute | solution.py:53
  8.6 4.1 %collective-permute-done.2 = bf16[128,1152]{1,0:T(8,128)(2,1)S(1)} collective-permute-done((bf16[128,1152]{1,0:T(8,128)(2,1)}, bf16[128,1152]{1,0:T(8,128)(2,1)S(1)}, u32[]{:S(2)}, u32[]{:S(2)}) %collective-permute-start.2) | collective-permute-done | bytes 294944 | tf_op jit(solution)/shard_map/ppermute | solution.py:53
  12.7 2.0 %collective-permute-start.4 = (bf16[128,1152]{1,0:T(8,128)(2,1)}, bf16[128,1152]{1,0:T(8,128)(2,1)S(1)}, u32[]{:S(2)}, u32[]{:S(2)}) collective-permute-start(bf16[128,1152]{1,0:T(8,128)(2,1)} %bitcast.31), channel_id=1, source_target_pairs={{0,4},{1,5},{2,6},{3,7},{4,0},{5,1},{6,2},{7,3},{8,12},{9,13},{10,... | collective-permute-start | bytes 884744 | tf_op jit(solution)/shard_map/ppermute | solution.py:53
  14.7 4.4 %collective-permute-done.1 = bf16[128,1152]{1,0:T(8,128)(2,1)S(1)} collective-permute-done((bf16[128,1152]{1,0:T(8,128)(2,1)}, bf16[128,1152]{1,0:T(8,128)(2,1)S(1)}, u32[]{:S(2)}, u32[]{:S(2)}) %collective-permute-start.1) | collective-permute-done | bytes 294944 | tf_op jit(solution)/shard_map/ppermute | solution.py:53
  20.8 4.6 %collective-permute-done.6 = bf16[128,1152]{1,0:T(8,128)(2,1)S(1)} collective-permute-done((bf16[128,1152]{1,0:T(8,128)(2,1)}, bf16[128,1152]{1,0:T(8,128)(2,1)S(1)}, u32[]{:S(2)}, u32[]{:S(2)}) %collective-permute-start.6) | collective-permute-done | bytes 294944 | tf_op jit(solution)/shard_map/ppermute | solution.py:53
  25.4 5.4 %collective-permute-done.5 = bf16[128,1152]{1,0:T(8,128)(2,1)S(1)} collective-permute-done((bf16[128,1152]{1,0:T(8,128)(2,1)}, bf16[128,1152]{1,0:T(8,128)(2,1)S(1)}, u32[]{:S(2)}, u32[]{:S(2)}) %collective-permute-start.5) | collective-permute-done | bytes 294944 | tf_op jit(solution)/shard_map/ppermute | solution.py:53
  31.5 2.7 %shard_map.77 = (bf16[72,432]{1,0:T(8,128)(2,1)S(1)}, bf16[72,432]{1,0:T(8,128)(2,1)S(1)}, bf16[72,432]{1,0:T(8,128)(2,1)S(1)}, bf16[72,432]{1,0:T(8,128)(2,1)S(1)}) custom-call(s32[4]{0:T(128)S(1)} %pad_add_fusion.at_ref, bf16[72,1152]{1,0:T(8,128)(2,1)} %refs_0_.1, bf16[72,1152]{1,0:T(8,128)(2,1)} %refs_1_.1, bf16[72,1152]{1,0:T(8,128)(2,1)} %refs_2_.1), custom_call_target="tpu_custom_call" | custom-call | tf_op jit(solution)/shard_map/pallas_call | solution.py:355
  34.7 1.5 collective-permute-start.9
  36.2 2.9 %collective-permute-done.9.refs_2_ = bf16[72,432]{1,0:T(8,128)(2,1)S(1)} collective-permute-done((bf16[72,432]{1,0:T(8,128)(2,1)S(1)}, bf16[72,432]{1,0:T(8,128)(2,1)S(1)}, u32[]{:S(2)}, u32[]{:S(2)}) %collective-permute-start.9) | collective-permute-done | bytes 62240 | tf_op jit(solution)/shard_map/ppermute | solution.py:53
  39.1 1.7 %collective-permute-done.10.refs_3_ = bf16[72,432]{1,0:T(8,128)(2,1)S(1)} collective-permute-done((bf16[72,432]{1,0:T(8,128)(2,1)S(1)}, bf16[72,432]{1,0:T(8,128)(2,1)S(1)}, u32[]{:S(2)}, u32[]{:S(2)}) %collective-permute-start.10) | collective-permute-done | bytes 62240 | tf_op jit(solution)/shard_map/ppermute | solution.py:53
  41.6 2.7 %collective-permute-start.12 = (bf16[2,72,864]{2,1,0:T(8,128)(2,1)S(1)}, bf16[2,72,864]{2,1,0:T(8,128)(2,1)S(1)}, u32[]{:S(2)}, u32[]{:S(2)}) collective-permute-start(bf16[2,72,864]{2,1,0:T(8,128)(2,1)S(1)} %shard_map.78.refs_2_), channel_id=1, source_target_pairs={{0,16},{1,17},{2,18},{3,19},{4,20},{5,21},{6,22},{7,23},{8,24},{9,... | collective-permute-start | bytes 746504 | tf_op jit(solution)/shard_map/ppermute | solution.py:53
  45.5 4.6 %collective-permute-start.11 = (bf16[2,72,864]{2,1,0:T(8,128)(2,1)S(1)}, bf16[2,72,864]{2,1,0:T(8,128)(2,1)S(1)}, u32[]{:S(2)}, u32[]{:S(2)}) collective-permute-start(bf16[2,72,864]{2,1,0:T(8,128)(2,1)S(1)} %shard_map.78.refs_2_), channel_id=1, source_target_pairs={{0,8},{1,9},{2,10},{3,11},{4,12},{5,13},{6,14},{7,15},{8,16},{9,17... | collective-permute-start | bytes 746504 | tf_op jit(solution)/shard_map/ppermute | solution.py:53
  50.1 7.1 %collective-permute-done.12.refs_4_ = bf16[2,72,864]{2,1,0:T(8,128)(2,1)S(1)} collective-permute-done((bf16[2,72,864]{2,1,0:T(8,128)(2,1)S(1)}, bf16[2,72,864]{2,1,0:T(8,128)(2,1)S(1)}, u32[]{:S(2)}, u32[]{:S(2)}) %collective-permute-start.12) | collective-permute-done | bytes 248864 | tf_op jit(solution)/shard_map/ppermute | solution.py:53
  58.5 5.8 %collective-permute-start.16 = (bf16[72,1152]{1,0:T(8,128)(2,1)}, bf16[72,1152]{1,0:T(8,128)(2,1)S(1)}, u32[]{:S(2)}, u32[]{:S(2)}) collective-permute-start(bf16[72,1152]{1,0:T(8,128)(2,1)} %param.11), channel_id=1, source_target_pairs={{0,8},{3,9},{4,12},{7,13},{8,16},{11,17},{12,20},{15,21},{16,26},{... | collective-permute-start | bytes 497672 | tf_op jit(solution)/shard_map/ppermute | solution.py:53
  64.3 1.6 collective-permute-start.15
  67.3 4.4 %collective-permute-start.18 = (bf16[72,1152]{1,0:T(8,128)(2,1)}, bf16[72,1152]{1,0:T(8,128)(2,1)S(1)}, u32[]{:S(2)}, u32[]{:S(2)}) collective-permute-start(bf16[72,1152]{1,0:T(8,128)(2,1)} %param.11), channel_id=1, source_target_pairs={{0,24},{3,25},{4,28},{7,29},{8,0},{11,1},{12,4},{15,5},{16,10},{19... | collective-permute-start | bytes 497672 | tf_op jit(solution)/shard_map/ppermute | solution.py:53
  73.1 2.5 %shard_map.79 = (bf16[1024,432]{1,0:T(8,128)(2,1)S(1)}, bf16[1152,432]{1,0:T(8,128)(2,1)S(1)}) custom-call(s32[4]{0:T(128)S(1)} %pad_add_fusion.at_ref, bf16[4,128,1152]{2,1,0:T(8,128)(2,1)S(1)} %pad_maximum_fusion.refs_0_, bf16[4,128,1152]{2,1,0:T(8,128)(2,1)S(1)} %collective-permute-done.3.refs_1_, bf16[2,72,864]{2,1,0:T(8,128)(2,1)S(1)} %shard_map.78.refs_2_, ...), custom_call_target="tpu_custom_call" | custom-call | flops 1019215872 | bytes 6291456 | tf_op jit(solution)/shard_map/pallas_call | solution.py:409
  76.7 10.8 %shard_map.80 = (bf16[2,72,864]{2,1,0:T(8,128)(2,1)S(1)}, bf16[2,72,864]{2,1,0:T(8,128)(2,1)S(1)}, bf16[2,72,864]{2,1,0:T(8,128)(2,1)S(1)}, bf16[2,72,864]{2,1,0...) custom-call(s32[4]{0:T(128)S(1)} %pad_add_fusion.at_ref, ...), custom_call_target="tpu_custom_call" | custom-call | flops 2038431744 | bytes 10485760 | tf_op jit(solution)/shard_map/pallas_call | solution.py:410
  87.6 1.6 shard_map.81
  89.2 5.1 %collective-permute-start.26 = (bf16[2,72,864]{2,1,0:T(8,128)(2,1)S(1)}, bf16[2,72,864]{2,1,0:T(8,128)(2,1)S(1)}, u32[]{:S(2)}, u32[]{:S(2)}) collective-permute-start(bf16[2,72,864]{2,1,0:T(8,128)(2,1)S(1)} %get-tuple-element.39), channel_id=1, source_target_pairs={{0,8},{1,9},{2,10},{3,11},{4,12},{5,13},{6,14},{7,15},{24,16},{25,... | collective-permute-start | bytes 746504 | tf_op jit(solution)/shard_map/ppermute | solution.py:53
  95.0 1.9 %collective-permute-start.29 = (bf16[72,1152]{1,0:T(8,128)(2,1)S(1)}, bf16[72,1152]{1,0:T(8,128)(2,1)S(1)}, u32[]{:S(2)}, u32[]{:S(2)}) collective-permute-start(bf16[72,1152]{1,0:T(8,128)(2,1)S(1)} %get-tuple-element.41), channel_id=1, source_target_pairs={{0,8},{1,11},{4,12},{5,15},{10,16},{11,19},{14,20},{15,23},{18,24}... | collective-permute-start | bytes 497672 | tf_op jit(solution)/shard_map/ppermute | solution.py:53
  98.2 2.7 %collective-permute-done.26 = bf16[2,72,864]{2,1,0:T(8,128)(2,1)S(1)} collective-permute-done((bf16[2,72,864]{2,1,0:T(8,128)(2,1)S(1)}, bf16[2,72,864]{2,1,0:T(8,128)(2,1)S(1)}, u32[]{:S(2)}, u32[]{:S(2)}) %collective-permute-start.26) | collective-permute-done | bytes 248864 | tf_op jit(solution)/shard_map/ppermute | solution.py:53
  102.3 6.5 %collective-permute-start.23 = (bf16[2,72,864]{2,1,0:T(8,128)(2,1)S(1)}, bf16[2,72,864]{2,1,0:T(8,128)(2,1)S(1)}, u32[]{:S(2)}, u32[]{:S(2)}) collective-permute-start(bf16[2,72,864]{2,1,0:T(8,128)(2,1)S(1)} %get-tuple-element.36), channel_id=1, source_target_pairs={{0,16},{1,17},{2,18},{3,19},{4,20},{5,21},{6,22},{7,23},{24,8},{25... | collective-permute-start | bytes 746504 | tf_op jit(solution)/shard_map/ppermute | solution.py:53
  112.7 5.4 %collective-permute-done.24.refs_2_ = bf16[2,72,864]{2,1,0:T(8,128)(2,1)S(1)} collective-permute-done((bf16[2,72,864]{2,1,0:T(8,128)(2,1)S(1)}, bf16[2,72,864]{2,1,0:T(8,128)(2,1)S(1)}, u32[]{:S(2)}, u32[]{:S(2)}) %collective-permute-start.24) | collective-permute-done | bytes 248864 | tf_op jit(solution)/shard_map/ppermute | solution.py:53
  118.3 8.7 %collective-permute-done.27.refs_4_ = bf16[2,72,864]{2,1,0:T(8,128)(2,1)S(1)} collective-permute-done((bf16[2,72,864]{2,1,0:T(8,128)(2,1)S(1)}, bf16[2,72,864]{2,1,0:T(8,128)(2,1)S(1)}, u32[]{:S(2)}, u32[]{:S(2)}) %collective-permute-start.27) | collective-permute-done | bytes 248864 | tf_op jit(solution)/shard_map/ppermute | solution.py:53
  129.7 1.6 collective-permute-start.22
  135.2 11.7 %collective-permute-done.36.refs_5_ = bf16[72,432]{1,0:T(8,128)(2,1)S(1)} collective-permute-done((bf16[72,432]{1,0:T(8,128)(2,1)S(1)}, bf16[72,432]{1,0:T(8,128)(2,1)S(1)}, u32[]{:S(2)}, u32[]{:S(2)}) %collective-permute-start.36) | collective-permute-done | bytes 62240 | tf_op jit(solution)/shard_map/ppermute | solution.py:53
  148.1 3.2 %collective-permute-done.35.refs_4_ = bf16[72,432]{1,0:T(8,128)(2,1)S(1)} collective-permute-done((bf16[72,432]{1,0:T(8,128)(2,1)S(1)}, bf16[72,432]{1,0:T(8,128)(2,1)S(1)}, u32[]{:S(2)}, u32[]{:S(2)}) %collective-permute-start.35) | collective-permute-done | bytes 62240 | tf_op jit(solution)/shard_map/ppermute | solution.py:53
  151.3 4.7 %collective-permute-done.38.refs_7_ = bf16[72,432]{1,0:T(8,128)(2,1)S(1)} collective-permute-done((bf16[72,432]{1,0:T(8,128)(2,1)S(1)}, bf16[72,432]{1,0:T(8,128)(2,1)S(1)}, u32[]{:S(2)}, u32[]{:S(2)}) %collective-permute-start.38) | collective-permute-done | bytes 62240 | tf_op jit(solution)/shard_map/ppermute | solution.py:53
  156.1 4.2 %collective-permute-done.37.refs_6_ = bf16[72,432]{1,0:T(8,128)(2,1)S(1)} collective-permute-done((bf16[72,432]{1,0:T(8,128)(2,1)S(1)}, bf16[72,432]{1,0:T(8,128)(2,1)S(1)}, u32[]{:S(2)}, u32[]{:S(2)}) %collective-permute-start.37) | collective-permute-done | bytes 62240 | tf_op jit(solution)/shard_map/ppermute | solution.py:53
  160.3 2.5 %shard_map.83 = f32[72,4608]{1,0:T(8,128)} custom-call(s32[4]{0:T(128)S(1)} %pad_add_fusion.at_ref, bf16[72,432]{1,0:T(8,128)(2,1)S(1)} %get-tuple-element.44.refs_0_, bf16[72,1584]{1,0:T(8,128)(2,1)S(1)} %collective-permute-done.32.refs_1_, bf16[72,432]{1,0:T(8,128)(2,1)S(1)} %collective-permute-done.33.refs_2_, ...), custom_call_target="tpu_custom_call" | custom-call | tf_op jit(solution)/shard_map/pallas_call | solution.py:483
  (61 shorter events, 27.6 us)
Async XLA Ops:
  0.6 12.1 %collective-permute-start.2 = (bf16[128,1152]{1,0:T(8,128)(2,1)}, bf16[128,1152]{1,0:T(8,128)(2,1)S(1)}, u32[]{:S(2)}, u32[]{:S(2)}) collective-permute-start(bf16[128,1152]{1,0:T(8,128)(2,1)} %bitcast.25), channel_id=1, source_target_pairs={{0,5},{1,4},{2,7},{3,6},{4,1},{5,0},{6,3},{7,2},{8,13},{9,12},{10,... | collective-permute-start | bytes 884744 | tf_op jit(solution)/shard_map/ppermute | solution.py:53
  4.6 14.5 %collective-permute-start.1 = (bf16[128,1152]{1,0:T(8,128)(2,1)}, bf16[128,1152]{1,0:T(8,128)(2,1)S(1)}, u32[]{:S(2)}, u32[]{:S(2)}) collective-permute-start(bf16[128,1152]{1,0:T(8,128)(2,1)} %bitcast.26), channel_id=1, source_target_pairs={{0,1},{1,0},{2,3},{3,2},{4,5},{5,4},{6,7},{7,6},{8,9},{9,8},{10,11... | collective-permute-start | bytes 884744 | tf_op jit(solution)/shard_map/ppermute | solution.py:53
  5.1 14.5 %collective-permute-start = (bf16[128,1152]{1,0:T(8,128)(2,1)}, bf16[128,1152]{1,0:T(8,128)(2,1)S(1)}, u32[]{:S(2)}, u32[]{:S(2)}) collective-permute-start(bf16[128,1152]{1,0:T(8,128)(2,1)} %bitcast.27), channel_id=1, source_target_pairs={{0,4},{1,5},{2,6},{3,7},{4,0},{5,1},{6,2},{7,3},{8,12},{9,13},{10,... | collective-permute-start | bytes 884744 | tf_op jit(solution)/shard_map/ppermute | solution.py:53
  5.3 20.2 %collective-permute-start.6 = (bf16[128,1152]{1,0:T(8,128)(2,1)}, bf16[128,1152]{1,0:T(8,128)(2,1)S(1)}, u32[]{:S(2)}, u32[]{:S(2)}) collective-permute-start(bf16[128,1152]{1,0:T(8,128)(2,1)} %bitcast.29), channel_id=1, source_target_pairs={{0,5},{1,4},{2,7},{3,6},{4,1},{5,0},{6,3},{7,2},{8,13},{9,12},{10,... | collective-permute-start | bytes 884744 | tf_op jit(solution)/shard_map/ppermute | solution.py:53
  8.1 22.7 %collective-permute-start.5 = (bf16[128,1152]{1,0:T(8,128)(2,1)}, bf16[128,1152]{1,0:T(8,128)(2,1)S(1)}, u32[]{:S(2)}, u32[]{:S(2)}) collective-permute-start(bf16[128,1152]{1,0:T(8,128)(2,1)} %bitcast.30), channel_id=1, source_target_pairs={{0,1},{1,0},{2,3},{3,2},{4,5},{5,4},{6,7},{7,6},{8,9},{9,8},{10,11... | collective-permute-start | bytes 884744 | tf_op jit(solution)/shard_map/ppermute | solution.py:53
  12.7 18.4 %collective-permute-start.4 = (bf16[128,1152]{1,0:T(8,128)(2,1)}, bf16[128,1152]{1,0:T(8,128)(2,1)S(1)}, u32[]{:S(2)}, u32[]{:S(2)}) collective-permute-start(bf16[128,1152]{1,0:T(8,128)(2,1)} %bitcast.31), channel_id=1, source_target_pairs={{0,4},{1,5},{2,6},{3,7},{4,0},{5,1},{6,2},{7,3},{8,12},{9,13},{10,... | collective-permute-start | bytes 884744 | tf_op jit(solution)/shard_map/ppermute | solution.py:53
  20.8 51.0 %collective-permute-start.3 = (bf16[4,128,1152]{2,1,0:T(8,128)(2,1)S(1)}, bf16[4,128,1152]{2,1,0:T(8,128)(2,1)S(1)}, u32[]{:S(2)}, u32[]{:S(2)}) collective-permute-start(bf16[4,128,1152]{2,1,0:T(8,128)(2,1)S(1)} %pad_maximum_fusion.refs_0_), channel_id=1, source_target_pairs={{0,2},{1,3},{2,0},{3,1},{4,6},{5,7},{6,4},{7,5},{8,10},{9,11},{10,... | collective-permute-start | bytes 3538952 | tf_op jit(solution)/shard_map/ppermute | solution.py:53
  31.3 45.4 %collective-permute-start.7 = (bf16[4,128,1152]{2,1,0:T(8,128)(2,1)S(1)}, bf16[4,128,1152]{2,1,0:T(8,128)(2,1)}, u32[]{:S(2)}, u32[]{:S(2)}) collective-permute-start(bf16[4,128,1152]{2,1,0:T(8,128)(2,1)S(1)} %pad_maximum_fusion.1.refs_2_), channel_id=1, source_target_pairs={{0,2},{1,3},{2,0},{3,1},{4,6},{5,7},{6,4},{7,5},{8,10},{9,11},{10,... | collective-permute-start | bytes 3538952 | tf_op jit(solution)/shard_map/ppermute | solution.py:53
  41.6 15.6 %collective-permute-start.12 = (bf16[2,72,864]{2,1,0:T(8,128)(2,1)S(1)}, bf16[2,72,864]{2,1,0:T(8,128)(2,1)S(1)}, u32[]{:S(2)}, u32[]{:S(2)}) collective-permute-start(bf16[2,72,864]{2,1,0:T(8,128)(2,1)S(1)} %shard_map.78.refs_2_), channel_id=1, source_target_pairs={{0,16},{1,17},{2,18},{3,19},{4,20},{5,21},{6,22},{7,23},{8,24},{9,... | collective-permute-start | bytes 746504 | tf_op jit(solution)/shard_map/ppermute | solution.py:53
  44.2 14.3 %collective-permute-start.13 = (bf16[2,72,864]{2,1,0:T(8,128)(2,1)S(1)}, bf16[2,72,864]{2,1,0:T(8,128)(2,1)S(1)}, u32[]{:S(2)}, u32[]{:S(2)}) collective-permute-start(bf16[2,72,864]{2,1,0:T(8,128)(2,1)S(1)} %shard_map.78.refs_2_), channel_id=1, source_target_pairs={{8,0},{9,1},{10,2},{11,3},{12,4},{13,5},{14,6},{15,7},{16,8},{17,9... | collective-permute-start | bytes 746504 | tf_op jit(solution)/shard_map/ppermute | solution.py:53
  45.5 18.8 %collective-permute-start.11 = (bf16[2,72,864]{2,1,0:T(8,128)(2,1)S(1)}, bf16[2,72,864]{2,1,0:T(8,128)(2,1)S(1)}, u32[]{:S(2)}, u32[]{:S(2)}) collective-permute-start(bf16[2,72,864]{2,1,0:T(8,128)(2,1)S(1)} %shard_map.78.refs_2_), channel_id=1, source_target_pairs={{0,8},{1,9},{2,10},{3,11},{4,12},{5,13},{6,14},{7,15},{8,16},{9,17... | collective-permute-start | bytes 746504 | tf_op jit(solution)/shard_map/ppermute | solution.py:53
  57.2 10.1 %collective-permute-start.14 = (bf16[2,72,864]{2,1,0:T(8,128)(2,1)S(1)}, bf16[2,72,864]{2,1,0:T(8,128)(2,1)S(1)}, u32[]{:S(2)}, u32[]{:S(2)}) collective-permute-start(bf16[2,72,864]{2,1,0:T(8,128)(2,1)S(1)} %collective-permute-done.12.refs_4_), channel_id=1, source_target_pairs={{8,0},{9,1},{10,2},{11,3},{12,4},{13,5},{14,6},{15,7},{16,24},{17,... | collective-permute-start | bytes 746504 | tf_op jit(solution)/shard_map/ppermute | solution.py:53
  58.5 17.1 %collective-permute-start.16 = (bf16[72,1152]{1,0:T(8,128)(2,1)}, bf16[72,1152]{1,0:T(8,128)(2,1)S(1)}, u32[]{:S(2)}, u32[]{:S(2)}) collective-permute-start(bf16[72,1152]{1,0:T(8,128)(2,1)} %param.11), channel_id=1, source_target_pairs={{0,8},{3,9},{4,12},{7,13},{8,16},{11,17},{12,20},{15,21},{16,26},{... | collective-permute-start | bytes 497672 | tf_op jit(solution)/shard_map/ppermute | solution.py:53
  64.3 11.2 %collective-permute-start.15 = (bf16[72,1152]{1,0:T(8,128)(2,1)}, bf16[72,1152]{1,0:T(8,128)(2,1)S(1)}, u32[]{:S(2)}, u32[]{:S(2)}) collective-permute-start(bf16[72,1152]{1,0:T(8,128)(2,1)} %param.11), channel_id=1, source_target_pairs={{0,0},{3,1},{4,4},{7,5},{8,8},{11,9},{12,12},{15,13},{16,18},{19,1... | collective-permute-start | bytes 497672 | tf_op jit(solution)/shard_map/ppermute | solution.py:53
  67.3 9.1 %collective-permute-start.18 = (bf16[72,1152]{1,0:T(8,128)(2,1)}, bf16[72,1152]{1,0:T(8,128)(2,1)S(1)}, u32[]{:S(2)}, u32[]{:S(2)}) collective-permute-start(bf16[72,1152]{1,0:T(8,128)(2,1)} %param.11), channel_id=1, source_target_pairs={{0,24},{3,25},{4,28},{7,29},{8,0},{11,1},{12,4},{15,5},{16,10},{19... | collective-permute-start | bytes 497672 | tf_op jit(solution)/shard_map/ppermute | solution.py:53
  71.7 5.0 %collective-permute-start.17 = (bf16[72,1152]{1,0:T(8,128)(2,1)}, bf16[72,1152]{1,0:T(8,128)(2,1)S(1)}, u32[]{:S(2)}, u32[]{:S(2)}) collective-permute-start(bf16[72,1152]{1,0:T(8,128)(2,1)} %param.11), channel_id=1, source_target_pairs={{0,16},{3,17},{4,20},{7,21},{8,24},{11,25},{12,28},{15,29},{16,2},... | collective-permute-start | bytes 497672 | tf_op jit(solution)/shard_map/ppermute | solution.py:53
  89.1 39.3 %collective-permute-start.19 = (bf16[4,128,1152]{2,1,0:T(8,128)(2,1)S(1)}, bf16[4,128,1152]{2,1,0:T(8,128)(2,1)S(1)}, u32[]{:S(2)}, u32[]{:S(2)}) collective-permute-start(bf16[4,128,1152]{2,1,0:T(8,128)(2,1)S(1)} %get-tuple-element.34), channel_id=1, source_target_pairs={{0,2},{1,3},{2,0},{3,1},{4,6},{5,7},{6,4},{7,5},{8,10},{9,11},{10,... | collective-permute-start | bytes 3538952 | tf_op jit(solution)/shard_map/ppermute | solution.py:53
  89.2 11.7 %collective-permute-start.26 = (bf16[2,72,864]{2,1,0:T(8,128)(2,1)S(1)}, bf16[2,72,864]{2,1,0:T(8,128)(2,1)S(1)}, u32[]{:S(2)}, u32[]{:S(2)}) collective-permute-start(bf16[2,72,864]{2,1,0:T(8,128)(2,1)S(1)} %get-tuple-element.39), channel_id=1, source_target_pairs={{0,8},{1,9},{2,10},{3,11},{4,12},{5,13},{6,14},{7,15},{24,16},{25,... | collective-permute-start | bytes 746504 | tf_op jit(solution)/shard_map/ppermute | solution.py:53
  94.3 7.9 %collective-permute-start.28 = (bf16[72,1152]{1,0:T(8,128)(2,1)S(1)}, bf16[72,1152]{1,0:T(8,128)(2,1)S(1)}, u32[]{:S(2)}, u32[]{:S(2)}) collective-permute-start(bf16[72,1152]{1,0:T(8,128)(2,1)S(1)} %get-tuple-element.40), channel_id=1, source_target_pairs={{0,0},{1,3},{4,4},{5,7},{8,8},{9,11},{12,12},{13,15},{18,16},{19,1... | collective-permute-start | bytes 497672 | tf_op jit(solution)/shard_map/ppermute | solution.py:53
  95.0 13.8 %collective-permute-start.29 = (bf16[72,1152]{1,0:T(8,128)(2,1)S(1)}, bf16[72,1152]{1,0:T(8,128)(2,1)S(1)}, u32[]{:S(2)}, u32[]{:S(2)}) collective-permute-start(bf16[72,1152]{1,0:T(8,128)(2,1)S(1)} %get-tuple-element.41), channel_id=1, source_target_pairs={{0,8},{1,11},{4,12},{5,15},{10,16},{11,19},{14,20},{15,23},{18,24}... | collective-permute-start | bytes 497672 | tf_op jit(solution)/shard_map/ppermute | solution.py:53
  96.9 13.2 %collective-permute-start.30 = (bf16[72,1152]{1,0:T(8,128)(2,1)S(1)}, bf16[72,1152]{1,0:T(8,128)(2,1)S(1)}, u32[]{:S(2)}, u32[]{:S(2)}) collective-permute-start(bf16[72,1152]{1,0:T(8,128)(2,1)S(1)} %get-tuple-element.42), channel_id=1, source_target_pairs={{2,16},{3,19},{6,20},{7,23},{10,24},{11,27},{14,28},{15,31},{16,0}... | collective-permute-start | bytes 497672 | tf_op jit(solution)/shard_map/ppermute | solution.py:53
  100.9 10.5 %collective-permute-start.31 = (bf16[72,1152]{1,0:T(8,128)(2,1)S(1)}, bf16[72,1152]{1,0:T(8,128)(2,1)S(1)}, u32[]{:S(2)}, u32[]{:S(2)}) collective-permute-start(bf16[72,1152]{1,0:T(8,128)(2,1)S(1)} %get-tuple-element.43), channel_id=1, source_target_pairs={{2,24},{3,27},{6,28},{7,31},{8,0},{9,3},{12,4},{13,7},{16,8},{17,1... | collective-permute-start | bytes 497672 | tf_op jit(solution)/shard_map/ppermute | solution.py:53
  102.3 16.0 %collective-permute-start.23 = (bf16[2,72,864]{2,1,0:T(8,128)(2,1)S(1)}, bf16[2,72,864]{2,1,0:T(8,128)(2,1)S(1)}, u32[]{:S(2)}, u32[]{:S(2)}) collective-permute-start(bf16[2,72,864]{2,1,0:T(8,128)(2,1)S(1)} %get-tuple-element.36), channel_id=1, source_target_pairs={{0,16},{1,17},{2,18},{3,19},{4,20},{5,21},{6,22},{7,23},{24,8},{25... | collective-permute-start | bytes 746504 | tf_op jit(solution)/shard_map/ppermute | solution.py:53
  108.8 9.3 %collective-permute-start.24 = (bf16[2,72,864]{2,1,0:T(8,128)(2,1)S(1)}, bf16[2,72,864]{2,1,0:T(8,128)(2,1)S(1)}, u32[]{:S(2)}, u32[]{:S(2)}) collective-permute-start(bf16[2,72,864]{2,1,0:T(8,128)(2,1)S(1)} %get-tuple-element.37), channel_id=1, source_target_pairs={{0,8},{1,9},{2,10},{3,11},{4,12},{5,13},{6,14},{7,15},{8,16},{9,17... | collective-permute-start | bytes 746504 | tf_op jit(solution)/shard_map/ppermute | solution.py:53
  110.1 8.2 %collective-permute-start.25 = (bf16[2,72,864]{2,1,0:T(8,128)(2,1)S(1)}, bf16[2,72,864]{2,1,0:T(8,128)(2,1)S(1)}, u32[]{:S(2)}, u32[]{:S(2)}) collective-permute-start(bf16[2,72,864]{2,1,0:T(8,128)(2,1)S(1)} %get-tuple-element.38), channel_id=1, source_target_pairs={{8,0},{9,1},{10,2},{11,3},{12,4},{13,5},{14,6},{15,7},{16,8},{17,9... | collective-permute-start | bytes 746504 | tf_op jit(solution)/shard_map/ppermute | solution.py:53
  111.4 15.6 %collective-permute-start.27 = (bf16[2,72,864]{2,1,0:T(8,128)(2,1)S(1)}, bf16[2,72,864]{2,1,0:T(8,128)(2,1)S(1)}, u32[]{:S(2)}, u32[]{:S(2)}) collective-permute-start(bf16[2,72,864]{2,1,0:T(8,128)(2,1)S(1)} %add_convert_fusion.3), channel_id=1, source_target_pairs={{8,24},{9,25},{10,26},{11,27},{12,28},{13,29},{14,30},{15,31},{16,... | collective-permute-start | bytes 746504 | tf_op jit(solution)/shard_map/ppermute | solution.py:53
  128.6 34.2 %collective-permute-start.20 = (bf16[128,1152]{1,0:T(8,128)(2,1)S(1)}, bf16[128,1152]{1,0:T(8,128)(2,1)S(1)}, u32[]{:S(2)}, u32[]{:S(2)}) collective-permute-start(bf16[128,1152]{1,0:T(8,128)(2,1)S(1)} %get-tuple-element.50), channel_id=1, source_target_pairs={{0,4},{1,5},{2,6},{3,7},{4,0},{5,1},{6,2},{7,3},{8,12},{9,13},{10,... | collective-permute-start | bytes 884744 | tf_op jit(solution)/shard_map/ppermute | solution.py:53
  129.7 33.1 %collective-permute-start.22 = (bf16[128,1152]{1,0:T(8,128)(2,1)S(1)}, bf16[128,1152]{1,0:T(8,128)(2,1)S(1)}, u32[]{:S(2)}, u32[]{:S(2)}) collective-permute-start(bf16[128,1152]{1,0:T(8,128)(2,1)S(1)} %get-tuple-element.51), channel_id=1, source_target_pairs={{0,5},{1,4},{2,7},{3,6},{4,1},{5,0},{6,3},{7,2},{8,13},{9,12},{10,... | collective-permute-start | bytes 884744 | tf_op jit(solution)/shard_map/ppermute | solution.py:53
  131.2 31.6 %collective-permute-start.21 = (bf16[128,1152]{1,0:T(8,128)(2,1)S(1)}, bf16[128,1152]{1,0:T(8,128)(2,1)S(1)}, u32[]{:S(2)}, u32[]{:S(2)}) collective-permute-start(bf16[128,1152]{1,0:T(8,128)(2,1)S(1)} %get-tuple-element.52), channel_id=1, source_target_pairs={{0,1},{1,0},{2,3},{3,2},{4,5},{5,4},{6,7},{7,6},{8,9},{9,8},{10,11... | collective-permute-start | bytes 884744 | tf_op jit(solution)/shard_map/ppermute | solution.py:53
  132.6 14.3 %collective-permute-start.36 = (bf16[72,432]{1,0:T(8,128)(2,1)S(1)}, bf16[72,432]{1,0:T(8,128)(2,1)S(1)}, u32[]{:S(2)}, u32[]{:S(2)}) collective-permute-start(bf16[72,432]{1,0:T(8,128)(2,1)S(1)} %get-tuple-element.47), channel_id=1, source_target_pairs={{0,5},{1,4},{2,7},{3,6},{4,1},{5,0},{6,3},{7,2},{8,13},{9,12},{10,... | collective-permute-start | bytes 186632 | tf_op jit(solution)/shard_map/ppermute | solution.py:53
  134.0 26.3 %collective-permute-start.32 = (bf16[72,1584]{1,0:T(8,128)(2,1)S(1)}, bf16[72,1584]{1,0:T(8,128)(2,1)S(1)}, u32[]{:S(2)}, u32[]{:S(2)}) collective-permute-start(bf16[72,1584]{1,0:T(8,128)(2,1)S(1)} %get-tuple-element.45), channel_id=1, source_target_pairs={{0,1},{1,0},{2,3},{3,2},{4,5},{5,4},{6,7},{7,6},{8,9},{9,8},{10,11... | collective-permute-start | bytes 684296 | tf_op jit(solution)/shard_map/ppermute | solution.py:53
  151.3 4.7 %collective-permute-start.38 = (bf16[72,432]{1,0:T(8,128)(2,1)S(1)}, bf16[72,432]{1,0:T(8,128)(2,1)S(1)}, u32[]{:S(2)}, u32[]{:S(2)}) collective-permute-start(bf16[72,432]{1,0:T(8,128)(2,1)S(1)} %get-tuple-element.48), channel_id=1, source_target_pairs={{0,7},{1,6},{2,5},{3,4},{4,3},{5,2},{6,1},{7,0},{8,15},{9,14},{10,... | collective-permute-start | bytes 186632 | tf_op jit(solution)/shard_map/ppermute | solution.py:53
  (8 other events, 37.4 us)

commit v5 on v4

--- a/solution.py
+++ b/solution.py
@@ -143,11 +143,11 @@
                 out_ref[index // 2, :, side * wide : (side + 1) * wide] = piece[...]
 
 
-def sum_kernel(terms, at_ref, *refs):
-    parts, heads, outs = refs[:terms], refs[terms : len(refs) - 6], refs[len(refs) - 6 :]
+def sum_kernel(at_ref, *refs):
+    parts, outs = refs[: len(refs) - 4], refs[len(refs) - 4 :]
     here = 2 * at_ref[1] + at_ref[2]
     wide = outs[0].shape[1]
-    for n, out in enumerate(outs[:4]):
+    for n, out in enumerate(outs):
         index = here ^ n
         for side in range(2):
 
@@ -156,12 +156,6 @@
                 cut = slice(side * wide, (side + 1) * wide)
                 total = sum(p[index // 2, :, cut].astype(jnp.float32) for p in parts)
                 out[...] = total.astype(jnp.bfloat16)
-
-    kept, other = outs[4:]
-    kept[...] = sum(h[...].astype(jnp.float32) for h in heads).astype(kept.dtype)
-    width = kept.shape[1]
-    other[:, :width] = kept[...]
-    other[:, width:] = outs[0][...]
 
 
 def attend(query, keyed, valued, dattn, scale, bias):
@@ -214,14 +208,11 @@
 
 
 def attention_kernel(scale, lines, owed, at_ref, *refs):
-    xs, xc, ds, dc, qkv_ref = refs[:5]
-    sent = lines + (lines == 4)
-    out_ws, grads_in = refs[5 : 5 + owed], refs[5 + owed : 5 + owed + sent]
-    grads_out = refs[5 + owed + sent : 5 + 2 * owed + sent]
-    dqkv_ref, loose, out_w, att, grads, bias = refs[5 + 2 * owed + sent :]
-    shard, wide = loose.shape[1:]
-    dim = wide // (3 * KEPT)
-    width = xs.shape[-1]
+    ds, dc, qkv_ref = refs[:3]
+    out_ws, grads_out = refs[3 : 3 + owed], refs[3 + owed : 3 + 2 * owed]
+    dqkv_ref, out_w, att, bias = refs[3 + 2 * owed :]
+    dim = out_w.shape[0] // KEPT
+    width = ds.shape[-1]
     if owed == 1:
         out_w[...] = out_ws[0][...]
     else:
@@ -235,8 +226,8 @@
 
     site = lambda axis: lax.broadcasted_iota(jnp.int32, (BLOCK, BLOCK), axis) // FRAMES
     bias[...] = jnp.where(site(0) == site(1), 0.0, -1e30)
-    half = xs.shape[0] * xs.shape[1]
-    each = BLOCK // xs.shape[1]
+    half = ds.shape[0] * ds.shape[1]
+    each = BLOCK // ds.shape[1]
     for part, d_ref in enumerate((ds, dc)):
 
         def block(j, _, part=part, d_ref=d_ref):
@@ -274,12 +265,25 @@
         for s in range(owed if owed > 1 else 0):
             upper = lax.rem(at_ref[0] + s, lines) != KEPT * at_ref[2]
             grads_out[s][:, pl.ds(at, 128)] = jnp.where(upper, term[dim:], term[:dim])
+        return 0
+
+    lax.fori_loop(0, width // 128, columns, 0, unroll=True)
+
+
+def weight_kernel(at_ref, xs, xc, dqkv_ref, *refs):
+    grads_in, (loose, grads) = refs[:-2], refs[-2:]
+    lines = loose.shape[0] // 4
+    shard, wide = loose.shape[1:]
+    half = xs.shape[0] * xs.shape[1]
+
+    def columns(m, _):
+        at = pl.multiple_of(m * 128, 128)
         first = matmul(xs[:, :, pl.ds(at, 128)].reshape(half, 128), dqkv_ref[:half, :], ((0,), (0,)))
         second = matmul(xc[:, :, pl.ds(at, 128)].reshape(half, 128), dqkv_ref[half:, :], ((0,), (0,)))
         grads[pl.ds(at, 128), :] = first + second
         return 0
 
-    lax.fori_loop(0, width // 128, columns, 0, unroll=True)
+    lax.fori_loop(0, xs.shape[-1] // 128, columns, 0, unroll=True)
     for p in range(4 * lines):
         loose[p] = grads[p * shard : (p + 1) * shard, :].astype(jnp.bfloat16)
     for s, out in enumerate(grads_in):
@@ -305,7 +309,7 @@
 
 
 def spread_kernel(dim, at_ref, *refs):
-    *pieces, kept_ref, out_ref, table = refs
+    *pieces, kept_ref, moved_ref, out_ref, table = refs
     step = pl.program_id(0)
 
     @pl.when(step == 0)
@@ -315,9 +319,8 @@
             b = lax.rem(at_ref[1] + db, 2)
             c = lax.rem(at_ref[2] + dc, 2)
             y = lax.rem(at_ref[3] + dy, 2)
-            table[4 * b + 2 * c + y] = piece[:, piece.shape[1] - table.shape[2] :]
-        moved = pieces[1][:, : out_ref.shape[1]].astype(jnp.float32)
-        out_ref[...] = kept_ref[...].astype(jnp.float32) + moved
+            table[4 * b + 2 * c + y] = piece[...]
+        out_ref[...] = kept_ref[...].astype(jnp.float32) + moved_ref[...].astype(jnp.float32)
 
     for w in range(3):
 
@@ -407,27 +410,37 @@
         ),
     )
     qkv, full = project(at, xs, xc, *planes)
-    *results, dqkv = pl.pallas_call(
+    *grads_out, dqkv = pl.pallas_call(
         functools.partial(attention_kernel, scale, lines, owed),
-        compiler_params=room(28),
-        out_shape=(shape_of(2, shard, 6 * wide),) * sent
-        + (shape_of(head_rows, width),) * owed
-        + (shape_of(total, 3 * wide),),
-        in_specs=[SMEM] + [VMEM] * (5 + owed),
-        out_specs=(VMEM,) * (sent + owed + 1),
+        compiler_params=room(24),
+        out_shape=(shape_of(head_rows, width),) * owed + (shape_of(total, 3 * wide),),
+        in_specs=[SMEM] + [VMEM] * (3 + owed),
+        out_specs=(VMEM,) * (owed + 1),
         scratch_shapes=[
-            pltpu.VMEM((pix, shard, 3 * wide), jnp.bfloat16),
             pltpu.VMEM((wide, width), jnp.bfloat16),
             pltpu.VMEM((total, wide), jnp.bfloat16),
-            pltpu.VMEM((width, 3 * wide), jnp.float32),
             pltpu.VMEM((BLOCK, BLOCK), jnp.float32),
         ],
         cost_estimate=pl.CostEstimate(
-            flops=12 * total * width * wide, bytes_accessed=10 << 20, transcendentals=total * 512
+            flops=6 * total * width * wide, bytes_accessed=6 << 20, transcendentals=total * 512
         ),
-    )(at, xs, xc, ds, dc, qkv, *out_ws)
-
-    grads_in, grads_out = results[:sent], results[sent:]
+    )(at, ds, dc, qkv, *out_ws)
+    weigh = pl.pallas_call(
+        weight_kernel,
+        compiler_params=room(20),
+        out_shape=(shape_of(2, shard, 6 * wide),) * sent,
+        in_specs=[SMEM] + [VMEM] * 3,
+        out_specs=(VMEM,) * sent,
+        scratch_shapes=[
+            pltpu.VMEM((pix, shard, 3 * wide), jnp.bfloat16),
+            pltpu.VMEM((width, 3 * wide), jnp.float32),
+        ],
+        cost_estimate=pl.CostEstimate(
+            flops=6 * total * width * wide, bytes_accessed=5 << 20, transcendentals=0
+        ),
+    )
+    grads_in = weigh(at, xs, xc, dqkv)
+
     parts = grid.scatter_lines(grads_in)
     if one_head:
         heads = [
@@ -447,17 +460,21 @@
             (c, 0, b, y, 0, 0),
         ).reshape(width, width)
         heads = [lax.psum_scatter(whole, "pix", scatter_dimension=0, tiled=True)]
-    *summed, kept, other = pl.pallas_call(
-        functools.partial(sum_kernel, len(parts)),
-        compiler_params=room(10),
-        out_shape=(shape_of(shard, 3 * wide),) * 4
-        + (shape_of(shard, width), shape_of(shard, width + 3 * wide)),
-        in_specs=[SMEM] + [VMEM] * (len(parts) + len(heads)),
-        out_specs=(VMEM,) * 6,
-    )(at, *parts, *heads)
+    kept = sum(head.astype(jnp.float32) for head in heads).astype(jnp.bfloat16)
+    if one_head:
+        moved = grid.send(kept, lambda a, b, c, g, y: (a, b, c, g, y ^ 1) if c == y else None)
+    else:
+        moved = grid.flip(kept, 0, 0, 1)
+    summed = pl.pallas_call(
+        sum_kernel,
+        compiler_params=room(8),
+        out_shape=(shape_of(shard, 3 * wide),) * 4,
+        in_specs=[SMEM] + [VMEM] * len(parts),
+        out_specs=(VMEM,) * 4,
+    )(at, *parts)
     square = []
     for n in range(8):
-        block = other if n == 1 else summed[n // 2]
+        block = summed[n // 2]
         square.append(grid.flip(block, n // 4, (n // 2) % 2, n % 2) if n else block)
 
     input_call = pl.pallas_call(
@@ -485,10 +502,10 @@
         compiler_params=room(12),
         out_shape=shape_of(shard, 4 * width, dtype=jnp.float32),
         grid=(4,),
-        in_specs=[SMEM] + [VMEM] * 9,
+        in_specs=[SMEM] + [VMEM] * 10,
         out_specs=pl.BlockSpec((shard, width), lambda i: (0, (i + 3) % 4)),
         scratch_shapes=[pltpu.VMEM((8, shard, 3 * wide), jnp.bfloat16)],
-    )(at, *square, kept)
+    )(at, *square, kept, moved)
     if grid.groups > 1:
         same = [[2 * g + y for g in range(grid.groups)] for y in range(2)]
         grads = lax.psum(grads, "rep", axis_index_groups=same)

time: 164 us -> 159 us (0.970); the launches traced: 164 us -> 156 us
  waiting for transfers between devices: 74.7 us -> 53 us
  starting transfers between devices: 63.4 us -> 75.9 us
    ppermute x39 -> x40, waiting for transfers between devices: 74.7 us -> 53 us  [send(): return lax.ppermute(value, BOTH, pairs)]
    ppermute x39 -> x40, starting transfers between devices: 63.4 us -> 75.9 us  [send(): return lax.ppermute(value, BOTH, pairs)]
    pallas_call x1 -> x2, Pallas kernels: 1.1 us -> 3.98 us  [the longest x1 3.03 us: local(): grads_in = weigh(at, xs, xc, dqkv)]
    pallas_call x1, Pallas kernels: 10.8 us -> 8.43 us  [local(): pl.pallas_call(functools.partial(attention_kernel, scale, lines, owed), c...]
  transfers between devices with their start and end apart: 39 -> 40, of which waited for: 21 -> 20; matrix products, arithmetic and copies ran while one was open for 1% -> 1% of each run, Pallas kernels for 6% -> 9%
where the time goes in v5:
time: 159 us; the launch traced here: 156 us
  starting transfers between devices  75.9 us (48%)
  waiting for transfers between devices  53 us (33%)
  Pallas kernels  23.2 us (15%)
  other arithmetic  2.7 us (2%)
    ppermute x40, starting transfers between devices, send(): return lax.ppermute(value, BOTH, pairs)  75.9 us
    ppermute x40, waiting for transfers between devices, send(): return lax.ppermute(value, BOTH, pairs)  53 us
    pallas_call x1, Pallas kernels, local(): pl.pallas_call(functools.partial(attention_kernel, scale, lines, owed), c...  8.43 us
    pallas_call x1, Pallas kernels, local(): qkv, full = project(at, xs, xc, *planes)  3.23 us
  transfers between devices with their start and end apart: 40, of which 20 were waited for; matrix products, arithmetic and copies ran while one was open for 1% of the time, Pallas kernels for 9%

profile of v5, /device:TPU:0, one launch (start us, length us, event | category | flops | bytes accessed | tf_op | source)
XLA Modules:
  0.0 155.9 jit_solution(1377061025366724485)
XLA Ops:
  0.6 4.0 %collective-permute-start.6 = (bf16[128,1152]{1,0:T(8,128)(2,1)}, bf16[128,1152]{1,0:T(8,128)(2,1)S(1)}, u32[]{:S(2)}, u32[]{:S(2)}) collective-permute-start(bf16[128,1152]{1,0:T(8,128)(2,1)} %bitcast.25), channel_id=1, source_target_pairs={{0,5},{1,4},{2,7},{3,6},{4,1},{5,0},{6,3},{7,2},{8,13},{9,12},{10,... | collective-permute-start | bytes 884744 | tf_op jit(solution)/shard_map/ppermute | solution.py:53
  5.3 2.8 %collective-permute-start.2 = (bf16[128,1152]{1,0:T(8,128)(2,1)}, bf16[128,1152]{1,0:T(8,128)(2,1)S(1)}, u32[]{:S(2)}, u32[]{:S(2)}) collective-permute-start(bf16[128,1152]{1,0:T(8,128)(2,1)} %bitcast.29), channel_id=1, source_target_pairs={{0,5},{1,4},{2,7},{3,6},{4,1},{5,0},{6,3},{7,2},{8,13},{9,12},{10,... | collective-permute-start | bytes 884744 | tf_op jit(solution)/shard_map/ppermute | solution.py:53
  8.6 4.1 %collective-permute-done.6 = bf16[128,1152]{1,0:T(8,128)(2,1)S(1)} collective-permute-done((bf16[128,1152]{1,0:T(8,128)(2,1)}, bf16[128,1152]{1,0:T(8,128)(2,1)S(1)}, u32[]{:S(2)}, u32[]{:S(2)}) %collective-permute-start.6) | collective-permute-done | bytes 294944 | tf_op jit(solution)/shard_map/ppermute | solution.py:53
  12.7 2.0 %collective-permute-start = (bf16[128,1152]{1,0:T(8,128)(2,1)}, bf16[128,1152]{1,0:T(8,128)(2,1)S(1)}, u32[]{:S(2)}, u32[]{:S(2)}) collective-permute-start(bf16[128,1152]{1,0:T(8,128)(2,1)} %bitcast.31), channel_id=1, source_target_pairs={{0,4},{1,5},{2,6},{3,7},{4,0},{5,1},{6,2},{7,3},{8,12},{9,13},{10,... | collective-permute-start | bytes 884744 | tf_op jit(solution)/shard_map/ppermute | solution.py:53
  14.7 4.4 %collective-permute-done.5 = bf16[128,1152]{1,0:T(8,128)(2,1)S(1)} collective-permute-done((bf16[128,1152]{1,0:T(8,128)(2,1)}, bf16[128,1152]{1,0:T(8,128)(2,1)S(1)}, u32[]{:S(2)}, u32[]{:S(2)}) %collective-permute-start.5) | collective-permute-done | bytes 294944 | tf_op jit(solution)/shard_map/ppermute | solution.py:53
  20.8 4.6 %collective-permute-done.2 = bf16[128,1152]{1,0:T(8,128)(2,1)S(1)} collective-permute-done((bf16[128,1152]{1,0:T(8,128)(2,1)}, bf16[128,1152]{1,0:T(8,128)(2,1)S(1)}, u32[]{:S(2)}, u32[]{:S(2)}) %collective-permute-start.2) | collective-permute-done | bytes 294944 | tf_op jit(solution)/shard_map/ppermute | solution.py:53
  25.4 5.4 %collective-permute-done.1 = bf16[128,1152]{1,0:T(8,128)(2,1)S(1)} collective-permute-done((bf16[128,1152]{1,0:T(8,128)(2,1)}, bf16[128,1152]{1,0:T(8,128)(2,1)S(1)}, u32[]{:S(2)}, u32[]{:S(2)}) %collective-permute-start.1) | collective-permute-done | bytes 294944 | tf_op jit(solution)/shard_map/ppermute | solution.py:53
  31.5 2.7 %shard_map.77 = (bf16[72,432]{1,0:T(8,128)(2,1)S(1)}, bf16[72,432]{1,0:T(8,128)(2,1)S(1)}, bf16[72,432]{1,0:T(8,128)(2,1)S(1)}, bf16[72,432]{1,0:T(8,128)(2,1)S(1)}) custom-call(s32[4]{0:T(128)S(1)} %pad_add_fusion.at_ref, bf16[72,1152]{1,0:T(8,128)(2,1)} %refs_0_.1, bf16[72,1152]{1,0:T(8,128)(2,1)} %refs_1_.1, bf16[72,1152]{1,0:T(8,128)(2,1)} %refs_2_.1), custom_call_target="tpu_custom_call" | custom-call | tf_op jit(solution)/shard_map/pallas_call | solution.py:358
  36.2 2.9 %collective-permute-done.9.refs_2_ = bf16[72,432]{1,0:T(8,128)(2,1)S(1)} collective-permute-done((bf16[72,432]{1,0:T(8,128)(2,1)S(1)}, bf16[72,432]{1,0:T(8,128)(2,1)S(1)}, u32[]{:S(2)}, u32[]{:S(2)}) %collective-permute-start.9) | collective-permute-done | bytes 62240 | tf_op jit(solution)/shard_map/ppermute | solution.py:53
  39.1 1.7 %collective-permute-done.10.refs_3_ = bf16[72,432]{1,0:T(8,128)(2,1)S(1)} collective-permute-done((bf16[72,432]{1,0:T(8,128)(2,1)S(1)}, bf16[72,432]{1,0:T(8,128)(2,1)S(1)}, u32[]{:S(2)}, u32[]{:S(2)}) %collective-permute-start.10) | collective-permute-done | bytes 62240 | tf_op jit(solution)/shard_map/ppermute | solution.py:53
  41.6 2.7 %collective-permute-start.12 = (bf16[2,72,864]{2,1,0:T(8,128)(2,1)S(1)}, bf16[2,72,864]{2,1,0:T(8,128)(2,1)S(1)}, u32[]{:S(2)}, u32[]{:S(2)}) collective-permute-start(bf16[2,72,864]{2,1,0:T(8,128)(2,1)S(1)} %shard_map.78.refs_2_), channel_id=1, source_target_pairs={{0,16},{1,17},{2,18},{3,19},{4,20},{5,21},{6,22},{7,23},{8,24},{9,... | collective-permute-start | bytes 746504 | tf_op jit(solution)/shard_map/ppermute | solution.py:53
  45.5 4.6 %collective-permute-start.11 = (bf16[2,72,864]{2,1,0:T(8,128)(2,1)S(1)}, bf16[2,72,864]{2,1,0:T(8,128)(2,1)S(1)}, u32[]{:S(2)}, u32[]{:S(2)}) collective-permute-start(bf16[2,72,864]{2,1,0:T(8,128)(2,1)S(1)} %shard_map.78.refs_2_), channel_id=1, source_target_pairs={{0,8},{1,9},{2,10},{3,11},{4,12},{5,13},{6,14},{7,15},{8,16},{9,17... | collective-permute-start | bytes 746504 | tf_op jit(solution)/shard_map/ppermute | solution.py:53
  50.1 7.1 %collective-permute-done.12.refs_4_ = bf16[2,72,864]{2,1,0:T(8,128)(2,1)S(1)} collective-permute-done((bf16[2,72,864]{2,1,0:T(8,128)(2,1)S(1)}, bf16[2,72,864]{2,1,0:T(8,128)(2,1)S(1)}, u32[]{:S(2)}, u32[]{:S(2)}) %collective-permute-start.12) | collective-permute-done | bytes 248864 | tf_op jit(solution)/shard_map/ppermute | solution.py:53
  58.5 5.8 %collective-permute-start.16 = (bf16[72,1152]{1,0:T(8,128)(2,1)}, bf16[72,1152]{1,0:T(8,128)(2,1)S(1)}, u32[]{:S(2)}, u32[]{:S(2)}) collective-permute-start(bf16[72,1152]{1,0:T(8,128)(2,1)} %param.11), channel_id=1, source_target_pairs={{0,8},{3,9},{4,12},{7,13},{8,16},{11,17},{12,20},{15,21},{16,26},{... | collective-permute-start | bytes 497672 | tf_op jit(solution)/shard_map/ppermute | solution.py:53
  67.3 4.4 %collective-permute-start.18 = (bf16[72,1152]{1,0:T(8,128)(2,1)}, bf16[72,1152]{1,0:T(8,128)(2,1)S(1)}, u32[]{:S(2)}, u32[]{:S(2)}) collective-permute-start(bf16[72,1152]{1,0:T(8,128)(2,1)} %param.11), channel_id=1, source_target_pairs={{0,24},{3,25},{4,28},{7,29},{8,0},{11,1},{12,4},{15,5},{16,10},{19... | collective-permute-start | bytes 497672 | tf_op jit(solution)/shard_map/ppermute | solution.py:53
  73.1 3.2 %shard_map.79 = (bf16[1024,432]{1,0:T(8,128)(2,1)S(1)}, bf16[1152,432]{1,0:T(8,128)(2,1)S(1)}) custom-call(s32[4]{0:T(128)S(1)} %pad_add_fusion.at_ref, bf16[4,128,1152]{2,1,0:T(8,128)(2,1)S(1)} %pad_maximum_fusion.1.refs_0_.xs, bf16[4,128,1152]{2,1,0:T(8,128)(2,1)} %collective-permute-done.7.refs_1_.xc, bf16[2,72,864]{2,1,0:T(8,128)(2,1)S(1)} %shard_map.78.refs_2_, ...), custom_call_target="tpu_custom_call" | custom-call | flops 1019215872 | bytes 6291456 | tf_op jit(solution)/shard_map/pallas_call | solution.py:412
  76.7 8.4 %shard_map.80 = (bf16[72,1152]{1,0:T(8,128)(2,1)S(1)}, bf16[72,1152]{1,0:T(8,128)(2,1)S(1)}, bf16[72,1152]{1,0:T(8,128)(2,1)S(1)}, bf16[72,1152]{1,0:T(8,128)(2,1)S(1)}, bf16[1024,432]{1,0:T(8,128)(2,1)S(1)}) custom-call(s32[4]{0:T(128)S(1)} %pad_add_fusion.at_ref, bf16[4,128,1152]{2,1,0:T(8,128)(2,1)S(1)} %pad_maximum_fusion.refs_0_, ...), custom_call_target="tpu_custom_call" | custom-call | flops 1019215872 | bytes 6291456 | tf_op jit(solution)/shard_map/pallas_call | solution.py:413
  87.5 5.1 %collective-permute-start.36 = (bf16[72,1152]{1,0:T(8,128)(2,1)S(1)}, bf16[72,1152]{1,0:T(8,128)(2,1)S(1)}, u32[]{:S(2)}, u32[]{:S(2)}) collective-permute-start(bf16[72,1152]{1,0:T(8,128)(2,1)S(1)} %get-tuple-element.43), channel_id=1, source_target_pairs={{0,8},{1,11},{4,12},{5,15},{10,16},{11,19},{14,20},{15,23},{18,24}... | collective-permute-start | bytes 497672 | tf_op jit(solution)/shard_map/ppermute | solution.py:53
  95.2 3.0 %shard_map.82 = (bf16[2,72,864]{2,1,0:T(8,128)(2,1)S(1)}, bf16[2,72,864]{2,1,0:T(8,128)(2,1)S(1)}, bf16[2,72,864]{2,1,0:T(8,128)(2,1)S(1)}, bf16[2,72,864]{2,1,0:T(8,128)(2,1)S(1)}, bf16[2,72,864]{2,1,0:T(8,128)(2,1)S(1)}) custom-call(s32[4]{0:T(128)S(1)} %pad_add_fusion.at_ref, bf16[4,128,1152]{2,1,0:T(8,128)(2,1)S(1)} %pad_maximum_fusion.1.refs_0_.xs, ...), custom_call_target="tpu_custom_call" | custom-call | flops 1019215872 | bytes 5242880 | tf_op jit(solution)/shard_map/pallas_call | solution.py:442
  98.2 4.6 %collective-permute-start.24 = (bf16[2,72,864]{2,1,0:T(8,128)(2,1)S(1)}, bf16[2,72,864]{2,1,0:T(8,128)(2,1)S(1)}, u32[]{:S(2)}, u32[]{:S(2)}) collective-permute-start(bf16[2,72,864]{2,1,0:T(8,128)(2,1)S(1)} %get-tuple-element.35), channel_id=1, source_target_pairs={{0,8},{1,9},{2,10},{3,11},{4,12},{5,13},{6,14},{7,15},{8,16},{9,17... | collective-permute-start | bytes 746504 | tf_op jit(solution)/shard_map/ppermute | solution.py:53
  104.1 4.6 %collective-permute-start.26 = (bf16[2,72,864]{2,1,0:T(8,128)(2,1)S(1)}, bf16[2,72,864]{2,1,0:T(8,128)(2,1)S(1)}, u32[]{:S(2)}, u32[]{:S(2)}) collective-permute-start(bf16[2,72,864]{2,1,0:T(8,128)(2,1)S(1)} %get-tuple-element.37), channel_id=1, source_target_pairs={{0,8},{1,9},{2,10},{3,11},{4,12},{5,13},{6,14},{7,15},{24,16},{25,... | collective-permute-start | bytes 746504 | tf_op jit(solution)/shard_map/ppermute | solution.py:53
  108.8 2.7 %collective-permute-start.23 = (bf16[2,72,864]{2,1,0:T(8,128)(2,1)S(1)}, bf16[2,72,864]{2,1,0:T(8,128)(2,1)S(1)}, u32[]{:S(2)}, u32[]{:S(2)}) collective-permute-start(bf16[2,72,864]{2,1,0:T(8,128)(2,1)S(1)} %get-tuple-element.34), channel_id=1, source_target_pairs={{0,16},{1,17},{2,18},{3,19},{4,20},{5,21},{6,22},{7,23},{24,8},{25... | collective-permute-start | bytes 746504 | tf_op jit(solution)/shard_map/ppermute | solution.py:53
  111.6 3.6 %collective-permute-done.26 = bf16[2,72,864]{2,1,0:T(8,128)(2,1)S(1)} collective-permute-done((bf16[2,72,864]{2,1,0:T(8,128)(2,1)S(1)}, bf16[2,72,864]{2,1,0:T(8,128)(2,1)S(1)}, u32[]{:S(2)}, u32[]{:S(2)}) %collective-permute-start.26) | collective-permute-done | bytes 248864 | tf_op jit(solution)/shard_map/ppermute | solution.py:53
  115.2 6.5 %collective-permute-start.39 = (bf16[72,1152]{1,0:T(8,128)(2,1)S(1)}, bf16[72,1152]{1,0:T(8,128)(2,1)S(1)}, u32[]{:S(2)}, u32[]{:S(2)}) collective-permute-start(bf16[72,1152]{1,0:T(8,128)(2,1)S(1)} %add_convert_fusion.4.refs_8_), channel_id=1, source_target_pairs={{0,1},{3,2},{4,5},{7,6},{8,9},{11,10},{12,13},{15,14},{16,17},{19,... | collective-permute-start | bytes 497672 | tf_op jit(solution)/shard_map/ppermute | solution.py:53
  124.3 2.5 %collective-permute-start.21 = (bf16[128,1152]{1,0:T(8,128)(2,1)S(1)}, bf16[128,1152]{1,0:T(8,128)(2,1)S(1)}, u32[]{:S(2)}, u32[]{:S(2)}) collective-permute-start(bf16[128,1152]{1,0:T(8,128)(2,1)S(1)} %get-tuple-element.48), channel_id=1, source_target_pairs={{0,1},{1,0},{2,3},{3,2},{4,5},{5,4},{6,7},{7,6},{8,9},{9,8},{10,11... | collective-permute-start | bytes 884744 | tf_op jit(solution)/shard_map/ppermute | solution.py:53
  126.9 4.9 %collective-permute-done.27.refs_4_ = bf16[2,72,864]{2,1,0:T(8,128)(2,1)S(1)} collective-permute-done((bf16[2,72,864]{2,1,0:T(8,128)(2,1)S(1)}, bf16[2,72,864]{2,1,0:T(8,128)(2,1)S(1)}, u32[]{:S(2)}, u32[]{:S(2)}) %collective-permute-start.27) | collective-permute-done | bytes 248864 | tf_op jit(solution)/shard_map/ppermute | solution.py:53
  134.2 5.3 %collective-permute-done.28.refs_1_ = bf16[72,432]{1,0:T(8,128)(2,1)S(1)} collective-permute-done((bf16[72,432]{1,0:T(8,128)(2,1)S(1)}, bf16[72,432]{1,0:T(8,128)(2,1)S(1)}, u32[]{:S(2)}, u32[]{:S(2)}) %collective-permute-start.28) | collective-permute-done | bytes 62240 | tf_op jit(solution)/shard_map/ppermute | solution.py:53
  139.8 2.3 %collective-permute-start.32 = (bf16[72,432]{1,0:T(8,128)(2,1)S(1)}, bf16[72,432]{1,0:T(8,128)(2,1)S(1)}, u32[]{:S(2)}, u32[]{:S(2)}) collective-permute-start(bf16[72,432]{1,0:T(8,128)(2,1)S(1)} %get-tuple-element.40), channel_id=1, source_target_pairs={{0,5},{1,4},{2,7},{3,6},{4,1},{5,0},{6,3},{7,2},{8,13},{9,12},{10,... | collective-permute-start | bytes 186632 | tf_op jit(solution)/shard_map/ppermute | solution.py:53
  143.0 2.3 %collective-permute-done.32.refs_5_ = bf16[72,432]{1,0:T(8,128)(2,1)S(1)} collective-permute-done((bf16[72,432]{1,0:T(8,128)(2,1)S(1)}, bf16[72,432]{1,0:T(8,128)(2,1)S(1)}, u32[]{:S(2)}, u32[]{:S(2)}) %collective-permute-start.32) | collective-permute-done | bytes 62240 | tf_op jit(solution)/shard_map/ppermute | solution.py:53
  145.3 1.8 %collective-permute-start.34 = (bf16[72,432]{1,0:T(8,128)(2,1)S(1)}, bf16[72,432]{1,0:T(8,128)(2,1)S(1)}, u32[]{:S(2)}, u32[]{:S(2)}) collective-permute-start(bf16[72,432]{1,0:T(8,128)(2,1)S(1)} %get-tuple-element.41), channel_id=1, source_target_pairs={{0,7},{1,6},{2,5},{3,4},{4,3},{5,2},{6,1},{7,0},{8,15},{9,14},{10,... | collective-permute-start | bytes 186632 | tf_op jit(solution)/shard_map/ppermute | solution.py:53
  150.3 2.1 %collective-permute-done.33.refs_6_ = bf16[72,432]{1,0:T(8,128)(2,1)S(1)} collective-permute-done((bf16[72,432]{1,0:T(8,128)(2,1)S(1)}, bf16[72,432]{1,0:T(8,128)(2,1)S(1)}, u32[]{:S(2)}, u32[]{:S(2)}) %collective-permute-start.33) | collective-permute-done | bytes 62240 | tf_op jit(solution)/shard_map/ppermute | solution.py:53
  152.4 2.6 %shard_map.84 = f32[72,4608]{1,0:T(8,128)} custom-call(s32[4]{0:T(128)S(1)} %pad_add_fusion.at_ref, bf16[72,432]{1,0:T(8,128)(2,1)S(1)} %get-tuple-element.38.refs_0_, bf16[72,432]{1,0:T(8,128)(2,1)S(1)} %collective-permute-done.28.refs_1_, bf16[72,432]{1,0:T(8,128)(2,1)S(1)} %collective-permute-done.29.refs_2_, ...), custom_call_target="tpu_custom_call" | custom-call | tf_op jit(solution)/shard_map/pallas_call | solution.py:500
  (65 shorter events, 30.3 us)
Async XLA Ops:
  0.6 12.1 %collective-permute-start.6 = (bf16[128,1152]{1,0:T(8,128)(2,1)}, bf16[128,1152]{1,0:T(8,128)(2,1)S(1)}, u32[]{:S(2)}, u32[]{:S(2)}) collective-permute-start(bf16[128,1152]{1,0:T(8,128)(2,1)} %bitcast.25), channel_id=1, source_target_pairs={{0,5},{1,4},{2,7},{3,6},{4,1},{5,0},{6,3},{7,2},{8,13},{9,12},{10,... | collective-permute-start | bytes 884744 | tf_op jit(solution)/shard_map/ppermute | solution.py:53
  4.6 14.5 %collective-permute-start.5 = (bf16[128,1152]{1,0:T(8,128)(2,1)}, bf16[128,1152]{1,0:T(8,128)(2,1)S(1)}, u32[]{:S(2)}, u32[]{:S(2)}) collective-permute-start(bf16[128,1152]{1,0:T(8,128)(2,1)} %bitcast.26), channel_id=1, source_target_pairs={{0,1},{1,0},{2,3},{3,2},{4,5},{5,4},{6,7},{7,6},{8,9},{9,8},{10,11... | collective-permute-start | bytes 884744 | tf_op jit(solution)/shard_map/ppermute | solution.py:53
  5.1 14.5 %collective-permute-start.4 = (bf16[128,1152]{1,0:T(8,128)(2,1)}, bf16[128,1152]{1,0:T(8,128)(2,1)S(1)}, u32[]{:S(2)}, u32[]{:S(2)}) collective-permute-start(bf16[128,1152]{1,0:T(8,128)(2,1)} %bitcast.27), channel_id=1, source_target_pairs={{0,4},{1,5},{2,6},{3,7},{4,0},{5,1},{6,2},{7,3},{8,12},{9,13},{10,... | collective-permute-start | bytes 884744 | tf_op jit(solution)/shard_map/ppermute | solution.py:53
  5.3 20.2 %collective-permute-start.2 = (bf16[128,1152]{1,0:T(8,128)(2,1)}, bf16[128,1152]{1,0:T(8,128)(2,1)S(1)}, u32[]{:S(2)}, u32[]{:S(2)}) collective-permute-start(bf16[128,1152]{1,0:T(8,128)(2,1)} %bitcast.29), channel_id=1, source_target_pairs={{0,5},{1,4},{2,7},{3,6},{4,1},{5,0},{6,3},{7,2},{8,13},{9,12},{10,... | collective-permute-start | bytes 884744 | tf_op jit(solution)/shard_map/ppermute | solution.py:53
  8.1 22.7 %collective-permute-start.1 = (bf16[128,1152]{1,0:T(8,128)(2,1)}, bf16[128,1152]{1,0:T(8,128)(2,1)S(1)}, u32[]{:S(2)}, u32[]{:S(2)}) collective-permute-start(bf16[128,1152]{1,0:T(8,128)(2,1)} %bitcast.30), channel_id=1, source_target_pairs={{0,1},{1,0},{2,3},{3,2},{4,5},{5,4},{6,7},{7,6},{8,9},{9,8},{10,11... | collective-permute-start | bytes 884744 | tf_op jit(solution)/shard_map/ppermute | solution.py:53
  12.7 18.4 %collective-permute-start = (bf16[128,1152]{1,0:T(8,128)(2,1)}, bf16[128,1152]{1,0:T(8,128)(2,1)S(1)}, u32[]{:S(2)}, u32[]{:S(2)}) collective-permute-start(bf16[128,1152]{1,0:T(8,128)(2,1)} %bitcast.31), channel_id=1, source_target_pairs={{0,4},{1,5},{2,6},{3,7},{4,0},{5,1},{6,2},{7,3},{8,12},{9,13},{10,... | collective-permute-start | bytes 884744 | tf_op jit(solution)/shard_map/ppermute | solution.py:53
  20.8 51.0 %collective-permute-start.7 = (bf16[4,128,1152]{2,1,0:T(8,128)(2,1)S(1)}, bf16[4,128,1152]{2,1,0:T(8,128)(2,1)}, u32[]{:S(2)}, u32[]{:S(2)}) collective-permute-start(bf16[4,128,1152]{2,1,0:T(8,128)(2,1)S(1)} %pad_maximum_fusion.1.refs_0_.xs), channel_id=1, source_target_pairs={{0,2},{1,3},{2,0},{3,1},{4,6},{5,7},{6,4},{7,5},{8,10},{9,11},{10,... | collective-permute-start | bytes 3538952 | tf_op jit(solution)/shard_map/ppermute | solution.py:53
  31.3 45.4 %collective-permute-start.3 = (bf16[4,128,1152]{2,1,0:T(8,128)(2,1)S(1)}, bf16[4,128,1152]{2,1,0:T(8,128)(2,1)S(1)}, u32[]{:S(2)}, u32[]{:S(2)}) collective-permute-start(bf16[4,128,1152]{2,1,0:T(8,128)(2,1)S(1)} %pad_maximum_fusion.refs_0_), channel_id=1, source_target_pairs={{0,2},{1,3},{2,0},{3,1},{4,6},{5,7},{6,4},{7,5},{8,10},{9,11},{10,... | collective-permute-start | bytes 3538952 | tf_op jit(solution)/shard_map/ppermute | solution.py:53
  41.6 15.6 %collective-permute-start.12 = (bf16[2,72,864]{2,1,0:T(8,128)(2,1)S(1)}, bf16[2,72,864]{2,1,0:T(8,128)(2,1)S(1)}, u32[]{:S(2)}, u32[]{:S(2)}) collective-permute-start(bf16[2,72,864]{2,1,0:T(8,128)(2,1)S(1)} %shard_map.78.refs_2_), channel_id=1, source_target_pairs={{0,16},{1,17},{2,18},{3,19},{4,20},{5,21},{6,22},{7,23},{8,24},{9,... | collective-permute-start | bytes 746504 | tf_op jit(solution)/shard_map/ppermute | solution.py:53
  44.2 14.3 %collective-permute-start.13 = (bf16[2,72,864]{2,1,0:T(8,128)(2,1)S(1)}, bf16[2,72,864]{2,1,0:T(8,128)(2,1)S(1)}, u32[]{:S(2)}, u32[]{:S(2)}) collective-permute-start(bf16[2,72,864]{2,1,0:T(8,128)(2,1)S(1)} %shard_map.78.refs_2_), channel_id=1, source_target_pairs={{8,0},{9,1},{10,2},{11,3},{12,4},{13,5},{14,6},{15,7},{16,8},{17,9... | collective-permute-start | bytes 746504 | tf_op jit(solution)/shard_map/ppermute | solution.py:53
  45.5 18.8 %collective-permute-start.11 = (bf16[2,72,864]{2,1,0:T(8,128)(2,1)S(1)}, bf16[2,72,864]{2,1,0:T(8,128)(2,1)S(1)}, u32[]{:S(2)}, u32[]{:S(2)}) collective-permute-start(bf16[2,72,864]{2,1,0:T(8,128)(2,1)S(1)} %shard_map.78.refs_2_), channel_id=1, source_target_pairs={{0,8},{1,9},{2,10},{3,11},{4,12},{5,13},{6,14},{7,15},{8,16},{9,17... | collective-permute-start | bytes 746504 | tf_op jit(solution)/shard_map/ppermute | solution.py:53
  57.2 10.1 %collective-permute-start.14 = (bf16[2,72,864]{2,1,0:T(8,128)(2,1)S(1)}, bf16[2,72,864]{2,1,0:T(8,128)(2,1)S(1)}, u32[]{:S(2)}, u32[]{:S(2)}) collective-permute-start(bf16[2,72,864]{2,1,0:T(8,128)(2,1)S(1)} %collective-permute-done.12.refs_4_), channel_id=1, source_target_pairs={{8,0},{9,1},{10,2},{11,3},{12,4},{13,5},{14,6},{15,7},{16,24},{17,... | collective-permute-start | bytes 746504 | tf_op jit(solution)/shard_map/ppermute | solution.py:53
  58.5 17.8 %collective-permute-start.16 = (bf16[72,1152]{1,0:T(8,128)(2,1)}, bf16[72,1152]{1,0:T(8,128)(2,1)S(1)}, u32[]{:S(2)}, u32[]{:S(2)}) collective-permute-start(bf16[72,1152]{1,0:T(8,128)(2,1)} %param.11), channel_id=1, source_target_pairs={{0,8},{3,9},{4,12},{7,13},{8,16},{11,17},{12,20},{15,21},{16,26},{... | collective-permute-start | bytes 497672 | tf_op jit(solution)/shard_map/ppermute | solution.py:53
  64.3 12.0 %collective-permute-start.15 = (bf16[72,1152]{1,0:T(8,128)(2,1)}, bf16[72,1152]{1,0:T(8,128)(2,1)S(1)}, u32[]{:S(2)}, u32[]{:S(2)}) collective-permute-start(bf16[72,1152]{1,0:T(8,128)(2,1)} %param.11), channel_id=1, source_target_pairs={{0,0},{3,1},{4,4},{7,5},{8,8},{11,9},{12,12},{15,13},{16,18},{19,1... | collective-permute-start | bytes 497672 | tf_op jit(solution)/shard_map/ppermute | solution.py:53
  67.3 9.1 %collective-permute-start.18 = (bf16[72,1152]{1,0:T(8,128)(2,1)}, bf16[72,1152]{1,0:T(8,128)(2,1)S(1)}, u32[]{:S(2)}, u32[]{:S(2)}) collective-permute-start(bf16[72,1152]{1,0:T(8,128)(2,1)} %param.11), channel_id=1, source_target_pairs={{0,24},{3,25},{4,28},{7,29},{8,0},{11,1},{12,4},{15,5},{16,10},{19... | collective-permute-start | bytes 497672 | tf_op jit(solution)/shard_map/ppermute | solution.py:53
  86.7 35.0 %collective-permute-start.19 = (bf16[4,128,1152]{2,1,0:T(8,128)(2,1)S(1)}, bf16[4,128,1152]{2,1,0:T(8,128)(2,1)S(1)}, u32[]{:S(2)}, u32[]{:S(2)}) collective-permute-start(bf16[4,128,1152]{2,1,0:T(8,128)(2,1)S(1)} %get-tuple-element.32), channel_id=1, source_target_pairs={{0,2},{1,3},{2,0},{3,1},{4,6},{5,7},{6,4},{7,5},{8,10},{9,11},{10,... | collective-permute-start | bytes 3538952 | tf_op jit(solution)/shard_map/ppermute | solution.py:53
  86.8 11.4 %collective-permute-start.35 = (bf16[72,1152]{1,0:T(8,128)(2,1)S(1)}, bf16[72,1152]{1,0:T(8,128)(2,1)S(1)}, u32[]{:S(2)}, u32[]{:S(2)}) collective-permute-start(bf16[72,1152]{1,0:T(8,128)(2,1)S(1)} %get-tuple-element.42), channel_id=1, source_target_pairs={{0,0},{1,3},{4,4},{5,7},{8,8},{9,11},{12,12},{13,15},{18,16},{19,1... | collective-permute-start | bytes 497672 | tf_op jit(solution)/shard_map/ppermute | solution.py:53
  87.5 15.3 %collective-permute-start.36 = (bf16[72,1152]{1,0:T(8,128)(2,1)S(1)}, bf16[72,1152]{1,0:T(8,128)(2,1)S(1)}, u32[]{:S(2)}, u32[]{:S(2)}) collective-permute-start(bf16[72,1152]{1,0:T(8,128)(2,1)S(1)} %get-tuple-element.43), channel_id=1, source_target_pairs={{0,8},{1,11},{4,12},{5,15},{10,16},{11,19},{14,20},{15,23},{18,24}... | collective-permute-start | bytes 497672 | tf_op jit(solution)/shard_map/ppermute | solution.py:53
  92.6 11.5 %collective-permute-start.37 = (bf16[72,1152]{1,0:T(8,128)(2,1)S(1)}, bf16[72,1152]{1,0:T(8,128)(2,1)S(1)}, u32[]{:S(2)}, u32[]{:S(2)}) collective-permute-start(bf16[72,1152]{1,0:T(8,128)(2,1)S(1)} %get-tuple-element.44), channel_id=1, source_target_pairs={{2,16},{3,19},{6,20},{7,23},{10,24},{11,27},{14,28},{15,31},{16,0}... | collective-permute-start | bytes 497672 | tf_op jit(solution)/shard_map/ppermute | solution.py:53
  93.9 14.9 %collective-permute-start.38 = (bf16[72,1152]{1,0:T(8,128)(2,1)S(1)}, bf16[72,1152]{1,0:T(8,128)(2,1)S(1)}, u32[]{:S(2)}, u32[]{:S(2)}) collective-permute-start(bf16[72,1152]{1,0:T(8,128)(2,1)S(1)} %get-tuple-element.45), channel_id=1, source_target_pairs={{2,24},{3,27},{6,28},{7,31},{8,0},{9,3},{12,4},{13,7},{16,8},{17,1... | collective-permute-start | bytes 497672 | tf_op jit(solution)/shard_map/ppermute | solution.py:53
  98.2 25.0 %collective-permute-start.24 = (bf16[2,72,864]{2,1,0:T(8,128)(2,1)S(1)}, bf16[2,72,864]{2,1,0:T(8,128)(2,1)S(1)}, u32[]{:S(2)}, u32[]{:S(2)}) collective-permute-start(bf16[2,72,864]{2,1,0:T(8,128)(2,1)S(1)} %get-tuple-element.35), channel_id=1, source_target_pairs={{0,8},{1,9},{2,10},{3,11},{4,12},{5,13},{6,14},{7,15},{8,16},{9,17... | collective-permute-start | bytes 746504 | tf_op jit(solution)/shard_map/ppermute | solution.py:53
  102.8 21.5 %collective-permute-start.25 = (bf16[2,72,864]{2,1,0:T(8,128)(2,1)S(1)}, bf16[2,72,864]{2,1,0:T(8,128)(2,1)S(1)}, u32[]{:S(2)}, u32[]{:S(2)}) collective-permute-start(bf16[2,72,864]{2,1,0:T(8,128)(2,1)S(1)} %get-tuple-element.36), channel_id=1, source_target_pairs={{8,0},{9,1},{10,2},{11,3},{12,4},{13,5},{14,6},{15,7},{16,8},{17,9... | collective-permute-start | bytes 746504 | tf_op jit(solution)/shard_map/ppermute | solution.py:53
  104.1 11.1 %collective-permute-start.26 = (bf16[2,72,864]{2,1,0:T(8,128)(2,1)S(1)}, bf16[2,72,864]{2,1,0:T(8,128)(2,1)S(1)}, u32[]{:S(2)}, u32[]{:S(2)}) collective-permute-start(bf16[2,72,864]{2,1,0:T(8,128)(2,1)S(1)} %get-tuple-element.37), channel_id=1, source_target_pairs={{0,8},{1,9},{2,10},{3,11},{4,12},{5,13},{6,14},{7,15},{24,16},{25,... | collective-permute-start | bytes 746504 | tf_op jit(solution)/shard_map/ppermute | solution.py:53
  108.8 15.6 %collective-permute-start.23 = (bf16[2,72,864]{2,1,0:T(8,128)(2,1)S(1)}, bf16[2,72,864]{2,1,0:T(8,128)(2,1)S(1)}, u32[]{:S(2)}, u32[]{:S(2)}) collective-permute-start(bf16[2,72,864]{2,1,0:T(8,128)(2,1)S(1)} %get-tuple-element.34), channel_id=1, source_target_pairs={{0,16},{1,17},{2,18},{3,19},{4,20},{5,21},{6,22},{7,23},{24,8},{25... | collective-permute-start | bytes 746504 | tf_op jit(solution)/shard_map/ppermute | solution.py:53
  115.2 19.0 %collective-permute-start.39 = (bf16[72,1152]{1,0:T(8,128)(2,1)S(1)}, bf16[72,1152]{1,0:T(8,128)(2,1)S(1)}, u32[]{:S(2)}, u32[]{:S(2)}) collective-permute-start(bf16[72,1152]{1,0:T(8,128)(2,1)S(1)} %add_convert_fusion.4.refs_8_), channel_id=1, source_target_pairs={{0,1},{3,2},{4,5},{7,6},{8,9},{11,10},{12,13},{15,14},{16,17},{19,... | collective-permute-start | bytes 497672 | tf_op jit(solution)/shard_map/ppermute | solution.py:53
  121.8 9.9 %collective-permute-start.27 = (bf16[2,72,864]{2,1,0:T(8,128)(2,1)S(1)}, bf16[2,72,864]{2,1,0:T(8,128)(2,1)S(1)}, u32[]{:S(2)}, u32[]{:S(2)}) collective-permute-start(bf16[2,72,864]{2,1,0:T(8,128)(2,1)S(1)} %add_convert_fusion.3), channel_id=1, source_target_pairs={{8,24},{9,25},{10,26},{11,27},{12,28},{13,29},{14,30},{15,31},{16,... | collective-permute-start | bytes 746504 | tf_op jit(solution)/shard_map/ppermute | solution.py:53
  123.3 31.7 %collective-permute-start.20 = (bf16[128,1152]{1,0:T(8,128)(2,1)S(1)}, bf16[128,1152]{1,0:T(8,128)(2,1)S(1)}, u32[]{:S(2)}, u32[]{:S(2)}) collective-permute-start(bf16[128,1152]{1,0:T(8,128)(2,1)S(1)} %get-tuple-element.46), channel_id=1, source_target_pairs={{0,4},{1,5},{2,6},{3,7},{4,0},{5,1},{6,2},{7,3},{8,12},{9,13},{10,... | collective-permute-start | bytes 884744 | tf_op jit(solution)/shard_map/ppermute | solution.py:53
  124.3 30.6 %collective-permute-start.22 = (bf16[128,1152]{1,0:T(8,128)(2,1)S(1)}, bf16[128,1152]{1,0:T(8,128)(2,1)S(1)}, u32[]{:S(2)}, u32[]{:S(2)}) collective-permute-start(bf16[128,1152]{1,0:T(8,128)(2,1)S(1)} %get-tuple-element.47), channel_id=1, source_target_pairs={{0,5},{1,4},{2,7},{3,6},{4,1},{5,0},{6,3},{7,2},{8,13},{9,12},{10,... | collective-permute-start | bytes 884744 | tf_op jit(solution)/shard_map/ppermute | solution.py:53
  124.3 30.6 %collective-permute-start.21 = (bf16[128,1152]{1,0:T(8,128)(2,1)S(1)}, bf16[128,1152]{1,0:T(8,128)(2,1)S(1)}, u32[]{:S(2)}, u32[]{:S(2)}) collective-permute-start(bf16[128,1152]{1,0:T(8,128)(2,1)S(1)} %get-tuple-element.48), channel_id=1, source_target_pairs={{0,1},{1,0},{2,3},{3,2},{4,5},{5,4},{6,7},{7,6},{8,9},{9,8},{10,11... | collective-permute-start | bytes 884744 | tf_op jit(solution)/shard_map/ppermute | solution.py:53
  132.7 6.8 %collective-permute-start.28 = (bf16[72,432]{1,0:T(8,128)(2,1)S(1)}, bf16[72,432]{1,0:T(8,128)(2,1)S(1)}, u32[]{:S(2)}, u32[]{:S(2)}) collective-permute-start(bf16[72,432]{1,0:T(8,128)(2,1)S(1)} %get-tuple-element.38.refs_0_), channel_id=1, source_target_pairs={{0,1},{1,0},{2,3},{3,2},{4,5},{5,4},{6,7},{7,6},{8,9},{9,8},{10,11... | collective-permute-start | bytes 186632 | tf_op jit(solution)/shard_map/ppermute | solution.py:53
  134.2 5.6 %collective-permute-start.30 = (bf16[72,432]{1,0:T(8,128)(2,1)S(1)}, bf16[72,432]{1,0:T(8,128)(2,1)S(1)}, u32[]{:S(2)}, u32[]{:S(2)}) collective-permute-start(bf16[72,432]{1,0:T(8,128)(2,1)S(1)} %get-tuple-element.39), channel_id=1, source_target_pairs={{0,3},{1,2},{2,1},{3,0},{4,7},{5,6},{6,5},{7,4},{8,11},{9,10},{10,... | collective-permute-start | bytes 186632 | tf_op jit(solution)/shard_map/ppermute | solution.py:53
  139.8 5.5 %collective-permute-start.32 = (bf16[72,432]{1,0:T(8,128)(2,1)S(1)}, bf16[72,432]{1,0:T(8,128)(2,1)S(1)}, u32[]{:S(2)}, u32[]{:S(2)}) collective-permute-start(bf16[72,432]{1,0:T(8,128)(2,1)S(1)} %get-tuple-element.40), channel_id=1, source_target_pairs={{0,5},{1,4},{2,7},{3,6},{4,1},{5,0},{6,3},{7,2},{8,13},{9,12},{10,... | collective-permute-start | bytes 186632 | tf_op jit(solution)/shard_map/ppermute | solution.py:53
  (9 other events, 45.4 us)

commit v6 on v5

--- a/solution.py
+++ b/solution.py
@@ -85,24 +85,6 @@
             found[1], found[last], found[lines] = up, down, ends
         return [found[s] for s in range(len(found))]
 
-    def scatter_lines(self, values):
-        lines = self.lines
-        if lines != 4:
-            return [values[0]] + [self.shift(values[s], s) for s in range(1, lines)]
-
-        def way(hops):
-            return lambda a, b, c, g, y: (hops[a], b, c, g, y) if a in hops else None
-
-        relay = self.send(values[4], way({0: 1, 3: 2}))
-        terms = [
-            values[0],
-            self.send(values[2], way({0: 2, 3: 1})),
-            self.send(values[1], way({0: 1, 1: 2, 2: 3})),
-            self.send(values[3], way({1: 0, 2: 1, 3: 2})),
-        ]
-        both = values[2].astype(jnp.float32) + relay.astype(jnp.float32)
-        return terms + [self.send(both.astype(jnp.bfloat16), way({1: 3, 2: 0}))]
-
 
 def pack_kernel(dim, at_ref, *refs):
     sources, outs, weights, sems = refs[:3], refs[3:7], refs[7:10], refs[10]
@@ -288,8 +270,6 @@
         loose[p] = grads[p * shard : (p + 1) * shard, :].astype(jnp.bfloat16)
     for s, out in enumerate(grads_in):
         line = lax.rem(at_ref[0] + s, lines)
-        if s == lines:
-            line = jnp.where(at_ref[0] == 0, lines - 1, 0)
         for n in range(4):
             out[n // 2, :, (n % 2) * wide : (n % 2 + 1) * wide] = loose[4 * line + n]
 
@@ -395,7 +375,6 @@
         out_ws = [out_w]
     ds, dc = gather_rows(drows)
 
-    sent = lines + (lines == 4)
     owed = len(out_ws)
     head_rows = dim if one_head else wide
     project = pl.pallas_call(
@@ -428,9 +407,9 @@
     weigh = pl.pallas_call(
         weight_kernel,
         compiler_params=room(20),
-        out_shape=(shape_of(2, shard, 6 * wide),) * sent,
+        out_shape=(shape_of(2, shard, 6 * wide),) * lines,
         in_specs=[SMEM] + [VMEM] * 3,
-        out_specs=(VMEM,) * sent,
+        out_specs=(VMEM,) * lines,
         scratch_shapes=[
             pltpu.VMEM((pix, shard, 3 * wide), jnp.bfloat16),
             pltpu.VMEM((width, 3 * wide), jnp.float32),
@@ -441,7 +420,7 @@
     )
     grads_in = weigh(at, xs, xc, dqkv)
 
-    parts = grid.scatter_lines(grads_in)
+    parts = [grads_in[0]] + [grid.shift(grads_in[s], s) for s in range(1, lines)]
     if one_head:
         heads = [
             grid.send(

time: 159 us -> 155 us (0.975); the launches traced: 156 us -> 154 us
  starting transfers between devices: 75.9 us -> 67.3 us
  waiting for transfers between devices: 53 us -> 59.8 us
    ppermute x40 -> x38, starting transfers between devices: 75.9 us -> 67.3 us  [send(): return lax.ppermute(value, BOTH, pairs)]
    ppermute x40 -> x38, waiting for transfers between devices: 53 us -> 59.8 us  [send(): return lax.ppermute(value, BOTH, pairs)]
  transfers between devices with their start and end apart: 40 -> 38, of which waited for: 20 -> 17; matrix products, arithmetic and copies ran while one was open for 1% -> 1% of each run, Pallas kernels for 9% -> 9%
where the time goes in v6:
time: 155 us; the launch traced here: 154 us
  starting transfers between devices  67.3 us (43%)
  waiting for transfers between devices  59.8 us (39%)
  Pallas kernels  23.4 us (15%)
  other arithmetic  2.63 us (2%)
    ppermute x38, starting transfers between devices, send(): return lax.ppermute(value, BOTH, pairs)  67.3 us
    ppermute x38, waiting for transfers between devices, send(): return lax.ppermute(value, BOTH, pairs)  59.8 us
    pallas_call x1, Pallas kernels, local(): pl.pallas_call(functools.partial(attention_kernel, scale, lines, owed), c...  8.43 us
    pallas_call x1, Pallas kernels, local(): qkv, full = project(at, xs, xc, *planes)  3.28 us
    pallas_call x1, Pallas kernels, local(): grads_in = weigh(at, xs, xc, dqkv)  3.17 us
  transfers between devices with their start and end apart: 38, of which 17 were waited for; matrix products, arithmetic and copies ran while one was open for 1% of the time, Pallas kernels for 9%

profile of v6, /device:TPU:0, one launch (start us, length us, event | category | flops | bytes accessed | tf_op | source)
XLA Modules:
  0.0 154.1 jit_solution(3851373109421275629)
XLA Ops:
  0.6 4.0 %collective-permute-start.6 = (bf16[128,1152]{1,0:T(8,128)(2,1)}, bf16[128,1152]{1,0:T(8,128)(2,1)S(1)}, u32[]{:S(2)}, u32[]{:S(2)}) collective-permute-start(bf16[128,1152]{1,0:T(8,128)(2,1)} %bitcast.25), channel_id=1, source_target_pairs={{0,5},{1,4},{2,7},{3,6},{4,1},{5,0},{6,3},{7,2},{8,13},{9,12},{10,... | collective-permute-start | bytes 884744 | tf_op jit(solution)/shard_map/ppermute | solution.py:53
  5.3 2.8 %collective-permute-start.2 = (bf16[128,1152]{1,0:T(8,128)(2,1)}, bf16[128,1152]{1,0:T(8,128)(2,1)S(1)}, u32[]{:S(2)}, u32[]{:S(2)}) collective-permute-start(bf16[128,1152]{1,0:T(8,128)(2,1)} %bitcast.29), channel_id=1, source_target_pairs={{0,5},{1,4},{2,7},{3,6},{4,1},{5,0},{6,3},{7,2},{8,13},{9,12},{10,... | collective-permute-start | bytes 884744 | tf_op jit(solution)/shard_map/ppermute | solution.py:53
  8.6 4.1 %collective-permute-done.6 = bf16[128,1152]{1,0:T(8,128)(2,1)S(1)} collective-permute-done((bf16[128,1152]{1,0:T(8,128)(2,1)}, bf16[128,1152]{1,0:T(8,128)(2,1)S(1)}, u32[]{:S(2)}, u32[]{:S(2)}) %collective-permute-start.6) | collective-permute-done | bytes 294944 | tf_op jit(solution)/shard_map/ppermute | solution.py:53
  12.7 2.0 %collective-permute-start = (bf16[128,1152]{1,0:T(8,128)(2,1)}, bf16[128,1152]{1,0:T(8,128)(2,1)S(1)}, u32[]{:S(2)}, u32[]{:S(2)}) collective-permute-start(bf16[128,1152]{1,0:T(8,128)(2,1)} %bitcast.31), channel_id=1, source_target_pairs={{0,4},{1,5},{2,6},{3,7},{4,0},{5,1},{6,2},{7,3},{8,12},{9,13},{10,... | collective-permute-start | bytes 884744 | tf_op jit(solution)/shard_map/ppermute | solution.py:53
  14.7 4.4 %collective-permute-done.5 = bf16[128,1152]{1,0:T(8,128)(2,1)S(1)} collective-permute-done((bf16[128,1152]{1,0:T(8,128)(2,1)}, bf16[128,1152]{1,0:T(8,128)(2,1)S(1)}, u32[]{:S(2)}, u32[]{:S(2)}) %collective-permute-start.5) | collective-permute-done | bytes 294944 | tf_op jit(solution)/shard_map/ppermute | solution.py:53
  20.8 4.6 %collective-permute-done.2 = bf16[128,1152]{1,0:T(8,128)(2,1)S(1)} collective-permute-done((bf16[128,1152]{1,0:T(8,128)(2,1)}, bf16[128,1152]{1,0:T(8,128)(2,1)S(1)}, u32[]{:S(2)}, u32[]{:S(2)}) %collective-permute-start.2) | collective-permute-done | bytes 294944 | tf_op jit(solution)/shard_map/ppermute | solution.py:53
  25.4 5.4 %collective-permute-done.1 = bf16[128,1152]{1,0:T(8,128)(2,1)S(1)} collective-permute-done((bf16[128,1152]{1,0:T(8,128)(2,1)}, bf16[128,1152]{1,0:T(8,128)(2,1)S(1)}, u32[]{:S(2)}, u32[]{:S(2)}) %collective-permute-start.1) | collective-permute-done | bytes 294944 | tf_op jit(solution)/shard_map/ppermute | solution.py:53
  31.5 2.7 %shard_map.77 = (bf16[72,432]{1,0:T(8,128)(2,1)S(1)}, bf16[72,432]{1,0:T(8,128)(2,1)S(1)}, bf16[72,432]{1,0:T(8,128)(2,1)S(1)}, bf16[72,432]{1,0:T(8,128)(2,1)S(1)}) custom-call(s32[4]{0:T(128)S(1)} %pad_add_fusion.at_ref, bf16[72,1152]{1,0:T(8,128)(2,1)} %refs_0_.1, bf16[72,1152]{1,0:T(8,128)(2,1)} %refs_1_.1, bf16[72,1152]{1,0:T(8,128)(2,1)} %refs_2_.1), custom_call_target="tpu_custom_call" | custom-call | tf_op jit(solution)/shard_map/pallas_call | solution.py:338
  36.2 2.9 %collective-permute-done.9.refs_2_ = bf16[72,432]{1,0:T(8,128)(2,1)S(1)} collective-permute-done((bf16[72,432]{1,0:T(8,128)(2,1)S(1)}, bf16[72,432]{1,0:T(8,128)(2,1)S(1)}, u32[]{:S(2)}, u32[]{:S(2)}) %collective-permute-start.9) | collective-permute-done | bytes 62240 | tf_op jit(solution)/shard_map/ppermute | solution.py:53
  39.1 1.7 %collective-permute-done.10.refs_3_ = bf16[72,432]{1,0:T(8,128)(2,1)S(1)} collective-permute-done((bf16[72,432]{1,0:T(8,128)(2,1)S(1)}, bf16[72,432]{1,0:T(8,128)(2,1)S(1)}, u32[]{:S(2)}, u32[]{:S(2)}) %collective-permute-start.10) | collective-permute-done | bytes 62240 | tf_op jit(solution)/shard_map/ppermute | solution.py:53
  41.6 2.7 %collective-permute-start.12 = (bf16[2,72,864]{2,1,0:T(8,128)(2,1)S(1)}, bf16[2,72,864]{2,1,0:T(8,128)(2,1)S(1)}, u32[]{:S(2)}, u32[]{:S(2)}) collective-permute-start(bf16[2,72,864]{2,1,0:T(8,128)(2,1)S(1)} %shard_map.78.refs_2_), channel_id=1, source_target_pairs={{0,16},{1,17},{2,18},{3,19},{4,20},{5,21},{6,22},{7,23},{8,24},{9,... | collective-permute-start | bytes 746504 | tf_op jit(solution)/shard_map/ppermute | solution.py:53
  45.5 4.6 %collective-permute-start.11 = (bf16[2,72,864]{2,1,0:T(8,128)(2,1)S(1)}, bf16[2,72,864]{2,1,0:T(8,128)(2,1)S(1)}, u32[]{:S(2)}, u32[]{:S(2)}) collective-permute-start(bf16[2,72,864]{2,1,0:T(8,128)(2,1)S(1)} %shard_map.78.refs_2_), channel_id=1, source_target_pairs={{0,8},{1,9},{2,10},{3,11},{4,12},{5,13},{6,14},{7,15},{8,16},{9,17... | collective-permute-start | bytes 746504 | tf_op jit(solution)/shard_map/ppermute | solution.py:53
  50.1 7.1 %collective-permute-done.12.refs_4_ = bf16[2,72,864]{2,1,0:T(8,128)(2,1)S(1)} collective-permute-done((bf16[2,72,864]{2,1,0:T(8,128)(2,1)S(1)}, bf16[2,72,864]{2,1,0:T(8,128)(2,1)S(1)}, u32[]{:S(2)}, u32[]{:S(2)}) %collective-permute-start.12) | collective-permute-done | bytes 248864 | tf_op jit(solution)/shard_map/ppermute | solution.py:53
  58.5 5.8 %collective-permute-start.16 = (bf16[72,1152]{1,0:T(8,128)(2,1)}, bf16[72,1152]{1,0:T(8,128)(2,1)S(1)}, u32[]{:S(2)}, u32[]{:S(2)}) collective-permute-start(bf16[72,1152]{1,0:T(8,128)(2,1)} %param.11), channel_id=1, source_target_pairs={{0,8},{3,9},{4,12},{7,13},{8,16},{11,17},{12,20},{15,21},{16,26},{... | collective-permute-start | bytes 497672 | tf_op jit(solution)/shard_map/ppermute | solution.py:53
  64.3 1.6 %collective-permute-start.15 = (bf16[72,1152]{1,0:T(8,128)(2,1)}, bf16[72,1152]{1,0:T(8,128)(2,1)S(1)}, u32[]{:S(2)}, u32[]{:S(2)}) collective-permute-start(bf16[72,1152]{1,0:T(8,128)(2,1)} %param.11), channel_id=1, source_target_pairs={{0,0},{3,1},{4,4},{7,5},{8,8},{11,9},{12,12},{15,13},{16,18},{19,1... | collective-permute-start | bytes 497672 | tf_op jit(solution)/shard_map/ppermute | solution.py:53
  67.3 4.4 %collective-permute-start.18 = (bf16[72,1152]{1,0:T(8,128)(2,1)}, bf16[72,1152]{1,0:T(8,128)(2,1)S(1)}, u32[]{:S(2)}, u32[]{:S(2)}) collective-permute-start(bf16[72,1152]{1,0:T(8,128)(2,1)} %param.11), channel_id=1, source_target_pairs={{0,24},{3,25},{4,28},{7,29},{8,0},{11,1},{12,4},{15,5},{16,10},{19... | collective-permute-start | bytes 497672 | tf_op jit(solution)/shard_map/ppermute | solution.py:53
  73.1 3.3 %shard_map.79 = (bf16[1024,432]{1,0:T(8,128)(2,1)S(1)}, bf16[1152,432]{1,0:T(8,128)(2,1)S(1)}) custom-call(s32[4]{0:T(128)S(1)} %pad_add_fusion.at_ref, bf16[4,128,1152]{2,1,0:T(8,128)(2,1)S(1)} %pad_maximum_fusion.1.refs_0_.xs, bf16[4,128,1152]{2,1,0:T(8,128)(2,1)} %collective-permute-done.7.refs_1_.xc, bf16[2,72,864]{2,1,0:T(8,128)(2,1)S(1)} %shard_map.78.refs_2_, ...), custom_call_target="tpu_custom_call" | custom-call | flops 1019215872 | bytes 6291456 | tf_op jit(solution)/shard_map/pallas_call | solution.py:391
  76.7 8.4 %shard_map.80 = (bf16[72,1152]{1,0:T(8,128)(2,1)S(1)}, bf16[72,1152]{1,0:T(8,128)(2,1)S(1)}, bf16[72,1152]{1,0:T(8,128)(2,1)S(1)}, bf16[72,1152]{1,0:T(8,128)(2,1)S(1)}, bf16[1024,432]{1,0:T(8,128)(2,1)S(1)}) custom-call(s32[4]{0:T(128)S(1)} %pad_add_fusion.at_ref, bf16[4,128,1152]{2,1,0:T(8,128)(2,1)S(1)} %pad_maximum_fusion.refs_0_, ...), custom_call_target="tpu_custom_call" | custom-call | flops 1019215872 | bytes 6291456 | tf_op jit(solution)/shard_map/pallas_call | solution.py:392
  86.8 3.2 %shard_map.82 = (bf16[2,72,864]{2,1,0:T(8,128)(2,1)S(1)}, bf16[2,72,864]{2,1,0:T(8,128)(2,1)S(1)}, bf16[2,72,864]{2,1,0:T(8,128)(2,1)S(1)}, bf16[2,72,864]{2,1,0:T(8,128)(2,1)S(1)}) custom-call(s32[4]{0:T(128)S(1)} %pad_add_fusion.at_ref, bf16[4,128,1152]{2,1,0:T(8,128)(2,1)S(1)} %pad_maximum_fusion.1.refs_0_.xs, ...), custom_call_target="tpu_custom_call" | custom-call | flops 1019215872 | bytes 5242880 | tf_op jit(solution)/shard_map/pallas_call | solution.py:421
  90.0 3.2 %collective-permute-start.23 = (bf16[2,72,864]{2,1,0:T(8,128)(2,1)S(1)}, bf16[2,72,864]{2,1,0:T(8,128)(2,1)S(1)}, u32[]{:S(2)}, u32[]{:S(2)}) collective-permute-start(bf16[2,72,864]{2,1,0:T(8,128)(2,1)S(1)} %get-tuple-element.33), channel_id=1, source_target_pairs={{0,8},{1,9},{2,10},{3,11},{4,12},{5,13},{6,14},{7,15},{8,16},{9,17... | collective-permute-start | bytes 746504 | tf_op jit(solution)/shard_map/ppermute | solution.py:53
  93.2 3.3 %collective-permute-start.24 = (bf16[2,72,864]{2,1,0:T(8,128)(2,1)S(1)}, bf16[2,72,864]{2,1,0:T(8,128)(2,1)S(1)}, u32[]{:S(2)}, u32[]{:S(2)}) collective-permute-start(bf16[2,72,864]{2,1,0:T(8,128)(2,1)S(1)} %get-tuple-element.34), channel_id=1, source_target_pairs={{0,16},{1,17},{2,18},{3,19},{4,20},{5,21},{6,22},{7,23},{8,24},{9,... | collective-permute-start | bytes 746504 | tf_op jit(solution)/shard_map/ppermute | solution.py:53
  97.2 6.0 %collective-permute-done.23.refs_1_ = bf16[2,72,864]{2,1,0:T(8,128)(2,1)S(1)} collective-permute-done((bf16[2,72,864]{2,1,0:T(8,128)(2,1)S(1)}, bf16[2,72,864]{2,1,0:T(8,128)(2,1)S(1)}, u32[]{:S(2)}, u32[]{:S(2)}) %collective-permute-start.23) | collective-permute-done | bytes 248864 | tf_op jit(solution)/shard_map/ppermute | solution.py:53
  103.1 1.9 %collective-permute-start.34 = (bf16[72,1152]{1,0:T(8,128)(2,1)S(1)}, bf16[72,1152]{1,0:T(8,128)(2,1)S(1)}, u32[]{:S(2)}, u32[]{:S(2)}) collective-permute-start(bf16[72,1152]{1,0:T(8,128)(2,1)S(1)} %get-tuple-element.41), channel_id=1, source_target_pairs={{0,8},{1,11},{4,12},{5,15},{10,16},{11,19},{14,20},{15,23},{18,24}... | collective-permute-start | bytes 497672 | tf_op jit(solution)/shard_map/ppermute | solution.py:53
  105.1 8.9 %collective-permute-done.24.refs_2_ = bf16[2,72,864]{2,1,0:T(8,128)(2,1)S(1)} collective-permute-done((bf16[2,72,864]{2,1,0:T(8,128)(2,1)S(1)}, bf16[2,72,864]{2,1,0:T(8,128)(2,1)S(1)}, u32[]{:S(2)}, u32[]{:S(2)}) %collective-permute-start.24) | collective-permute-done | bytes 248864 | tf_op jit(solution)/shard_map/ppermute | solution.py:53
  117.5 6.5 %collective-permute-start.28 = (bf16[72,432]{1,0:T(8,128)(2,1)S(1)}, bf16[72,432]{1,0:T(8,128)(2,1)S(1)}, u32[]{:S(2)}, u32[]{:S(2)}) collective-permute-start(bf16[72,432]{1,0:T(8,128)(2,1)S(1)} %get-tuple-element.37), channel_id=1, source_target_pairs={{0,3},{1,2},{2,1},{3,0},{4,7},{5,6},{6,5},{7,4},{8,11},{9,10},{10,... | collective-permute-start | bytes 186632 | tf_op jit(solution)/shard_map/ppermute | solution.py:53
  125.0 1.6 %collective-permute-start.26 = (bf16[72,432]{1,0:T(8,128)(2,1)S(1)}, bf16[72,432]{1,0:T(8,128)(2,1)S(1)}, u32[]{:S(2)}, u32[]{:S(2)}) collective-permute-start(bf16[72,432]{1,0:T(8,128)(2,1)S(1)} %get-tuple-element.36.refs_0_), channel_id=1, source_target_pairs={{0,1},{1,0},{2,3},{3,2},{4,5},{5,4},{6,7},{7,6},{8,9},{9,8},{10,11... | collective-permute-start | bytes 186632 | tf_op jit(solution)/shard_map/ppermute | solution.py:53
  131.4 2.3 %collective-permute-start.22 = (bf16[128,1152]{1,0:T(8,128)(2,1)S(1)}, bf16[128,1152]{1,0:T(8,128)(2,1)S(1)}, u32[]{:S(2)}, u32[]{:S(2)}) collective-permute-start(bf16[128,1152]{1,0:T(8,128)(2,1)S(1)} %get-tuple-element.45), channel_id=1, source_target_pairs={{0,5},{1,4},{2,7},{3,6},{4,1},{5,0},{6,3},{7,2},{8,13},{9,12},{10,... | collective-permute-start | bytes 884744 | tf_op jit(solution)/shard_map/ppermute | solution.py:53
  133.9 3.9 %collective-permute-start.37 = (bf16[72,1152]{1,0:T(8,128)(2,1)S(1)}, bf16[72,1152]{1,0:T(8,128)(2,1)S(1)}, u32[]{:S(2)}, u32[]{:S(2)}) collective-permute-start(bf16[72,1152]{1,0:T(8,128)(2,1)S(1)} %add_convert_fusion.3.refs_8_), channel_id=1, source_target_pairs={{0,1},{3,2},{4,5},{7,6},{8,9},{11,10},{12,13},{15,14},{16,17},{19,... | collective-permute-start | bytes 497672 | tf_op jit(solution)/shard_map/ppermute | solution.py:53
  137.9 8.7 %collective-permute-done.32.refs_7_ = bf16[72,432]{1,0:T(8,128)(2,1)S(1)} collective-permute-done((bf16[72,432]{1,0:T(8,128)(2,1)S(1)}, bf16[72,432]{1,0:T(8,128)(2,1)S(1)}, u32[]{:S(2)}, u32[]{:S(2)}) %collective-permute-start.32) | collective-permute-done | bytes 62240 | tf_op jit(solution)/shard_map/ppermute | solution.py:53
  146.6 2.1 %collective-permute-start.31 = (bf16[72,432]{1,0:T(8,128)(2,1)S(1)}, bf16[72,432]{1,0:T(8,128)(2,1)S(1)}, u32[]{:S(2)}, u32[]{:S(2)}) collective-permute-start(bf16[72,432]{1,0:T(8,128)(2,1)S(1)} %get-tuple-element.39), channel_id=1, source_target_pairs={{0,6},{1,7},{2,4},{3,5},{4,2},{5,3},{6,0},{7,1},{8,14},{9,15},{10,... | collective-permute-start | bytes 186632 | tf_op jit(solution)/shard_map/ppermute | solution.py:53
  148.6 2.0 %collective-permute-done.31.refs_6_ = bf16[72,432]{1,0:T(8,128)(2,1)S(1)} collective-permute-done((bf16[72,432]{1,0:T(8,128)(2,1)S(1)}, bf16[72,432]{1,0:T(8,128)(2,1)S(1)}, u32[]{:S(2)}, u32[]{:S(2)}) %collective-permute-start.31) | collective-permute-done | bytes 62240 | tf_op jit(solution)/shard_map/ppermute | solution.py:53
  150.7 2.6 %shard_map.84 = f32[72,4608]{1,0:T(8,128)} custom-call(s32[4]{0:T(128)S(1)} %pad_add_fusion.at_ref, bf16[72,432]{1,0:T(8,128)(2,1)S(1)} %get-tuple-element.36.refs_0_, bf16[72,432]{1,0:T(8,128)(2,1)S(1)} %collective-permute-done.26.refs_1_, bf16[72,432]{1,0:T(8,128)(2,1)S(1)} %collective-permute-done.27.refs_2_, ...), custom_call_target="tpu_custom_call" | custom-call | tf_op jit(solution)/shard_map/pallas_call | solution.py:479
  (60 shorter events, 24.7 us)
Async XLA Ops:
  0.6 12.1 %collective-permute-start.6 = (bf16[128,1152]{1,0:T(8,128)(2,1)}, bf16[128,1152]{1,0:T(8,128)(2,1)S(1)}, u32[]{:S(2)}, u32[]{:S(2)}) collective-permute-start(bf16[128,1152]{1,0:T(8,128)(2,1)} %bitcast.25), channel_id=1, source_target_pairs={{0,5},{1,4},{2,7},{3,6},{4,1},{5,0},{6,3},{7,2},{8,13},{9,12},{10,... | collective-permute-start | bytes 884744 | tf_op jit(solution)/shard_map/ppermute | solution.py:53
  4.6 14.5 %collective-permute-start.5 = (bf16[128,1152]{1,0:T(8,128)(2,1)}, bf16[128,1152]{1,0:T(8,128)(2,1)S(1)}, u32[]{:S(2)}, u32[]{:S(2)}) collective-permute-start(bf16[128,1152]{1,0:T(8,128)(2,1)} %bitcast.26), channel_id=1, source_target_pairs={{0,1},{1,0},{2,3},{3,2},{4,5},{5,4},{6,7},{7,6},{8,9},{9,8},{10,11... | collective-permute-start | bytes 884744 | tf_op jit(solution)/shard_map/ppermute | solution.py:53
  5.1 14.5 %collective-permute-start.4 = (bf16[128,1152]{1,0:T(8,128)(2,1)}, bf16[128,1152]{1,0:T(8,128)(2,1)S(1)}, u32[]{:S(2)}, u32[]{:S(2)}) collective-permute-start(bf16[128,1152]{1,0:T(8,128)(2,1)} %bitcast.27), channel_id=1, source_target_pairs={{0,4},{1,5},{2,6},{3,7},{4,0},{5,1},{6,2},{7,3},{8,12},{9,13},{10,... | collective-permute-start | bytes 884744 | tf_op jit(solution)/shard_map/ppermute | solution.py:53
  5.3 20.2 %collective-permute-start.2 = (bf16[128,1152]{1,0:T(8,128)(2,1)}, bf16[128,1152]{1,0:T(8,128)(2,1)S(1)}, u32[]{:S(2)}, u32[]{:S(2)}) collective-permute-start(bf16[128,1152]{1,0:T(8,128)(2,1)} %bitcast.29), channel_id=1, source_target_pairs={{0,5},{1,4},{2,7},{3,6},{4,1},{5,0},{6,3},{7,2},{8,13},{9,12},{10,... | collective-permute-start | bytes 884744 | tf_op jit(solution)/shard_map/ppermute | solution.py:53
  8.1 22.7 %collective-permute-start.1 = (bf16[128,1152]{1,0:T(8,128)(2,1)}, bf16[128,1152]{1,0:T(8,128)(2,1)S(1)}, u32[]{:S(2)}, u32[]{:S(2)}) collective-permute-start(bf16[128,1152]{1,0:T(8,128)(2,1)} %bitcast.30), channel_id=1, source_target_pairs={{0,1},{1,0},{2,3},{3,2},{4,5},{5,4},{6,7},{7,6},{8,9},{9,8},{10,11... | collective-permute-start | bytes 884744 | tf_op jit(solution)/shard_map/ppermute | solution.py:53
  12.7 18.4 %collective-permute-start = (bf16[128,1152]{1,0:T(8,128)(2,1)}, bf16[128,1152]{1,0:T(8,128)(2,1)S(1)}, u32[]{:S(2)}, u32[]{:S(2)}) collective-permute-start(bf16[128,1152]{1,0:T(8,128)(2,1)} %bitcast.31), channel_id=1, source_target_pairs={{0,4},{1,5},{2,6},{3,7},{4,0},{5,1},{6,2},{7,3},{8,12},{9,13},{10,... | collective-permute-start | bytes 884744 | tf_op jit(solution)/shard_map/ppermute | solution.py:53
  20.8 51.0 %collective-permute-start.7 = (bf16[4,128,1152]{2,1,0:T(8,128)(2,1)S(1)}, bf16[4,128,1152]{2,1,0:T(8,128)(2,1)}, u32[]{:S(2)}, u32[]{:S(2)}) collective-permute-start(bf16[4,128,1152]{2,1,0:T(8,128)(2,1)S(1)} %pad_maximum_fusion.1.refs_0_.xs), channel_id=1, source_target_pairs={{0,2},{1,3},{2,0},{3,1},{4,6},{5,7},{6,4},{7,5},{8,10},{9,11},{10,... | collective-permute-start | bytes 3538952 | tf_op jit(solution)/shard_map/ppermute | solution.py:53
  31.3 45.4 %collective-permute-start.3 = (bf16[4,128,1152]{2,1,0:T(8,128)(2,1)S(1)}, bf16[4,128,1152]{2,1,0:T(8,128)(2,1)S(1)}, u32[]{:S(2)}, u32[]{:S(2)}) collective-permute-start(bf16[4,128,1152]{2,1,0:T(8,128)(2,1)S(1)} %pad_maximum_fusion.refs_0_), channel_id=1, source_target_pairs={{0,2},{1,3},{2,0},{3,1},{4,6},{5,7},{6,4},{7,5},{8,10},{9,11},{10,... | collective-permute-start | bytes 3538952 | tf_op jit(solution)/shard_map/ppermute | solution.py:53
  41.6 15.6 %collective-permute-start.12 = (bf16[2,72,864]{2,1,0:T(8,128)(2,1)S(1)}, bf16[2,72,864]{2,1,0:T(8,128)(2,1)S(1)}, u32[]{:S(2)}, u32[]{:S(2)}) collective-permute-start(bf16[2,72,864]{2,1,0:T(8,128)(2,1)S(1)} %shard_map.78.refs_2_), channel_id=1, source_target_pairs={{0,16},{1,17},{2,18},{3,19},{4,20},{5,21},{6,22},{7,23},{8,24},{9,... | collective-permute-start | bytes 746504 | tf_op jit(solution)/shard_map/ppermute | solution.py:53
  44.2 14.3 %collective-permute-start.13 = (bf16[2,72,864]{2,1,0:T(8,128)(2,1)S(1)}, bf16[2,72,864]{2,1,0:T(8,128)(2,1)S(1)}, u32[]{:S(2)}, u32[]{:S(2)}) collective-permute-start(bf16[2,72,864]{2,1,0:T(8,128)(2,1)S(1)} %shard_map.78.refs_2_), channel_id=1, source_target_pairs={{8,0},{9,1},{10,2},{11,3},{12,4},{13,5},{14,6},{15,7},{16,8},{17,9... | collective-permute-start | bytes 746504 | tf_op jit(solution)/shard_map/ppermute | solution.py:53
  45.5 18.8 %collective-permute-start.11 = (bf16[2,72,864]{2,1,0:T(8,128)(2,1)S(1)}, bf16[2,72,864]{2,1,0:T(8,128)(2,1)S(1)}, u32[]{:S(2)}, u32[]{:S(2)}) collective-permute-start(bf16[2,72,864]{2,1,0:T(8,128)(2,1)S(1)} %shard_map.78.refs_2_), channel_id=1, source_target_pairs={{0,8},{1,9},{2,10},{3,11},{4,12},{5,13},{6,14},{7,15},{8,16},{9,17... | collective-permute-start | bytes 746504 | tf_op jit(solution)/shard_map/ppermute | solution.py:53
  57.2 10.1 %collective-permute-start.14 = (bf16[2,72,864]{2,1,0:T(8,128)(2,1)S(1)}, bf16[2,72,864]{2,1,0:T(8,128)(2,1)S(1)}, u32[]{:S(2)}, u32[]{:S(2)}) collective-permute-start(bf16[2,72,864]{2,1,0:T(8,128)(2,1)S(1)} %collective-permute-done.12.refs_4_), channel_id=1, source_target_pairs={{8,0},{9,1},{10,2},{11,3},{12,4},{13,5},{14,6},{15,7},{16,24},{17,... | collective-permute-start | bytes 746504 | tf_op jit(solution)/shard_map/ppermute | solution.py:53
  58.5 17.9 %collective-permute-start.16 = (bf16[72,1152]{1,0:T(8,128)(2,1)}, bf16[72,1152]{1,0:T(8,128)(2,1)S(1)}, u32[]{:S(2)}, u32[]{:S(2)}) collective-permute-start(bf16[72,1152]{1,0:T(8,128)(2,1)} %param.11), channel_id=1, source_target_pairs={{0,8},{3,9},{4,12},{7,13},{8,16},{11,17},{12,20},{15,21},{16,26},{... | collective-permute-start | bytes 497672 | tf_op jit(solution)/shard_map/ppermute | solution.py:53
  64.3 12.0 %collective-permute-start.15 = (bf16[72,1152]{1,0:T(8,128)(2,1)}, bf16[72,1152]{1,0:T(8,128)(2,1)S(1)}, u32[]{:S(2)}, u32[]{:S(2)}) collective-permute-start(bf16[72,1152]{1,0:T(8,128)(2,1)} %param.11), channel_id=1, source_target_pairs={{0,0},{3,1},{4,4},{7,5},{8,8},{11,9},{12,12},{15,13},{16,18},{19,1... | collective-permute-start | bytes 497672 | tf_op jit(solution)/shard_map/ppermute | solution.py:53
  67.3 9.1 %collective-permute-start.18 = (bf16[72,1152]{1,0:T(8,128)(2,1)}, bf16[72,1152]{1,0:T(8,128)(2,1)S(1)}, u32[]{:S(2)}, u32[]{:S(2)}) collective-permute-start(bf16[72,1152]{1,0:T(8,128)(2,1)} %param.11), channel_id=1, source_target_pairs={{0,24},{3,25},{4,28},{7,29},{8,0},{11,1},{12,4},{15,5},{16,10},{19... | collective-permute-start | bytes 497672 | tf_op jit(solution)/shard_map/ppermute | solution.py:53
  86.7 38.3 %collective-permute-start.19 = (bf16[4,128,1152]{2,1,0:T(8,128)(2,1)S(1)}, bf16[4,128,1152]{2,1,0:T(8,128)(2,1)S(1)}, u32[]{:S(2)}, u32[]{:S(2)}) collective-permute-start(bf16[4,128,1152]{2,1,0:T(8,128)(2,1)S(1)} %get-tuple-element.31), channel_id=1, source_target_pairs={{0,2},{1,3},{2,0},{3,1},{4,6},{5,7},{6,4},{7,5},{8,10},{9,11},{10,... | collective-permute-start | bytes 3538952 | tf_op jit(solution)/shard_map/ppermute | solution.py:53
  90.0 13.2 %collective-permute-start.23 = (bf16[2,72,864]{2,1,0:T(8,128)(2,1)S(1)}, bf16[2,72,864]{2,1,0:T(8,128)(2,1)S(1)}, u32[]{:S(2)}, u32[]{:S(2)}) collective-permute-start(bf16[2,72,864]{2,1,0:T(8,128)(2,1)S(1)} %get-tuple-element.33), channel_id=1, source_target_pairs={{0,8},{1,9},{2,10},{3,11},{4,12},{5,13},{6,14},{7,15},{8,16},{9,17... | collective-permute-start | bytes 746504 | tf_op jit(solution)/shard_map/ppermute | solution.py:53
  93.2 20.7 %collective-permute-start.24 = (bf16[2,72,864]{2,1,0:T(8,128)(2,1)S(1)}, bf16[2,72,864]{2,1,0:T(8,128)(2,1)S(1)}, u32[]{:S(2)}, u32[]{:S(2)}) collective-permute-start(bf16[2,72,864]{2,1,0:T(8,128)(2,1)S(1)} %get-tuple-element.34), channel_id=1, source_target_pairs={{0,16},{1,17},{2,18},{3,19},{4,20},{5,21},{6,22},{7,23},{8,24},{9,... | collective-permute-start | bytes 746504 | tf_op jit(solution)/shard_map/ppermute | solution.py:53
  96.5 18.7 %collective-permute-start.25 = (bf16[2,72,864]{2,1,0:T(8,128)(2,1)S(1)}, bf16[2,72,864]{2,1,0:T(8,128)(2,1)S(1)}, u32[]{:S(2)}, u32[]{:S(2)}) collective-permute-start(bf16[2,72,864]{2,1,0:T(8,128)(2,1)S(1)} %get-tuple-element.35), channel_id=1, source_target_pairs={{0,24},{1,25},{2,26},{3,27},{4,28},{5,29},{6,30},{7,31},{8,0},{9,1... | collective-permute-start | bytes 746504 | tf_op jit(solution)/shard_map/ppermute | solution.py:53
  96.5 21.0 %collective-permute-start.33 = (bf16[72,1152]{1,0:T(8,128)(2,1)S(1)}, bf16[72,1152]{1,0:T(8,128)(2,1)S(1)}, u32[]{:S(2)}, u32[]{:S(2)}) collective-permute-start(bf16[72,1152]{1,0:T(8,128)(2,1)S(1)} %get-tuple-element.40), channel_id=1, source_target_pairs={{0,0},{1,3},{4,4},{5,7},{8,8},{9,11},{12,12},{13,15},{18,16},{19,1... | collective-permute-start | bytes 497672 | tf_op jit(solution)/shard_map/ppermute | solution.py:53
  103.1 20.8 %collective-permute-start.34 = (bf16[72,1152]{1,0:T(8,128)(2,1)S(1)}, bf16[72,1152]{1,0:T(8,128)(2,1)S(1)}, u32[]{:S(2)}, u32[]{:S(2)}) collective-permute-start(bf16[72,1152]{1,0:T(8,128)(2,1)S(1)} %get-tuple-element.41), channel_id=1, source_target_pairs={{0,8},{1,11},{4,12},{5,15},{10,16},{11,19},{14,20},{15,23},{18,24}... | collective-permute-start | bytes 497672 | tf_op jit(solution)/shard_map/ppermute | solution.py:53
  113.9 12.9 %collective-permute-start.35 = (bf16[72,1152]{1,0:T(8,128)(2,1)S(1)}, bf16[72,1152]{1,0:T(8,128)(2,1)S(1)}, u32[]{:S(2)}, u32[]{:S(2)}) collective-permute-start(bf16[72,1152]{1,0:T(8,128)(2,1)S(1)} %get-tuple-element.42), channel_id=1, source_target_pairs={{2,16},{3,19},{6,20},{7,23},{10,24},{11,27},{14,28},{15,31},{16,0}... | collective-permute-start | bytes 497672 | tf_op jit(solution)/shard_map/ppermute | solution.py:53
  115.2 12.7 %collective-permute-start.36 = (bf16[72,1152]{1,0:T(8,128)(2,1)S(1)}, bf16[72,1152]{1,0:T(8,128)(2,1)S(1)}, u32[]{:S(2)}, u32[]{:S(2)}) collective-permute-start(bf16[72,1152]{1,0:T(8,128)(2,1)S(1)} %get-tuple-element.43), channel_id=1, source_target_pairs={{2,24},{3,27},{6,28},{7,31},{8,0},{9,3},{12,4},{13,7},{16,8},{17,1... | collective-permute-start | bytes 497672 | tf_op jit(solution)/shard_map/ppermute | solution.py:53
  117.5 14.0 %collective-permute-start.28 = (bf16[72,432]{1,0:T(8,128)(2,1)S(1)}, bf16[72,432]{1,0:T(8,128)(2,1)S(1)}, u32[]{:S(2)}, u32[]{:S(2)}) collective-permute-start(bf16[72,432]{1,0:T(8,128)(2,1)S(1)} %get-tuple-element.37), channel_id=1, source_target_pairs={{0,3},{1,2},{2,1},{3,0},{4,7},{5,6},{6,5},{7,4},{8,11},{9,10},{10,... | collective-permute-start | bytes 186632 | tf_op jit(solution)/shard_map/ppermute | solution.py:53
  123.9 9.8 %collective-permute-start.27 = (bf16[72,432]{1,0:T(8,128)(2,1)S(1)}, bf16[72,432]{1,0:T(8,128)(2,1)S(1)}, u32[]{:S(2)}, u32[]{:S(2)}) collective-permute-start(bf16[72,432]{1,0:T(8,128)(2,1)S(1)} %get-tuple-element.37), channel_id=1, source_target_pairs={{0,2},{1,3},{2,0},{3,1},{4,6},{5,7},{6,4},{7,5},{8,10},{9,11},{10,... | collective-permute-start | bytes 186632 | tf_op jit(solution)/shard_map/ppermute | solution.py:53
  126.9 7.0 %collective-permute-start.30 = (bf16[72,432]{1,0:T(8,128)(2,1)S(1)}, bf16[72,432]{1,0:T(8,128)(2,1)S(1)}, u32[]{:S(2)}, u32[]{:S(2)}) collective-permute-start(bf16[72,432]{1,0:T(8,128)(2,1)S(1)} %get-tuple-element.38), channel_id=1, source_target_pairs={{0,5},{1,4},{2,7},{3,6},{4,1},{5,0},{6,3},{7,2},{8,13},{9,12},{10,... | collective-permute-start | bytes 186632 | tf_op jit(solution)/shard_map/ppermute | solution.py:53
  127.9 9.9 %collective-permute-start.29 = (bf16[72,432]{1,0:T(8,128)(2,1)S(1)}, bf16[72,432]{1,0:T(8,128)(2,1)S(1)}, u32[]{:S(2)}, u32[]{:S(2)}) collective-permute-start(bf16[72,432]{1,0:T(8,128)(2,1)S(1)} %get-tuple-element.38), channel_id=1, source_target_pairs={{0,4},{1,5},{2,6},{3,7},{4,0},{5,1},{6,2},{7,3},{8,12},{9,13},{10,... | collective-permute-start | bytes 186632 | tf_op jit(solution)/shard_map/ppermute | solution.py:53
  130.3 22.9 %collective-permute-start.20 = (bf16[128,1152]{1,0:T(8,128)(2,1)S(1)}, bf16[128,1152]{1,0:T(8,128)(2,1)S(1)}, u32[]{:S(2)}, u32[]{:S(2)}) collective-permute-start(bf16[128,1152]{1,0:T(8,128)(2,1)S(1)} %get-tuple-element.44), channel_id=1, source_target_pairs={{0,4},{1,5},{2,6},{3,7},{4,0},{5,1},{6,2},{7,3},{8,12},{9,13},{10,... | collective-permute-start | bytes 884744 | tf_op jit(solution)/shard_map/ppermute | solution.py:53
  131.4 21.8 %collective-permute-start.22 = (bf16[128,1152]{1,0:T(8,128)(2,1)S(1)}, bf16[128,1152]{1,0:T(8,128)(2,1)S(1)}, u32[]{:S(2)}, u32[]{:S(2)}) collective-permute-start(bf16[128,1152]{1,0:T(8,128)(2,1)S(1)} %get-tuple-element.45), channel_id=1, source_target_pairs={{0,5},{1,4},{2,7},{3,6},{4,1},{5,0},{6,3},{7,2},{8,13},{9,12},{10,... | collective-permute-start | bytes 884744 | tf_op jit(solution)/shard_map/ppermute | solution.py:53
  133.8 19.5 %collective-permute-start.21 = (bf16[128,1152]{1,0:T(8,128)(2,1)S(1)}, bf16[128,1152]{1,0:T(8,128)(2,1)S(1)}, u32[]{:S(2)}, u32[]{:S(2)}) collective-permute-start(bf16[128,1152]{1,0:T(8,128)(2,1)S(1)} %get-tuple-element.46), channel_id=1, source_target_pairs={{0,1},{1,0},{2,3},{3,2},{4,5},{5,4},{6,7},{7,6},{8,9},{9,8},{10,11... | collective-permute-start | bytes 884744 | tf_op jit(solution)/shard_map/ppermute | solution.py:53
  133.9 16.8 %collective-permute-start.37 = (bf16[72,1152]{1,0:T(8,128)(2,1)S(1)}, bf16[72,1152]{1,0:T(8,128)(2,1)S(1)}, u32[]{:S(2)}, u32[]{:S(2)}) collective-permute-start(bf16[72,1152]{1,0:T(8,128)(2,1)S(1)} %add_convert_fusion.3.refs_8_), channel_id=1, source_target_pairs={{0,1},{3,2},{4,5},{7,6},{8,9},{11,10},{12,13},{15,14},{16,17},{19,... | collective-permute-start | bytes 497672 | tf_op jit(solution)/shard_map/ppermute | solution.py:53
  137.8 8.7 %collective-permute-start.32 = (bf16[72,432]{1,0:T(8,128)(2,1)S(1)}, bf16[72,432]{1,0:T(8,128)(2,1)S(1)}, u32[]{:S(2)}, u32[]{:S(2)}) collective-permute-start(bf16[72,432]{1,0:T(8,128)(2,1)S(1)} %get-tuple-element.39), channel_id=1, source_target_pairs={{0,7},{1,6},{2,5},{3,4},{4,3},{5,2},{6,1},{7,0},{8,15},{9,14},{10,... | collective-permute-start | bytes 186632 | tf_op jit(solution)/shard_map/ppermute | solution.py:53
  (7 other events, 36.8 us)
